TPU v7x, 32 devices: a whole 2x2x4 slice. The times are simulated.
32 devices in a mesh: row: 4 (over z), col: 8 (over y, x, core).
Axes of the slice: x: 2, y: 2, z: 4, core: 2. Of those that a mesh axis runs over, the one named last changes fastest.
Arguments:
- obj_re: float32 [2048, 4096], P('row', 'col'), may hold values from -4 to 4
- obj_im: float32 [2048, 4096], P('row', 'col'), may hold values from -4 to 4
- probe_re: float32 [512, 512], replicated, may hold values from -6 to 6
- probe_im: float32 [512, 512], replicated, may hold values from -6 to 6
- amplitude: bfloat16 [4, 32, 512, 512], P('row', 'col'), may hold values from 0.099609375 to 3
- offset_y: int32 [4, 32], P('row', 'col'), may hold values from 0 to 511
- offset_x: int32 [4, 32], P('row', 'col'), may hold values from 0 to 511
- counts: int32 [4, 8], P('row', 'col'), may hold values from 1 to 4, as said below
Outputs:
- new_re: float32 [2048, 4096], P('row', 'col')
- new_im: float32 [2048, 4096], P('row', 'col')
Inputs may be any that keep to these rules, and one draw needn't show every extreme that they name: The live slots of a device are its first counts[r, c] slots; some device has 4 live slots. `offset_y`: A window starts inside the tile of the device that holds its slot.
All inputs are finite; a program needn't handle non-finite values.
Results may differ from a plain program's by a relative error of at most 0.0024.
The roundings to bfloat16 on the way count: a program that leaves them out, or rounds other values in their place, can miss the bound.
Values may be sent and summed in bfloat16 or wider, within the bound.
No kernel may reach another device: no remote copies, remote signals or barrier semaphores. Data moves between devices by JAX's collectives and lax.ppermute only.
A program may use at most 128 MiB of HBM per device.

v0:
```python
import math

import jax
import jax.numpy as jnp
from jax import lax
from jax.sharding import PartitionSpec as P

modulus_floor = 0.5
shrink_level = 0.2
step_size = 0.5
epsilon = 1e-05


def passed_along(value, axis, steps):
    count = lax.axis_size(axis)
    pairs = [(source, (source + steps) % count) for source in range(count)]
    return lax.ppermute(value, axis, pairs)


def with_halo(cells, sides, width):
    for axis, dim in sides:
        count = lax.axis_size(axis)
        head = lax.slice_in_dim(cells, 0, width, axis=dim)
        tail = lax.slice_in_dim(cells, cells.shape[dim] - width, cells.shape[dim], axis=dim)
        cells = jnp.concatenate(
            [
                lax.ppermute(tail, axis, [(i, (i + 1) % count) for i in range(count)]),
                cells,
                lax.ppermute(head, axis, [((i + 1) % count, i) for i in range(count)]),
            ],
            axis=dim,
        )
    return cells


def dft_tables(pattern_side):
    ordinal = jnp.arange(pattern_side, dtype=jnp.int32)
    phase_index = ordinal[:, None] * ordinal[None, :] % pattern_side
    angles = phase_index.astype(jnp.float32) * (2.0 * math.pi / pattern_side)
    norming = 1.0 / math.sqrt(pattern_side)
    return (
        (jnp.cos(angles) * norming).astype(jnp.bfloat16),
        (-jnp.sin(angles) * norming).astype(jnp.bfloat16),
    )


def matmul(left_op, right_op):
    return jnp.dot(left_op, right_op, preferred_element_type=jnp.float32)


def spectrum_rows(patch_tile, probe_re, probe_im, cos_table, sin_table):
    object_re = patch_tile[0].astype(jnp.float32)
    object_im = patch_tile[1].astype(jnp.float32)
    exit_re = (probe_re * object_re - probe_im * object_im).astype(jnp.bfloat16)
    exit_im = (probe_re * object_im + probe_im * object_re).astype(jnp.bfloat16)
    half_re = matmul(cos_table, exit_re) - matmul(sin_table, exit_im)
    half_im = matmul(cos_table, exit_im) + matmul(sin_table, exit_re)
    return jnp.stack([half_re, half_im]).astype(jnp.bfloat16)


def correct_rows(half_spec, measured, cos_table, sin_table):
    spec_re = matmul(half_spec[0], cos_table) - matmul(half_spec[1], sin_table)
    spec_im = matmul(half_spec[0], sin_table) + matmul(half_spec[1], cos_table)
    modulus = jnp.sqrt(spec_re * spec_re + spec_im * spec_im)
    factor = measured.astype(jnp.float32) / jnp.maximum(modulus, modulus_floor) - 1.0
    delta_re = (spec_re * factor).astype(jnp.bfloat16)
    delta_im = (spec_im * factor).astype(jnp.bfloat16)
    back_re = matmul(delta_re, cos_table) + matmul(delta_im, sin_table)
    back_im = matmul(delta_im, cos_table) - matmul(delta_re, sin_table)
    return jnp.stack([back_re, back_im]).astype(jnp.bfloat16)


def object_term(partial_back, probe_re, probe_im, cos_table, sin_table):
    wave_re = matmul(cos_table, partial_back[0]) + matmul(sin_table, partial_back[1])
    wave_im = matmul(cos_table, partial_back[1]) - matmul(sin_table, partial_back[0])
    return jnp.stack(
        [probe_re * wave_re + probe_im * wave_im, probe_re * wave_im - probe_im * wave_re]
    )


def shrink(entries):
    return entries - jnp.clip(entries, -shrink_level, shrink_level)


def haar_clean(field):
    top_left = field[:, 0::2, 0::2]
    top_right = field[:, 0::2, 1::2]
    low_left = field[:, 1::2, 0::2]
    low_right = field[:, 1::2, 1::2]
    coarse = 0.5 * (top_left + top_right + low_left + low_right)
    across = shrink(0.5 * (top_left - top_right + low_left - low_right))
    downward = shrink(0.5 * (top_left + top_right - low_left - low_right))
    diagonal = shrink(0.5 * (top_left - top_right - low_left + low_right))
    new_top_left = 0.5 * (coarse + across + downward + diagonal)
    new_top_right = 0.5 * (coarse - across + downward - diagonal)
    new_low_left = 0.5 * (coarse + across - downward - diagonal)
    new_low_right = 0.5 * (coarse - across - downward + diagonal)
    planes, height, breadth = top_left.shape
    top_rows = jnp.stack([new_top_left, new_top_right], axis=-1).reshape(
        planes, height, 2 * breadth
    )
    bottom_rows = jnp.stack([new_low_left, new_low_right], axis=-1).reshape(
        planes, height, 2 * breadth
    )
    return jnp.stack([top_rows, bottom_rows], axis=2).reshape(planes, 2 * height, 2 * breadth)


def body(obj_re, obj_im, probe_re, probe_im, amplitude, offset_y, offset_x, counts):
    pattern_side = probe_re.shape[0]
    cos_table, sin_table = dft_tables(pattern_side)
    probe_power = jnp.mean(probe_re * probe_re + probe_im * probe_im) + epsilon
    anchor = jnp.int32(0)
    own_tile = jnp.stack([obj_re, obj_im]).astype(jnp.bfloat16)
    below_tile = passed_along(own_tile, "row", -1)
    tile_column = jnp.concatenate([own_tile, below_tile], axis=1)
    right_pair = passed_along(tile_column, "col", -1)
    region = jnp.concatenate([tile_column, right_pair], axis=2)
    live_count = counts[0, 0]

    def whole_slot(slot_index, accumulated):
        row_at = offset_y[0, slot_index]
        col_at = offset_x[0, slot_index]
        patch_tile = lax.dynamic_slice(
            region, (anchor, row_at, col_at), (2, pattern_side, pattern_side)
        )
        half_spec = spectrum_rows(patch_tile, probe_re, probe_im, cos_table, sin_table)
        partial_back = correct_rows(half_spec, amplitude[0, slot_index], cos_table, sin_table)
        update = object_term(partial_back, probe_re, probe_im, cos_table, sin_table)
        window = lax.dynamic_slice(
            accumulated, (anchor, row_at, col_at), (2, pattern_side, pattern_side)
        )
        return lax.dynamic_update_slice(accumulated, window + update, (anchor, row_at, col_at))

    empty_sums = jnp.zeros((2, 2 * pattern_side, 2 * pattern_side), jnp.float32)
    accumulated = lax.fori_loop(0, live_count, whole_slot, empty_sums)
    lower_part = passed_along(accumulated[:, pattern_side:, :], "row", 1)
    upper_part = accumulated[:, :pattern_side, :] + lower_part
    spill_over = passed_along(upper_part[:, :, pattern_side:], "col", 1)
    intersection = upper_part[:, :, :pattern_side] + spill_over
    half_step = jnp.stack([obj_re, obj_im]) + step_size / probe_power * intersection
    rimmed = with_halo(half_step, (("row", 1), ("col", 2)), 1)
    cleaned = 0.5 * (
        haar_clean(half_step) + haar_clean(rimmed)[:, 1 : pattern_side + 1, 1 : pattern_side + 1]
    )
    return (cleaned[0], cleaned[1])


def solution(mesh):
    return jax.shard_map(
        body,
        mesh=mesh,
        in_specs=(
            P("row", "col"),
            P("row", "col"),
            P(),
            P(),
            P("row", "col", None, None),
            P("row", "col"),
            P("row", "col"),
            P("row", "col"),
        ),
        out_specs=(P("row", "col"), P("row", "col")),
        check_vma=False,
    )
```

profile of v0, /device:TPU:0, one launch (start us, length us, event | category | flops | bytes accessed | tf_op | source)
XLA Modules:
  0.0 895.3 jit_solution(12196277727500850362)
XLA Ops:
  3.3 5.1 collective-permute-start
  8.4 22.4 %collective-permute-done = bf16[2,512,512]{1,2,0:T(8,128)(2,1)S(1)} collective-permute-done((bf16[2,512,512]{1,2,0:T(8,128)(2,1)S(1)}, bf16[2,512,512]{1,2,0:T(8,128)(2,1)S(1)}, u32[]{:S(2)}, u32[]{:S(2)}) %collective-permute-start) | collective-permute-done | bytes 1048608 | tf_op jit(solution)/shard_map/ppermute | solution.py:17
  37.7 19.7 %collective-permute-done.1 = bf16[2,1024,512]{1,2,0:T(8,128)(2,1)} collective-permute-done((bf16[2,1024,512]{1,2,0:T(8,128)(2,1)}, bf16[2,1024,512]{1,2,0:T(8,128)(2,1)}, u32[]{:S(2)}, u32[]{:S(2)}) %collective-permute-start.1) | collective-permute-done | bytes 2097184 | tf_op jit(solution)/shard_map/ppermute | solution.py:17
  65.1 138.0 %while.14 = (s32[]{:T(128)}, f32[2,1024,1024]{1,2,0:T(8,128)}, s32[]{:T(128)}, s32[1,4]{1,0:T(1,128)S(1)}, s32[1,4]{1,0:T(1,128)S(1)}, /*index=5*/bf16[2,1024,10...) while((s32[]{:T(128)}, f32[2,1024,1024]{1,2,0:T(8,128)}, ...), condition=%wide.region_2.3_spmd.clone.clone, body=%wide.region_1.2_spmd.clone.clone.sunk | while | flops 4375445504 | bytes 51904804 | solution.py:135
  99.0 5.0 fusion.182
  108.9 5.0 fusion.179
  113.9 5.0 fusion.180
  119.0 5.2 convolution_subtract_fusion.5
  124.2 5.1 fusion.183
  129.2 6.2 multiply_convert_fusion.53
  140.3 5.0 fusion.188
  150.2 5.0 fusion.185
  155.3 5.0 fusion.186
  160.3 5.2 fusion.189
  170.5 6.0 add_bitcast_fusion.2
  179.0 14.3 %dynamic_update_slice.9 = f32[2,1024,1024]{1,2,0:T(8,128)} dynamic-update-slice(f32[2,1024,1024]{1,2,0:T(8,128)} %get-tuple-element.415, f32[2,512,512]{1,2,0:T(8,128)S(1)} %maximum_add_fusion.2, s32[]{:T(128)} %constant.61.clone.1..sunk, s32[]{:T(128)S(6)} %select_n.141, s32[]{:T(128)S(6)} %select_n.142) | dynamic-update-slice | bytes 4194308 | tf_op jit(solution)/shard_map/while/body/dynamic_update_slice | solution.py:132
  205.9 319.8 %collective-permute-start.2 = (f32[2,512,1024]{1,2,0:T(8,128)S(1)}, f32[2,512,1024]{1,2,0:T(8,128)S(1)}, u32[]{:S(2)}, u32[]{:S(2)}) collective-permute-start(f32[2,512,1024]{1,2,0:T(8,128)S(1)} %slice.90), channel_id=1, source_target_pairs={{0,8},{8,16},{16,24},{24,0},{1,9},{9,17},{17,25},{25,1},{2,10},{10... | collective-permute-start | bytes 12582920 | tf_op jit(solution)/shard_map/ppermute | solution.py:17
  525.7 46.0 %collective-permute-done.2 = f32[2,512,1024]{1,2,0:T(8,128)S(1)} collective-permute-done((f32[2,512,1024]{1,2,0:T(8,128)S(1)}, f32[2,512,1024]{1,2,0:T(8,128)S(1)}, u32[]{:S(2)}, u32[]{:S(2)}) %collective-permute-start.2) | collective-permute-done | bytes 4194336 | tf_op jit(solution)/shard_map/ppermute | solution.py:17
  577.4 23.9 %collective-permute-done.3 = f32[2,512,512]{1,2,0:T(8,128)} collective-permute-done((f32[2,512,512]{1,2,0:T(8,128)S(1)}, f32[2,512,512]{1,2,0:T(8,128)}, u32[]{:S(2)}, u32[]{:S(2)}) %collective-permute-start.3) | collective-permute-done | bytes 2097184 | tf_op jit(solution)/shard_map/ppermute | solution.py:17
  604.6 23.6 %slice.93 = f32[2,256,256]{1,2,0:T(8,128)S(1)} slice(f32[2,512,512]{1,2,0:T(8,128)S(1)} %fusion.111), slice={[0:2:1], [0:512:2], [0:512:2]} | slice | bytes 1048576 | tf_op jit(solution)/shard_map/slice | solution.py:86
  628.2 23.6 %slice.94 = f32[2,256,256]{1,2,0:T(8,128)S(1)} slice(f32[2,512,512]{1,2,0:T(8,128)S(1)} %fusion.111), slice={[0:2:1], [0:512:2], [1:512:2]} | slice | bytes 1048576 | tf_op jit(solution)/shard_map/slice | solution.py:87
  651.8 24.1 %slice.95 = f32[2,256,256]{1,2,0:T(8,128)} slice(f32[2,512,512]{1,2,0:T(8,128)S(1)} %fusion.111), slice={[0:2:1], [1:512:2], [0:512:2]} | slice | bytes 1048576 | tf_op jit(solution)/shard_map/slice | solution.py:88
  675.9 24.3 %slice.96 = f32[2,256,256]{1,2,0:T(8,128)} slice(f32[2,512,512]{1,2,0:T(8,128)S(1)} %fusion.111), slice={[0:2:1], [1:512:2], [1:512:2]} | slice | bytes 1048576 | tf_op jit(solution)/shard_map/slice | solution.py:89
  700.3 45.3 %collective-permute-start.4 = (f32[2,1,512]{1,2,0:T(8,128)S(1)}, f32[2,1,512]{1,2,0:T(8,128)S(1)}, u32[]{:S(2)}, u32[]{:S(2)}) collective-permute-start(f32[2,1,512]{1,2,0:T(8,128)S(1)} %get-tuple-element.322), channel_id=1, source_target_pairs={{0,8},{8,16},{16,24},{24,0},{1,9},{9,17},{17,25},{25,1},{2,10},{10... | collective-permute-start | bytes 12296 | tf_op jit(solution)/shard_map/ppermute | solution.py:27
  749.6 10.3 %collective-permute-done.4 = f32[2,1,512]{1,2,0:T(8,128)S(1)} collective-permute-done((f32[2,1,512]{1,2,0:T(8,128)S(1)}, f32[2,1,512]{1,2,0:T(8,128)S(1)}, u32[]{:S(2)}, u32[]{:S(2)}) %collective-permute-start.4) | collective-permute-done | bytes 4128 | tf_op jit(solution)/shard_map/ppermute | solution.py:27
  759.8 7.2 collective-permute-done.5
  772.8 6.5 copy.29
  781.8 23.4 %slice.101 = f32[2,257,257]{1,2,0:T(8,128)S(1)} slice(f32[2,514,514]{1,2,0:T(8,128)} %pad_maximum_fusion.2), slice={[0:2:1], [0:514:2], [0:514:2]} | slice | bytes 1056784 | tf_op jit(solution)/shard_map/slice | solution.py:86
  805.2 23.7 %slice.102 = f32[2,257,257]{1,2,0:T(8,128)} slice(f32[2,514,514]{1,2,0:T(8,128)} %pad_maximum_fusion.2), slice={[0:2:1], [0:514:2], [1:514:2]} | slice | bytes 1056784 | tf_op jit(solution)/shard_map/slice | solution.py:87
  828.9 23.3 %slice.103 = f32[2,257,257]{1,2,0:T(8,128)} slice(f32[2,514,514]{1,2,0:T(8,128)S(1)} %copy-done.2), slice={[0:2:1], [1:514:2], [0:514:2]} | slice | bytes 1056784 | tf_op jit(solution)/shard_map/slice | solution.py:88
  852.2 23.4 %slice.104 = f32[2,257,257]{1,2,0:T(8,128)} slice(f32[2,514,514]{1,2,0:T(8,128)S(1)} %copy-done.2), slice={[0:2:1], [1:514:2], [1:514:2]} | slice | bytes 1056784 | tf_op jit(solution)/shard_map/slice | solution.py:89
  881.6 5.2 copy.32
  (85 shorter events, 84.7 us)
Async XLA Ops:
  0.6 1.7 copy-start.16
  2.3 1.0 copy-start.3
  2.6 29.8 %copy-start.5 = (f32[512,512]{0,1:T(8,128)}, f32[512,512]{0,1:T(8,128)S(1)}, u32[]{:S(2)}) copy-start(f32[512,512]{0,1:T(8,128)S(1)} %copy.24) | copy-start | bytes 3145732
  3.3 27.5 %collective-permute-start = (bf16[2,512,512]{1,2,0:T(8,128)(2,1)S(1)}, bf16[2,512,512]{1,2,0:T(8,128)(2,1)S(1)}, u32[]{:S(2)}, u32[]{:S(2)}) collective-permute-start(bf16[2,512,512]{1,2,0:T(8,128)(2,1)S(1)} %fusion.112), channel_id=1, source_target_pairs={{0,24},{8,0},{16,8},{24,16},{1,25},{9,1},{17,9},{25,17},{2,26},{10... | collective-permute-start | bytes 3145736 | tf_op jit(solution)/shard_map/ppermute | solution.py:17
  30.8 1.7 copy-start.8
  32.5 24.9 %collective-permute-start.1 = (bf16[2,1024,512]{1,2,0:T(8,128)(2,1)}, bf16[2,1024,512]{1,2,0:T(8,128)(2,1)}, u32[]{:S(2)}, u32[]{:S(2)}) collective-permute-start(bf16[2,1024,512]{1,2,0:T(8,128)(2,1)} %pad_maximum_fusion.4), channel_id=1, source_target_pairs={{0,7},{1,0},{2,1},{3,2},{4,3},{5,4},{6,5},{7,6},{8,15},{9,8},{10,9... | collective-permute-start | bytes 6291464 | tf_op jit(solution)/shard_map/ppermute | solution.py:17
  33.5 23.9 %copy-start.9 = (bf16[2,512,512]{1,2,0:T(8,128)(2,1)S(1)}, bf16[2,512,512]{1,2,0:T(8,128)(2,1)}, u32[]{:S(2)}) copy-start(bf16[2,512,512]{1,2,0:T(8,128)(2,1)} %copy-done.8) | copy-start | bytes 3145732
  60.8 4.3 copy-start.17
  60.8 4.3 copy-start.18
  203.1 368.6 %copy-start = (f32[2,1024,1024]{1,2,0:T(8,128)S(1)}, f32[2,1024,1024]{1,2,0:T(8,128)}, u32[]{:S(2)}) copy-start(f32[2,1024,1024]{1,2,0:T(8,128)} %get-tuple-element.184) | copy-start | bytes 25165828
  205.9 365.8 %collective-permute-start.2 = (f32[2,512,1024]{1,2,0:T(8,128)S(1)}, f32[2,512,1024]{1,2,0:T(8,128)S(1)}, u32[]{:S(2)}, u32[]{:S(2)}) collective-permute-start(f32[2,512,1024]{1,2,0:T(8,128)S(1)} %slice.90), channel_id=1, source_target_pairs={{0,8},{8,16},{16,24},{24,0},{1,9},{9,17},{17,25},{25,1},{2,10},{10... | collective-permute-start | bytes 12582920 | tf_op jit(solution)/shard_map/ppermute | solution.py:17
  572.7 2.1 copy-start.1
  572.7 2.1 copy-start.6
  572.7 3.0 copy-start.7
  574.9 26.5 %copy-start.4 = (f32[512,512]{0,1:T(8,128)S(1)}, f32[512,512]{0,1:T(8,128)}, u32[]{:S(2)}) copy-start(f32[512,512]{0,1:T(8,128)} %copy-done.3) | copy-start | bytes 3145732
  574.9 26.5 %collective-permute-start.3 = (f32[2,512,512]{1,2,0:T(8,128)S(1)}, f32[2,512,512]{1,2,0:T(8,128)}, u32[]{:S(2)}, u32[]{:S(2)}) collective-permute-start(f32[2,512,512]{1,2,0:T(8,128)S(1)} %slice.113), channel_id=1, source_target_pairs={{0,1},{1,2},{2,3},{3,4},{4,5},{5,6},{6,7},{7,0},{8,9},{9,10},{10,1... | collective-permute-start | bytes 6291464 | tf_op jit(solution)/shard_map/ppermute | solution.py:17
  700.1 47.0 %copy-start.10 = (f32[2,256,256]{1,2,0:T(8,128)S(1)}, f32[2,256,256]{1,2,0:T(8,128)}, u32[]{:S(2)}) copy-start(f32[2,256,256]{1,2,0:T(8,128)} %slice.95) | copy-start | bytes 1572868
  700.1 47.0 %copy-start.11 = (f32[2,256,256]{1,2,0:T(8,128)S(1)}, f32[2,256,256]{1,2,0:T(8,128)}, u32[]{:S(2)}) copy-start(f32[2,256,256]{1,2,0:T(8,128)} %slice.96) | copy-start | bytes 1572868
  700.3 59.5 %collective-permute-start.4 = (f32[2,1,512]{1,2,0:T(8,128)S(1)}, f32[2,1,512]{1,2,0:T(8,128)S(1)}, u32[]{:S(2)}, u32[]{:S(2)}) collective-permute-start(f32[2,1,512]{1,2,0:T(8,128)S(1)} %get-tuple-element.322), channel_id=1, source_target_pairs={{0,8},{8,16},{16,24},{24,0},{1,9},{9,17},{17,25},{25,1},{2,10},{10... | collective-permute-start | bytes 12296 | tf_op jit(solution)/shard_map/ppermute | solution.py:27
  745.7 21.3 %collective-permute-start.5 = (f32[2,1,512]{1,2,0:T(8,128)S(1)}, f32[2,1,512]{1,2,0:T(8,128)S(1)}, u32[]{:S(2)}, u32[]{:S(2)}) collective-permute-start(f32[2,1,512]{1,2,0:T(8,128)S(1)} %get-tuple-element.323), channel_id=1, source_target_pairs={{8,0},{16,8},{24,16},{0,24},{9,1},{17,9},{25,17},{1,25},{10,2},{18... | collective-permute-start | bytes 12296 | tf_op jit(solution)/shard_map/ppermute | solution.py:29
  759.8 7.2 copy-start.12
  767.0 0.8 copy-start.14
  767.8 11.5 %collective-permute-start.6 = (f32[2,514,1]{1,2,0:T(1,128)S(1)}, f32[2,514,1]{1,2,0:T(1,128)S(1)}, u32[]{:S(2)}, u32[]{:S(2)}) collective-permute-start(f32[2,514,1]{1,2,0:T(1,128)S(1)} %get-tuple-element.315), channel_id=1, source_target_pairs={{0,1},{1,2},{2,3},{3,4},{4,5},{5,6},{6,7},{7,0},{8,9},{9,10},{10,1... | collective-permute-start | bytes 12344 | tf_op jit(solution)/shard_map/ppermute | solution.py:27
  767.8 11.4 %collective-permute-start.7 = (f32[2,514,1]{1,2,0:T(1,128)S(1)}, f32[2,514,1]{1,2,0:T(1,128)S(1)}, u32[]{:S(2)}, u32[]{:S(2)}) collective-permute-start(f32[2,514,1]{1,2,0:T(1,128)S(1)} %get-tuple-element.316), channel_id=1, source_target_pairs={{1,0},{2,1},{3,2},{4,3},{5,4},{6,5},{7,6},{0,7},{9,8},{10,9},{11,1... | collective-permute-start | bytes 12344 | tf_op jit(solution)/shard_map/ppermute | solution.py:29
  772.8 6.5 copy-start.13
  772.8 6.5 copy-start.15
  781.8 47.1 %copy-start.2 = (f32[2,514,514]{1,2,0:T(8,128)S(1)}, f32[2,514,514]{1,2,0:T(8,128)}, u32[]{:S(2)}) copy-start(f32[2,514,514]{1,2,0:T(8,128)} %pad_maximum_fusion.2) | copy-start | bytes 6340708
where the time goes:
time: 901 us; the launch traced here: 895 us
  starting transfers between devices  375 us (42%)
  local copies, waits for them, and re-layouts  241 us (27%)
  waiting for transfers between devices  130 us (14%)
  matrix products  82.3 us (9%)
  loops' own time  35.9 us (4%)
  other arithmetic  29.8 us (3%)
    ppermute x4, starting transfers between devices, passed_along(): return lax.ppermute(value, axis, pairs)  326 us
    ppermute x4, waiting for transfers between devices, passed_along(): return lax.ppermute(value, axis, pairs)  112 us
    dot_general x16, matrix products, matmul(): return jnp.dot(left_op, right_op, preferred_element_type=jnp.float32)  82.3 us
    slice x2, local copies, waits for them, and re-layouts, haar_clean(): low_right = field[:, 1::2, 1::2]  47.7 us
    slice x2, local copies, waits for them, and re-layouts, haar_clean(): low_left = field[:, 1::2, 0::2]  47.4 us
    slice x2, local copies, waits for them, and re-layouts, haar_clean(): top_right = field[:, 0::2, 1::2]  47.3 us
    slice x2, local copies, waits for them, and re-layouts, haar_clean(): top_left = field[:, 0::2, 0::2]  47 us
    ppermute x2, starting transfers between devices, with_halo(): lax.ppermute(tail, axis, [(i, (i + 1) % count) for i in range(count)])  45.3 us
  transfers between devices with their start and end apart: 8, of which 6 were waited for; matrix products, arithmetic and copies ran while one was open for 2% of the time, Pallas kernels for 0%

commit v1 on v0

v1 whole, which is shorter than its diff:
```python
import functools
import math

import jax
import jax.numpy as jnp
import numpy as np
from jax import lax
from jax.experimental import pallas as pl
from jax.experimental.pallas import tpu as pltpu
from jax.sharding import PartitionSpec as P

modulus_floor = 0.5
shrink_level = 0.2
step_size = 0.5
epsilon = 1e-05
LANES = 128


def transform_tables(side):
    quarter, half = side // 4, side // 2
    bf16 = jnp.bfloat16

    def cos_sin(rows, cols):
        angle = (rows[:, None] * cols[None, :] % side) * (2.0 * math.pi / side)
        norm = 1.0 / math.sqrt(side)
        return np.cos(angle) * norm, -np.sin(angle) * norm

    base = np.arange(quarter)
    grouped = np.concatenate([base[c::4] for c in range(4)])
    rows_in, rows_out = [], []
    for c in range(4):
        members = 4 * base + c
        co, si = cos_sin(grouped, members)
        rows_in.append(np.block([[co, -si], [si, co]]))
        co, si = cos_sin(base, members)
        rows_out.append(np.block([[co, si], [-si, co]]))
    frequency = np.concatenate([np.arange(0, half, 2), np.arange(1, half, 2)])
    mirrored = (side - frequency) % side
    mirrored[0] = half
    every = np.arange(side)
    co, si = cos_sin(every, frequency)
    co[:, 0] = np.where(every % 2 == 0, co[:, 0], 0.0)
    si[:, 0] = np.where(every % 2 == 1, 1.0 / math.sqrt(side), 0.0)
    cols_in = np.concatenate([co, si], axis=1)
    cols_out = []
    for part in range(2):
        run = slice(part * quarter, (part + 1) * quarter)
        members = np.concatenate([frequency[run], mirrored[run]])
        co, si = cos_sin(members, np.arange(half))
        cols_out.append(np.block([[co, -si], [si, co]]))
    order = np.concatenate([frequency, mirrored])
    pick = np.zeros((side, side))
    pick[order, every] = 1.0
    as_bf16 = lambda table: jnp.asarray(np.asarray(table, np.float32)).astype(bf16)
    return tuple(
        np.asarray(np.asarray(table, np.float32), dtype=bf16)
        for table in (np.stack(rows_in), cols_in, np.stack(cols_out), np.stack(rows_out), pick)
    )


def dot(left_op, right_op):
    return jnp.dot(left_op, right_op, preferred_element_type=jnp.float32)


def slots_kernel(
    side,
    count_ref,
    oy_ref,
    ox_ref,
    own_re,
    own_im,
    right_ref,
    below_ref,
    diag_ref,
    probe_re,
    probe_im,
    amp_ref,
    rows_in,
    cols_in,
    cols_out,
    rows_out,
    pick,
    own_out,
    right_out,
    below_out,
    diag_out,
    region,
    sums,
    probe,
    exits,
    wide,
    half,
    delta,
    back,
    amp,
):
    quarter, chunks = side // 4, side // LANES
    f32, bf16 = jnp.float32, jnp.bfloat16
    tiles = ((own_re, own_im), right_ref, below_ref, diag_ref)

    for p in range(2):
        for a in range(chunks):
            lanes = slice(a * LANES, (a + 1) * LANES)
            own = (own_re, own_im)[p]
            region[p, a, :side, :] = own[:, lanes].astype(bf16).astype(f32)
            region[p, chunks + a, :side, :] = right_ref[p, :, lanes].astype(f32)
            region[p, a, side:, :] = below_ref[p, :, lanes].astype(f32)
            region[p, chunks + a, side:, :] = diag_ref[p, :, lanes].astype(f32)
            probe[p, a] = (probe_re, probe_im)[p][:, lanes]
    sums[...] = jnp.zeros_like(sums)

    lane = lax.broadcasted_iota(jnp.int32, (1, LANES), 1)

    def one_slot(s, carry):
        oy = oy_ref[0, s]
        ox = ox_ref[0, s]
        q = ox // LANES
        b = ox % LANES
        inward = (LANES - b) % LANES
        keep = lane < LANES - b
        placed = lane >= b

        for c in range(4):
            rows = pl.ds(oy + c, quarter, stride=4)
            before = None
            for a in range(chunks + 1):
                now = [pltpu.roll(region[p, q + a, rows, :], inward, axis=1) for p in range(2)]
                if a > 0:
                    o_re, o_im = (jnp.where(keep, before[p], now[p]) for p in range(2))
                    mine = pl.ds(c, quarter, stride=4)
                    p_re, p_im = probe[0, a - 1, mine, :], probe[1, a - 1, mine, :]
                    lanes = slice((a - 1) * LANES, a * LANES)
                    exits[c, :quarter, lanes] = (p_re * o_re - p_im * o_im).astype(bf16)
                    exits[c, quarter:, lanes] = (p_re * o_im + p_im * o_re).astype(bf16)
                before = now
        for c in range(4):
            wide[c] = dot(rows_in[c], exits[c])
        step = quarter // 4
        for cc in range(4):
            for a in range(chunks):
                lanes = slice(a * LANES, (a + 1) * LANES)
                re = [wide[c, cc * step : (cc + 1) * step, lanes] for c in range(4)]
                im = [wide[c, quarter + cc * step : quarter + (cc + 1) * step, lanes] for c in range(4)]
                er, ei, fr, fi = re[0] + re[2], im[0] + im[2], re[0] - re[2], im[0] - im[2]
                gr, gi, hr, hi = re[1] + re[3], im[1] + im[3], re[1] - re[3], im[1] - im[3]
                outs = (
                    (er + gr, ei + gi),
                    (fr + hi, fi - hr),
                    (er - gr, ei - gi),
                    (fr - hi, fi + hr),
                )
                for m, (o_re, o_im) in enumerate(outs):
                    half[cc, m * step : (m + 1) * step, lanes] = o_re.astype(bf16)
                    half[cc, quarter + m * step : quarter + (m + 1) * step, lanes] = o_im.astype(bf16)

        ordered = dot(amp_ref[0, s], pick[...])
        for a in range(chunks):
            amp[a] = ordered[:, a * LANES : (a + 1) * LANES]

        for cc in range(4):
            wide[cc] = dot(half[cc], cols_in[...])
        mid = chunks // 2
        for cc in range(4):
            for part in range(mid):
                lo = slice(part * LANES, (part + 1) * LANES)
                hi = slice((mid + part) * LANES, (mid + part + 1) * LANES)
                p1, p3 = wide[cc, :quarter, lo], wide[cc, :quarter, hi]
                p4, p2 = wide[cc, quarter:, lo], wide[cc, quarter:, hi]
                if part == 0:
                    p2, p3 = jnp.where(lane == 0, -p3, p2), jnp.where(lane == 0, p2, p3)
                for sign in range(2):
                    s_re = p1 - p2 if sign == 0 else p1 + p2
                    s_im = p4 + p3 if sign == 0 else p4 - p3
                    measured = amp[sign * mid + part, pl.ds(cc, quarter, stride=4), :]
                    inverse = jnp.minimum(lax.rsqrt(s_re * s_re + s_im * s_im), 1.0 / modulus_floor)
                    factor = measured * inverse - 1.0
                    rows = slice(cc * quarter, (cc + 1) * quarter)
                    for k, value in ((sign, s_re), (2 + sign, s_im)):
                        delta[part, rows, k * LANES : (k + 1) * LANES] = (value * factor).astype(bf16)

        for part in range(2):
            for r in range(2):
                wide[2 * part + r] = dot(delta[part, r * side // 2 : (r + 1) * side // 2, :], cols_out[part])
        for cc in range(4):
            for k in range(2):
                for a in range(mid):
                    lanes = slice((k * mid + a) * LANES, (k * mid + a + 1) * LANES)
                    rows = slice((cc % 2) * quarter, (cc % 2 + 1) * quarter)
                    even, odd = wide[cc // 2, rows, lanes], wide[2 + cc // 2, rows, lanes]
                    put = slice(k * quarter, (k + 1) * quarter)
                    back[cc, put, a * LANES : (a + 1) * LANES] = (even + odd).astype(bf16)
                    back[cc, put, (mid + a) * LANES : (mid + a + 1) * LANES] = (even - odd).astype(bf16)

        for c in range(4):
            wide[c] = dot(rows_out[c], back[c])
        rows_at = 16
        for r in range(quarter // rows_at):
            before = [None] * 8
            for a in range(chunks + 1):
                now = [None] * 8
                if a < chunks:
                    lanes = slice(a * LANES, (a + 1) * LANES)
                    at = r * rows_at
                    re = [wide[c, at : at + rows_at, lanes] for c in range(4)]
                    im = [wide[c, quarter + at : quarter + at + rows_at, lanes] for c in range(4)]
                    er, ei, fr, fi = re[0] + re[2], im[0] + im[2], re[0] - re[2], im[0] - im[2]
                    gr, gi, hr, hi = re[1] + re[3], im[1] + im[3], re[1] - re[3], im[1] - im[3]
                    outs = (
                        (er + gr, ei + gi),
                        (fr - hi, fi + hr),
                        (er - gr, ei - gi),
                        (fr + hi, fi - hr),
                    )
                    for m, (w_re, w_im) in enumerate(outs):
                        mine = slice(m * quarter + at, m * quarter + at + rows_at)
                        p_re, p_im = probe[0, a, mine, :], probe[1, a, mine, :]
                        now[2 * m] = pltpu.roll(p_re * w_re + p_im * w_im, b, axis=1)
                        now[2 * m + 1] = pltpu.roll(p_re * w_im - p_im * w_re, b, axis=1)
                for k in range(8):
                    one = jnp.zeros((rows_at, LANES), f32) if now[k] is None else now[k]
                    two = jnp.zeros((rows_at, LANES), f32) if before[k] is None else before[k]
                    rows = pl.ds(oy + (k // 2) * quarter + r * rows_at, rows_at)
                    sums[k % 2, q + a, rows, :] += jnp.where(placed, one, two)
                before = now
        return carry

    lax.fori_loop(0, count_ref[0, 0], one_slot, 0)

    for p in range(2):
        for a in range(chunks):
            lanes = slice(a * LANES, (a + 1) * LANES)
            own_out[p, :, lanes] = sums[p, a, :side, :]
            right_out[p, :, lanes] = sums[p, chunks + a, :side, :].astype(bf16)
            below_out[p, :, lanes] = sums[p, a, side:, :].astype(below_out.dtype)
            diag_out[p, :, lanes] = sums[p, chunks + a, side:, :].astype(bf16)


def run_slots(counts, offset_y, offset_x, obj_re, obj_im, right, below, diag, probe_re, probe_im, amplitude):
    side = probe_re.shape[0]
    chunks, quarter = side // LANES, side // 4
    f32, bf16 = jnp.float32, jnp.bfloat16
    tables = transform_tables(side)
    smem = pl.BlockSpec(memory_space=pltpu.SMEM)
    vmem = pl.BlockSpec(memory_space=pltpu.VMEM)
    tile = lambda kind: jax.ShapeDtypeStruct((2, side, side), kind)
    return pl.pallas_call(
        functools.partial(slots_kernel, side),
        out_shape=(tile(f32), tile(bf16), tile(f32), tile(bf16)),
        in_specs=[smem] * 3 + [vmem] * 13,
        out_specs=[vmem] * 4,
        scratch_shapes=[
            pltpu.VMEM((2, 2 * chunks, 2 * side, LANES), f32),
            pltpu.VMEM((2, 2 * chunks, 2 * side, LANES), f32),
            pltpu.VMEM((2, chunks, side, LANES), f32),
            pltpu.VMEM((4, 2 * quarter, side), bf16),
            pltpu.VMEM((4, 2 * quarter, side), f32),
            pltpu.VMEM((4, 2 * quarter, side), bf16),
            pltpu.VMEM((2, side, side), bf16),
            pltpu.VMEM((4, 2 * quarter, side), bf16),
            pltpu.VMEM((chunks, side, LANES), f32),
        ],
        name="slots",
    )(counts, offset_y, offset_x, obj_re, obj_im, right, below, diag, probe_re, probe_im, amplitude, *tables)


def haar_kernel(hs_ref, top_ref, bottom_ref, left_ref, right_ref, out_re, out_im):
    side = hs_ref.shape[1]
    chunks = side // LANES
    block = 64
    level = shrink_level
    soft = lambda t: t - jnp.clip(t, -level, level)
    lane = lax.broadcasted_iota(jnp.int32, (1, LANES), 1)
    row = lax.broadcasted_iota(jnp.int32, (block, 1), 0)
    even_lane, even_row = lane % 2 == 0, row % 2 == 0

    def finish(total, gap, total_x, gap_x):
        coarse = 0.5 * (total + total_x)
        across = soft(0.5 * (total - total_x))
        downward = soft(0.5 * (gap + gap_x))
        diagonal = soft(0.5 * (gap - gap_x))
        return 0.5 * (coarse + across + downward + diagonal)

    for p in range(2):
        out = (out_re, out_im)[p]
        for r in range(side // block):
            at = r * block
            sums_of, gaps_of, plain = [], [], []
            for a in range(chunks):
                lanes = slice(a * LANES, (a + 1) * LANES)
                x = hs_ref[p, at : at + block, lanes]
                down = pltpu.roll(x, block - 1, axis=0)
                up = pltpu.roll(x, 1, axis=0)
                mate = jnp.where(even_row, down, up)
                total, gap = x + mate, x - mate
                mirror = lambda t: jnp.where(even_lane, pltpu.roll(t, LANES - 1, axis=1), pltpu.roll(t, 1, axis=1))
                plain.append(finish(total, gap, mirror(total), mirror(gap)))
                after = hs_ref[p, at + block : at + block + 1, lanes] if at + block < side else bottom_ref[p, :, lanes]
                ahead = hs_ref[p, at - 1 : at, lanes] if at > 0 else top_ref[p, :, lanes]
                down = jnp.where(row == block - 1, after, down)
                up = jnp.where(row == 0, ahead, up)
                mate = jnp.where(even_row, up, down)
                sums_of.append(x + mate)
                gaps_of.append(x - mate)
            rows = slice(at, at + block)

            def beside(ref):
                x, up, down = ref[p, 0, rows, :], ref[p, 1, rows, :], ref[p, 2, rows, :]
                mate = jnp.where(even_row, up, down)
                return x + mate, x - mate

            left, right = beside(left_ref), beside(right_ref)
            turned = [[(pltpu.roll(t, 1, axis=1), pltpu.roll(t, LANES - 1, axis=1)) for t in both] for both in (sums_of, gaps_of)]
            for a in range(chunks):
                other = []
                for k in range(2):
                    from_left = turned[k][a - 1][0] if a > 0 else left[k]
                    from_right = turned[k][a + 1][1] if a + 1 < chunks else right[k]
                    to_left = jnp.where(lane == 0, from_left, turned[k][a][0])
                    to_right = jnp.where(lane == LANES - 1, from_right, turned[k][a][1])
                    other.append(jnp.where(even_lane, to_left, to_right))
                moved = finish(sums_of[a], gaps_of[a], other[0], other[1])
                out[rows, a * LANES : (a + 1) * LANES] = 0.5 * (plain[a] + moved)


def run_haar(hs, top, bottom, left, right):
    side = hs.shape[1]
    vmem = pl.BlockSpec(memory_space=pltpu.VMEM)
    tile = jax.ShapeDtypeStruct((side, side), jnp.float32)
    return pl.pallas_call(
        haar_kernel,
        out_shape=(tile, tile),
        in_specs=[vmem] * 5,
        out_specs=[vmem] * 2,
        name="haar",
    )(hs, top, bottom, left, right)


def shifted(value, axis, steps):
    count = lax.axis_size(axis)
    return lax.ppermute(value, axis, [(i, (i + steps) % count) for i in range(count)])


def body(obj_re, obj_im, probe_re, probe_im, amplitude, offset_y, offset_x, counts):
    f32, bf16 = jnp.float32, jnp.bfloat16
    side = probe_re.shape[0]
    probe_power = jnp.mean(probe_re * probe_re + probe_im * probe_im) + epsilon
    own = jnp.stack([obj_re, obj_im]).astype(bf16)
    below = shifted(own, "row", -1)
    right = shifted(own, "col", -1)
    diag = shifted(below, "col", -1)
    own_sum, right_sum, below_sum, diag_sum = run_slots(
        counts, offset_y, offset_x, obj_re, obj_im, right, below, diag, probe_re, probe_im, amplitude
    )
    diag_in = shifted(diag_sum, "col", 1)
    right_in = shifted(right_sum, "col", 1)
    below_in = shifted((below_sum + diag_in.astype(f32)).astype(bf16), "row", 1)
    total = own_sum + right_in.astype(f32) + below_in.astype(f32)
    half_step = jnp.stack([obj_re, obj_im]) + step_size / probe_power * total
    top = shifted(half_step[:, -1:, :], "row", 1)
    bottom = shifted(half_step[:, :1, :], "row", -1)
    edges = jnp.concatenate([top, half_step[:, :, :], bottom], axis=1)
    left = shifted(edges[:, :, -1], "col", 1)
    right = shifted(edges[:, :, 0], "col", -1)

    def three(column):
        return jnp.stack([column[:, 1:-1], column[:, :-2], column[:, 2:]], axis=1)[..., None]

    return run_haar(half_step, top, bottom, three(left), three(right))


def solution(mesh):
    split = P("row", "col")
    return jax.shard_map(
        body,
        mesh=mesh,
        in_specs=(split, split, P(), P(), P("row", "col", None, None), split, split, split),
        out_specs=(split, split),
        check_vma=False,
    )
```

time: 901 us -> 138 us (0.15)
  starting transfers between devices: 375 us -> 12.8 us
  local copies, waits for them, and re-layouts: 241 us -> 4.55 us
  matrix products: 82.3 us -> 0 us
  waiting for transfers between devices: 130 us -> 74.1 us
  loops' own time: 35.9 us -> 0 us
  Pallas kernels: 0 us -> 34.5 us
  other arithmetic: 29.8 us -> 9.44 us
    ppermute x8 -> x10, starting transfers between devices: 375 us -> 12.8 us  [shifted(): lax.ppermute(value, axis, [(i, (i + steps) % count) for i in range(count)])]
    slice x12 -> x1, local copies, waits for them, and re-layouts: 194 us -> 0.01 us  [body(): bottom = shifted(half_step[:, :1, :], 'row', -1)]
    dot_general x16 -> x0, matrix products: 82.3 us -> none  [matmul(): return jnp.dot(left_op, right_op, preferred_element_type=jnp.float32)]
    ppermute x8 -> x10, waiting for transfers between devices: 130 us -> 74.1 us  [shifted(): lax.ppermute(value, axis, [(i, (i + steps) % count) for i in range(count)])]
    another operation x1 -> x0, loops' own time: 35.9 us -> none  [body(): accumulated = lax.fori_loop(0, live_count, whole_slot, empty_sums)]
    pallas_call x0 -> x2, Pallas kernels: none -> 34.5 us  [the longest x1 25.3 us: run_slots(): pl.pallas_call(functools.partial(slots_kernel, side), out_shape=(tile(f32...]
    another operation x6 -> x2, local copies, waits for them, and re-layouts: 14.9 us -> 0.15 us  [three(): jnp.stack([column[:, 1:-1], column[:, :-2], column[:, 2:]], axis=1)]
    dynamic_update_slice x1 -> x0, local copies, waits for them, and re-layouts: 14.3 us -> none  [whole_slot(): lax.dynamic_update_slice(accumulated, window + update, (anchor, row_at, c...]
  transfers between devices with their start and end apart: 8 -> 10, of which waited for: 6 -> 8; matrix products, arithmetic and copies ran while one was open for 2% -> 4% of each run, Pallas kernels for 0% -> 0%
where the time goes in v1:
time: 138 us; the launch traced here: 137 us
  waiting for transfers between devices  74.1 us (54%)
  Pallas kernels  34.5 us (25%)
  starting transfers between devices  12.8 us (9%)
  other arithmetic  9.44 us (7%)
  local copies, waits for them, and re-layouts  4.55 us (3%)
  between operations  2.07 us (1%)
    ppermute x10, waiting for transfers between devices, shifted(): lax.ppermute(value, axis, [(i, (i + steps) % count) for i in range(count)])  74.1 us
    pallas_call x1, Pallas kernels, run_slots(): pl.pallas_call(functools.partial(slots_kernel, side), out_shape=(tile(f32...  25.3 us
    ppermute x10, starting transfers between devices, shifted(): lax.ppermute(value, axis, [(i, (i + steps) % count) for i in range(count)])  12.8 us
    pallas_call x1, Pallas kernels, run_haar(): pl.pallas_call(haar_kernel, out_shape=(tile, tile), in_specs=[vmem] * 5,...  9.15 us
    broadcast_in_dim x2, local copies, waits for them, and re-layouts, three(): jnp.stack([column[:, 1:-1], column[:, :-2], column[:, 2:]], axis=1)  3.35 us
    add x1, other arithmetic, body(): half_step = jnp.stack([obj_re, obj_im]) + step_size / probe_power * total  3.16 us
    convert_element_type x1, other arithmetic, body(): below_in = shifted((below_sum + diag_in.astype(f32)).astype(bf16), 'row', 1)  3.05 us
  transfers between devices with their start and end apart: 10, of which 8 were waited for; matrix products, arithmetic and copies ran while one was open for 4% of the time, Pallas kernels for 0%

profile of v1, /device:TPU:0, one launch (start us, length us, event | category | flops | bytes accessed | tf_op | source)
XLA Modules:
  0.0 137.4 jit_solution(10873400419366695579)
XLA Ops:
  0.6 1.7 %fusion = bf16[2,512,512]{2,1,0:T(8,128)(2,1)S(1)} fusion(f32[1,512,512]{2,1,0:T(8,128)} %bitcast.20, f32[1,512,512]{2,1,0:T(8,128)} %bitcast.18), kind=kLoop, calls=%fused_computation.3 | loop fusion | flops 524288 | bytes 3145728 | tf_op jit(solution)/shard_map/convert_element_type | solution.py:347
  2.3 5.1 %collective-permute-start.1 = (bf16[2,512,512]{2,1,0:T(8,128)(2,1)S(1)}, bf16[2,512,512]{2,1,0:T(8,128)(2,1)S(1)}, u32[]{:S(2)}, u32[]{:S(2)}) collective-permute-start(bf16[2,512,512]{2,1,0:T(8,128)(2,1)S(1)} %fusion), channel_id=1, source_target_pairs={{0,24},{8,0},{16,8},{24,16},{1,25},{9,1},{17,9},{25,17},{2,26},{10... | collective-permute-start | bytes 3145736 | tf_op jit(solution)/shard_map/ppermute | solution.py:340
  7.5 1.6 %collective-permute-start = (bf16[2,512,512]{2,1,0:T(8,128)(2,1)S(1)}, bf16[2,512,512]{2,1,0:T(8,128)(2,1)S(1)}, u32[]{:S(2)}, u32[]{:S(2)}) collective-permute-start(bf16[2,512,512]{2,1,0:T(8,128)(2,1)S(1)} %fusion), channel_id=1, source_target_pairs={{0,7},{1,0},{2,1},{3,2},{4,3},{5,4},{6,5},{7,6},{8,15},{9,8},{10,9... | collective-permute-start | bytes 3145736 | tf_op jit(solution)/shard_map/ppermute | solution.py:340
  9.1 20.8 %collective-permute-done.1.below_ref = bf16[2,512,512]{2,1,0:T(8,128)(2,1)S(1)} collective-permute-done((bf16[2,512,512]{2,1,0:T(8,128)(2,1)S(1)}, bf16[2,512,512]{2,1,0:T(8,128)(2,1)S(1)}, u32[]{:S(2)}, u32[]{:S(2)}) %collective-permute-start.1) | collective-permute-done | bytes 1048608 | tf_op jit(solution)/shard_map/ppermute | solution.py:340
  29.9 1.0 collective-permute-start.2
  31.6 0.0 collective-permute-done.right_ref
  31.6 0.0 copy-start.6
  31.6 11.6 %collective-permute-done.2.diag_ref = bf16[2,512,512]{2,1,0:T(8,128)(2,1)S(1)} collective-permute-done((bf16[2,512,512]{2,1,0:T(8,128)(2,1)S(1)}, bf16[2,512,512]{2,1,0:T(8,128)(2,1)S(1)}, u32[]{:S(2)}, u32[]{:S(2)}) %collective-permute-start.2) | collective-permute-done | bytes 1048608 | tf_op jit(solution)/shard_map/ppermute | solution.py:340
  43.2 1.0 copy-done.7
  44.2 25.3 %slots.1 = (f32[2,512,512]{2,1,0:T(8,128)}, bf16[2,512,512]{2,1,0:T(8,128)(2,1)}, f32[2,512,512]{2,1,0:T(8,128)}, bf16[2,512,512]{2,1,0:T(8,128)(2,1)}) custom-call(s32[1,1]{1,0:T(1,128)S(6)} %copy.49.count_ref, s32[1,4]{1,0:T(1,128)} %oy_ref.1, s32[1,4]{1,0:T(1,128)} %ox_ref.1, f32[512,512]{1,0:T(8,128)} %own_re.1, f32[512,512]{1,0:T(8,128)} %own_im.1, ...), custom_call_target="tpu_custom_call" | custom-call | tf_op jit(solution)/shard_map/slots/pallas_call | solution.py:246
  69.6 0.0 collective-permute-start.4
  69.6 0.6 collective-permute-start.3
  70.2 14.7 %collective-permute-done.4 = bf16[2,512,512]{2,1,0:T(8,128)(2,1)S(1)} collective-permute-done((bf16[2,512,512]{2,1,0:T(8,128)(2,1)}, bf16[2,512,512]{2,1,0:T(8,128)(2,1)S(1)}, u32[]{:S(2)}, u32[]{:S(2)}) %collective-permute-start.4) | collective-permute-done | bytes 1048608 | tf_op jit(solution)/shard_map/ppermute | solution.py:340
  84.9 3.1 %add_convert_fusion = bf16[2,512,512]{2,1,0:T(8,128)(2,1)} fusion(f32[2,512,512]{2,1,0:T(8,128)} %get-tuple-element.8, bf16[2,512,512]{2,1,0:T(8,128)(2,1)S(1)} %collective-permute-done.4), kind=kLoop, calls=%fused_computation.2 | loop fusion | flops 1572864 | bytes 4194304 | tf_op jit(solution)/shard_map/convert_element_type | solution.py:356
  88.0 0.0 collective-permute-start.5
  88.0 0.9 add_reduce_fusion
  89.6 6.5 %collective-permute-done.3 = bf16[2,512,512]{2,1,0:T(8,128)(2,1)S(1)} collective-permute-done((bf16[2,512,512]{2,1,0:T(8,128)(2,1)}, bf16[2,512,512]{2,1,0:T(8,128)(2,1)S(1)}, u32[]{:S(2)}, u32[]{:S(2)}) %collective-permute-start.3) | collective-permute-done | bytes 1048608 | tf_op jit(solution)/shard_map/ppermute | solution.py:340
  96.1 16.4 %collective-permute-done.5 = bf16[2,512,512]{2,1,0:T(8,128)(2,1)} collective-permute-done((bf16[2,512,512]{2,1,0:T(8,128)(2,1)}, bf16[2,512,512]{2,1,0:T(8,128)(2,1)}, u32[]{:S(2)}, u32[]{:S(2)}) %collective-permute-start.5) | collective-permute-done | bytes 1048608 | tf_op jit(solution)/shard_map/ppermute | solution.py:340
  112.5 3.2 %multiply_add_fusion.hs_ref = f32[2,512,512]{2,1,0:T(8,128)S(1)} fusion(bf16[2,512,512]{2,1,0:T(8,128)(2,1)} %collective-permute-done.5, f32[2,512,512]{2,1,0:T(8,128)} %get-tuple-element.6, bf16[2,512,512]{2,1,0:T(8,128)(2,1)} %copy-done.4, f32[1,512,512]{2,1,0:T(8,128)} %bitcast.21, f32[1,512,512]{2,1,0:T(8,128)S(1)} %bitcast.19, f32[]{:T(128)S(6)} %div.7), kind=kLoop, calls=%fused_computation.1 | loop fusion | flops 3670016 | bytes 8388612 | tf_op jit(solution)/shard_map/add | solution.py:358
  115.7 0.1 collective-permute-start.6
  115.8 3.8 %collective-permute-start.7 = (f32[2,1,512]{2,1,0:T(1,128)S(1)}, f32[2,1,512]{2,1,0:T(1,128)S(1)}, u32[]{:S(2)}, u32[]{:S(2)}) collective-permute-start(f32[2,1,512]{2,1,0:T(1,128)S(1)} %get-tuple-element.12), channel_id=1, source_target_pairs={{0,24},{8,0},{16,8},{24,16},{1,25},{9,1},{17,9},{25,17},{2,26},{10... | collective-permute-start | bytes 12296 | tf_op jit(solution)/shard_map/ppermute | solution.py:340
  119.6 1.6 %collective-permute-done.6.top_ref = f32[2,1,512]{2,1,0:T(1,128)S(1)} collective-permute-done((f32[2,1,512]{2,1,0:T(1,128)S(1)}, f32[2,1,512]{2,1,0:T(1,128)S(1)}, u32[]{:S(2)}, u32[]{:S(2)}) %collective-permute-start.6) | collective-permute-done | bytes 4128 | tf_op jit(solution)/shard_map/ppermute | solution.py:340
  121.2 0.6 fusion.1
  121.8 0.3 collective-permute-start.9
  122.1 0.2 collective-permute-start.8
  122.3 1.1 collective-permute-done.9
  123.4 0.1 slice_bitcast_fusion.2
  123.5 1.7 %copy.48.right_ref = f32[2,3,512,1]{3,2,1,0:T(8,128)} copy(f32[2,3,512,1]{2,0,1,3:T(2,128)S(1)} %maximum_bitcast_fusion.1) | data formatting | bytes 24576 | tf_op jit(solution)/shard_map/broadcast_in_dim | solution.py:366
  125.2 1.3 collective-permute-done.8
  126.5 0.1 slice_bitcast_fusion.5
  126.6 1.7 %copy.47.left_ref = f32[2,3,512,1]{3,2,1,0:T(8,128)} copy(f32[2,3,512,1]{2,0,1,3:T(2,128)S(1)} %maximum_bitcast_fusion) | data formatting | bytes 24576 | tf_op jit(solution)/shard_map/broadcast_in_dim | solution.py:366
  128.3 9.1 %haar.1 = (f32[512,512]{1,0:T(8,128)}, f32[512,512]{1,0:T(8,128)}) custom-call(f32[2,512,512]{2,1,0:T(8,128)} %copy-done, f32[2,1,512]{2,1,0:T(1,128)} %copy-done.8, f32[2,1,512]{2,1,0:T(1,128)} %copy-done.9, f32[2,3,512,1]{3,2,1,0:T(8,128)} %copy.47.left_ref, f32[2,3,512,1]{3,2,1,0:T(8,128)} %copy.48.right_ref), custom_call_target="tpu_custom_call" | custom-call | tf_op jit(solution)/shard_map/haar/pallas_call | solution.py:329
  (22 shorter events, 0.1 us)
Async XLA Ops:
  2.3 27.5 %collective-permute-start.1 = (bf16[2,512,512]{2,1,0:T(8,128)(2,1)S(1)}, bf16[2,512,512]{2,1,0:T(8,128)(2,1)S(1)}, u32[]{:S(2)}, u32[]{:S(2)}) collective-permute-start(bf16[2,512,512]{2,1,0:T(8,128)(2,1)S(1)} %fusion), channel_id=1, source_target_pairs={{0,24},{8,0},{16,8},{24,16},{1,25},{9,1},{17,9},{25,17},{2,26},{10... | collective-permute-start | bytes 3145736 | tf_op jit(solution)/shard_map/ppermute | solution.py:340
  7.5 24.1 %collective-permute-start = (bf16[2,512,512]{2,1,0:T(8,128)(2,1)S(1)}, bf16[2,512,512]{2,1,0:T(8,128)(2,1)S(1)}, u32[]{:S(2)}, u32[]{:S(2)}) collective-permute-start(bf16[2,512,512]{2,1,0:T(8,128)(2,1)S(1)} %fusion), channel_id=1, source_target_pairs={{0,7},{1,0},{2,1},{3,2},{4,3},{5,4},{6,5},{7,6},{8,15},{9,8},{10,9... | collective-permute-start | bytes 3145736 | tf_op jit(solution)/shard_map/ppermute | solution.py:340
  29.9 13.4 %copy-start.5 = (bf16[2,512,512]{2,1,0:T(8,128)(2,1)}, bf16[2,512,512]{2,1,0:T(8,128)(2,1)S(1)}, u32[]{:S(2)}) copy-start(bf16[2,512,512]{2,1,0:T(8,128)(2,1)S(1)} %collective-permute-done.1.below_ref) | copy-start | bytes 3145732
  29.9 13.3 %collective-permute-start.2 = (bf16[2,512,512]{2,1,0:T(8,128)(2,1)S(1)}, bf16[2,512,512]{2,1,0:T(8,128)(2,1)S(1)}, u32[]{:S(2)}, u32[]{:S(2)}) collective-permute-start(bf16[2,512,512]{2,1,0:T(8,128)(2,1)S(1)} %collective-permute-done.1.below_ref), channel_id=1, source_target_pairs={{0,7},{1,0},{2,1},{3,2},{4,3},{5,4},{6,5},{7,6},{8,15},{9,8},{10,9... | collective-permute-start | bytes 3145736 | tf_op jit(solution)/shard_map/ppermute | solution.py:340
  31.6 11.7 %copy-start.6 = (bf16[2,512,512]{2,1,0:T(8,128)(2,1)}, bf16[2,512,512]{2,1,0:T(8,128)(2,1)S(1)}, u32[]{:S(2)}) copy-start(bf16[2,512,512]{2,1,0:T(8,128)(2,1)S(1)} %collective-permute-done.right_ref) | copy-start | bytes 3145732
  43.2 1.0 copy-start.7
  69.6 15.3 %collective-permute-start.4 = (bf16[2,512,512]{2,1,0:T(8,128)(2,1)}, bf16[2,512,512]{2,1,0:T(8,128)(2,1)S(1)}, u32[]{:S(2)}, u32[]{:S(2)}) collective-permute-start(bf16[2,512,512]{2,1,0:T(8,128)(2,1)} %get-tuple-element.9), channel_id=1, source_target_pairs={{0,1},{1,2},{2,3},{3,4},{4,5},{5,6},{6,7},{7,0},{8,9},{9,10},{10,1... | collective-permute-start | bytes 3145736 | tf_op jit(solution)/shard_map/ppermute | solution.py:340
  69.6 26.6 %collective-permute-start.3 = (bf16[2,512,512]{2,1,0:T(8,128)(2,1)}, bf16[2,512,512]{2,1,0:T(8,128)(2,1)S(1)}, u32[]{:S(2)}, u32[]{:S(2)}) collective-permute-start(bf16[2,512,512]{2,1,0:T(8,128)(2,1)} %get-tuple-element.7), channel_id=1, source_target_pairs={{0,1},{1,2},{2,3},{3,4},{4,5},{5,6},{6,7},{7,0},{8,9},{9,10},{10,1... | collective-permute-start | bytes 3145736 | tf_op jit(solution)/shard_map/ppermute | solution.py:340
  84.9 3.1 %copy-start.2 = (f32[512,512]{1,0:T(8,128)S(1)}, f32[512,512]{1,0:T(8,128)}, u32[]{:S(2)}) copy-start(f32[512,512]{1,0:T(8,128)} %probe_re.1) | copy-start | bytes 3145732
  84.9 3.1 %copy-start.3 = (f32[512,512]{1,0:T(8,128)S(1)}, f32[512,512]{1,0:T(8,128)}, u32[]{:S(2)}) copy-start(f32[512,512]{1,0:T(8,128)} %probe_im.1) | copy-start | bytes 3145732
  88.0 24.6 %copy-start.1 = (f32[512,512]{1,0:T(8,128)S(1)}, f32[512,512]{1,0:T(8,128)}, u32[]{:S(2)}) copy-start(f32[512,512]{1,0:T(8,128)} %own_re.1) | copy-start | bytes 3145732
  88.0 24.5 %collective-permute-start.5 = (bf16[2,512,512]{2,1,0:T(8,128)(2,1)}, bf16[2,512,512]{2,1,0:T(8,128)(2,1)}, u32[]{:S(2)}, u32[]{:S(2)}) collective-permute-start(bf16[2,512,512]{2,1,0:T(8,128)(2,1)} %add_convert_fusion), channel_id=1, source_target_pairs={{0,8},{8,16},{16,24},{24,0},{1,9},{9,17},{17,25},{25,1},{2,10},{10... | collective-permute-start | bytes 3145736 | tf_op jit(solution)/shard_map/ppermute | solution.py:340
  96.1 16.4 %copy-start.4 = (bf16[2,512,512]{2,1,0:T(8,128)(2,1)}, bf16[2,512,512]{2,1,0:T(8,128)(2,1)S(1)}, u32[]{:S(2)}) copy-start(bf16[2,512,512]{2,1,0:T(8,128)(2,1)S(1)} %collective-permute-done.3) | copy-start | bytes 3145732
  115.7 12.6 %copy-start = (f32[2,512,512]{2,1,0:T(8,128)}, f32[2,512,512]{2,1,0:T(8,128)S(1)}, u32[]{:S(2)}) copy-start(f32[2,512,512]{2,1,0:T(8,128)S(1)} %multiply_add_fusion.hs_ref) | copy-start | bytes 6291460
  115.7 5.5 %collective-permute-start.6 = (f32[2,1,512]{2,1,0:T(1,128)S(1)}, f32[2,1,512]{2,1,0:T(1,128)S(1)}, u32[]{:S(2)}, u32[]{:S(2)}) collective-permute-start(f32[2,1,512]{2,1,0:T(1,128)S(1)} %get-tuple-element.13), channel_id=1, source_target_pairs={{0,8},{8,16},{16,24},{24,0},{1,9},{9,17},{17,25},{25,1},{2,10},{10... | collective-permute-start | bytes 12296 | tf_op jit(solution)/shard_map/ppermute | solution.py:340
  115.8 5.4 %collective-permute-start.7 = (f32[2,1,512]{2,1,0:T(1,128)S(1)}, f32[2,1,512]{2,1,0:T(1,128)S(1)}, u32[]{:S(2)}, u32[]{:S(2)}) collective-permute-start(f32[2,1,512]{2,1,0:T(1,128)S(1)} %get-tuple-element.12), channel_id=1, source_target_pairs={{0,24},{8,0},{16,8},{24,16},{1,25},{9,1},{17,9},{25,17},{2,26},{10... | collective-permute-start | bytes 12296 | tf_op jit(solution)/shard_map/ppermute | solution.py:340
  121.2 7.1 %copy-start.8 = (f32[2,1,512]{2,1,0:T(1,128)}, f32[2,1,512]{2,1,0:T(1,128)S(1)}, u32[]{:S(2)}) copy-start(f32[2,1,512]{2,1,0:T(1,128)S(1)} %collective-permute-done.6.top_ref) | copy-start | bytes 12292
  121.2 7.1 %copy-start.9 = (f32[2,1,512]{2,1,0:T(1,128)}, f32[2,1,512]{2,1,0:T(1,128)S(1)}, u32[]{:S(2)}) copy-start(f32[2,1,512]{2,1,0:T(1,128)S(1)} %collective-permute-done.7.bottom_ref) | copy-start | bytes 12292
  121.8 1.7 %collective-permute-start.9 = (f32[2,514]{1,0:T(2,128)S(1)}, f32[2,514]{1,0:T(2,128)S(1)}, u32[]{:S(2)}, u32[]{:S(2)}) collective-permute-start(f32[2,514]{1,0:T(2,128)S(1)} %get-tuple-element.10), channel_id=1, source_target_pairs={{0,7},{1,0},{2,1},{3,2},{4,3},{5,4},{6,5},{7,6},{8,15},{9,8},{10,9... | collective-permute-start | bytes 12344 | tf_op jit(solution)/shard_map/ppermute | solution.py:340
  122.1 4.4 %collective-permute-start.8 = (f32[2,514]{1,0:T(2,128)S(1)}, f32[2,514]{1,0:T(2,128)S(1)}, u32[]{:S(2)}, u32[]{:S(2)}) collective-permute-start(f32[2,514]{1,0:T(2,128)S(1)} %get-tuple-element.11), channel_id=1, source_target_pairs={{0,1},{1,2},{2,3},{3,4},{4,5},{5,6},{6,7},{7,0},{8,9},{9,10},{10,1... | collective-permute-start | bytes 12344 | tf_op jit(solution)/shard_map/ppermute | solution.py:340

commit v2 on v1

--- a/solution.py
+++ b/solution.py
@@ -62,41 +62,23 @@
     return jnp.dot(left_op, right_op, preferred_element_type=jnp.float32)
 
 
-def slots_kernel(
-    side,
-    count_ref,
-    oy_ref,
-    ox_ref,
-    own_re,
-    own_im,
-    right_ref,
-    below_ref,
-    diag_ref,
-    probe_re,
-    probe_im,
-    amp_ref,
-    rows_in,
-    cols_in,
-    cols_out,
-    rows_out,
-    pick,
-    own_out,
-    right_out,
-    below_out,
-    diag_out,
-    region,
-    sums,
-    probe,
-    exits,
-    wide,
-    half,
-    delta,
-    back,
-    amp,
-):
+def slots_kernel(side, in_parts, out_parts, *refs):
+    refs = list(refs)
+
+    def take(count):
+        taken = refs[:count]
+        del refs[:count]
+        return taken
+
+    count_ref, oy_ref, ox_ref, scale_ref, own_re, own_im, right_ref = take(7)
+    below_refs, diag_refs = take(len(in_parts)), take(len(in_parts))
+    probe_re, probe_im, amp_ref = take(3)
+    rows_in, cols_in, cols_out, rows_out, pick = take(5)
+    own_out, right_out, edge_out = take(3)
+    below_outs, diag_outs = take(len(out_parts)), take(len(out_parts))
+    region, sums, probe, exits, wide, half, delta, back, amp = refs
     quarter, chunks = side // 4, side // LANES
     f32, bf16 = jnp.float32, jnp.bfloat16
-    tiles = ((own_re, own_im), right_ref, below_ref, diag_ref)
 
     for p in range(2):
         for a in range(chunks):
@@ -104,8 +86,11 @@
             own = (own_re, own_im)[p]
             region[p, a, :side, :] = own[:, lanes].astype(bf16).astype(f32)
             region[p, chunks + a, :side, :] = right_ref[p, :, lanes].astype(f32)
-            region[p, a, side:, :] = below_ref[p, :, lanes].astype(f32)
-            region[p, chunks + a, side:, :] = diag_ref[p, :, lanes].astype(f32)
+            at = side
+            for rows, below_ref, diag_ref in zip(in_parts, below_refs, diag_refs):
+                region[p, a, at : at + rows, :] = below_ref[p, :, lanes].astype(f32)
+                region[p, chunks + a, at : at + rows, :] = diag_ref[p, :, lanes].astype(f32)
+                at += rows
             probe[p, a] = (probe_re, probe_im)[p][:, lanes]
     sums[...] = jnp.zeros_like(sums)
 
@@ -226,28 +211,42 @@
 
     lax.fori_loop(0, count_ref[0, 0], one_slot, 0)
 
+    scale = scale_ref[0, 0]
     for p in range(2):
+        own = (own_re, own_im)[p]
         for a in range(chunks):
             lanes = slice(a * LANES, (a + 1) * LANES)
-            own_out[p, :, lanes] = sums[p, a, :side, :]
-            right_out[p, :, lanes] = sums[p, chunks + a, :side, :].astype(bf16)
-            below_out[p, :, lanes] = sums[p, a, side:, :].astype(below_out.dtype)
-            diag_out[p, :, lanes] = sums[p, chunks + a, side:, :].astype(bf16)
-
-
-def run_slots(counts, offset_y, offset_x, obj_re, obj_im, right, below, diag, probe_re, probe_im, amplitude):
+            right_out[p, :, lanes] = (scale * sums[p, chunks + a, :side, :]).astype(bf16)
+            own_out[p, :, lanes] = own[:, lanes] + scale * sums[p, a, :side, :]
+            at = side
+            for rows, below_out, diag_out in zip(out_parts, below_outs, diag_outs):
+                below_out[p, :, lanes] = scale * sums[p, a, at : at + rows, :]
+                diag_out[p, :, lanes] = (scale * sums[p, chunks + a, at : at + rows, :]).astype(bf16)
+                at += rows
+        for k, (a, at) in enumerate(((0, 0), (chunks - 1, LANES - 1), (chunks, 0), (2 * chunks - 1, LANES - 1))):
+            for r in range(2 * side // LANES):
+                cells = scale * sums[p, a, r * LANES : (r + 1) * LANES, :]
+                if k < 2 and r < chunks:
+                    cells += own[r * LANES : (r + 1) * LANES, a * LANES : (a + 1) * LANES]
+                edge_out[p, k : k + 1, r * LANES : (r + 1) * LANES] = cells.T[at : at + 1, :]
+
+
+def run_slots(counts, offset_y, offset_x, scale, obj_re, obj_im, right, below, diag, probe_re, probe_im, amplitude, out_parts):
     side = probe_re.shape[0]
     chunks, quarter = side // LANES, side // 4
     f32, bf16 = jnp.float32, jnp.bfloat16
     tables = transform_tables(side)
+    in_parts = [part.shape[1] for part in below]
     smem = pl.BlockSpec(memory_space=pltpu.SMEM)
     vmem = pl.BlockSpec(memory_space=pltpu.VMEM)
-    tile = lambda kind: jax.ShapeDtypeStruct((2, side, side), kind)
-    return pl.pallas_call(
-        functools.partial(slots_kernel, side),
-        out_shape=(tile(f32), tile(bf16), tile(f32), tile(bf16)),
-        in_specs=[smem] * 3 + [vmem] * 13,
-        out_specs=[vmem] * 4,
+    tile = lambda rows, kind: jax.ShapeDtypeStruct((2, rows, side), kind)
+    outs = [tile(side, f32), tile(side, bf16), jax.ShapeDtypeStruct((2, 4, 2 * side), f32)]
+    outs += [tile(rows, f32) for rows in out_parts] + [tile(rows, bf16) for rows in out_parts]
+    results = pl.pallas_call(
+        functools.partial(slots_kernel, side, in_parts, out_parts),
+        out_shape=outs,
+        in_specs=[smem] * 4 + [vmem] * (11 + 2 * len(in_parts)),
+        out_specs=[vmem] * len(outs),
         scratch_shapes=[
             pltpu.VMEM((2, 2 * chunks, 2 * side, LANES), f32),
             pltpu.VMEM((2, 2 * chunks, 2 * side, LANES), f32),
@@ -259,80 +258,122 @@
             pltpu.VMEM((4, 2 * quarter, side), bf16),
             pltpu.VMEM((chunks, side, LANES), f32),
         ],
+        compiler_params=pltpu.CompilerParams(vmem_limit_bytes=46 * 2**20),
         name="slots",
-    )(counts, offset_y, offset_x, obj_re, obj_im, right, below, diag, probe_re, probe_im, amplitude, *tables)
-
-
-def haar_kernel(hs_ref, top_ref, bottom_ref, left_ref, right_ref, out_re, out_im):
-    side = hs_ref.shape[1]
+    )(counts, offset_y, offset_x, scale, obj_re, obj_im, right, *below, *diag, probe_re, probe_im, amplitude, *tables)
+    parts = len(out_parts)
+    return results[0], results[1], results[2], results[3 : 3 + parts], results[3 + parts :]
+
+
+def finish_kernel(parts, *refs):
+    own_ref, right_ref = refs[:2]
+    below_refs = refs[2 : 2 + len(parts)]
+    top_ref, bottom_ref, ring_ref, out_re, out_im, cells, spill, result = refs[2 + len(parts) :]
+    side = own_ref.shape[1]
     chunks = side // LANES
-    block = 64
-    level = shrink_level
-    soft = lambda t: t - jnp.clip(t, -level, level)
-    lane = lax.broadcasted_iota(jnp.int32, (1, LANES), 1)
-    row = lax.broadcasted_iota(jnp.int32, (block, 1), 0)
-    even_lane, even_row = lane % 2 == 0, row % 2 == 0
-
-    def finish(total, gap, total_x, gap_x):
-        coarse = 0.5 * (total + total_x)
-        across = soft(0.5 * (total - total_x))
-        downward = soft(0.5 * (gap + gap_x))
-        diagonal = soft(0.5 * (gap - gap_x))
-        return 0.5 * (coarse + across + downward + diagonal)
-
+    f32 = jnp.float32
+    pad, count = 16, 8
+    ring = ring_ref[...].T
     for p in range(2):
-        out = (out_re, out_im)[p]
-        for r in range(side // block):
-            at = r * block
-            sums_of, gaps_of, plain = [], [], []
+        for a in range(chunks):
+            lanes = slice(a * LANES, (a + 1) * LANES)
+            at = 0
+            for rows, below_ref in zip(parts, below_refs):
+                mine = slice(at, at + rows)
+                cells[p, a + 1, pad + at : pad + at + rows, :] = (
+                    own_ref[p, mine, lanes] + right_ref[p, mine, lanes].astype(f32) + below_ref[p, :, lanes].astype(f32)
+                )
+                at += rows
+        for k in range(2):
+            beside = jnp.broadcast_to(ring[:, 2 * k + p : 2 * k + p + 1], (side, LANES))
+            cells[p, k * (chunks + 1), pad : pad + side, :] = beside
+        for a in range(chunks + 2):
+            cells[p, a, pad - 1 : pad, :] = top_ref[p, a : a + 1, :]
+            cells[p, a, pad + side : pad + side + 1, :] = bottom_ref[p, a : a + 1, :]
+
+    bound = 2.0 * shrink_level
+    lane = lax.broadcasted_iota(jnp.int32, (count, LANES), 1)
+    even, first, last = lane % 2 == 0, lane == 0, lane == LANES - 1
+    cut = lambda t: jnp.clip(t, -bound, bound)
+    later = lambda t: pltpu.roll(t, 1, axis=1)
+    sooner = lambda t: pltpu.roll(t, LANES - 1, axis=1)
+
+    def clips(total, gap, total_x, gap_x):
+        side_by_side = cut(total - total_x)
+        other = cut(gap + gap_x) + cut(gap - gap_x)
+        return side_by_side + other, side_by_side - other
+
+    def moved(p, at):
+        upper = pl.ds(pad + 1 + 2 * at, count, stride=2)
+        lower = pl.ds(pad + 2 + 2 * at, count, stride=2)
+        high = [cells[p, a, upper, :] for a in range(chunks + 2)]
+        low = [cells[p, a, lower, :] for a in range(chunks + 2)]
+        fields = [[h + w for h, w in zip(high, low)], [h - w for h, w in zip(high, low)]]
+        turned = []
+        for field in fields:
+            right_of = [later(field[a]) for a in range(chunks + 1)]
+            left_of = [sooner(field[a]) for a in range(1, chunks + 2)]
+            turned.append(
+                [
+                    jnp.where(
+                        even,
+                        jnp.where(first, right_of[a - 1], right_of[a]),
+                        jnp.where(last, left_of[a], left_of[a - 1]),
+                    )
+                    for a in range(1, chunks + 1)
+                ]
+            )
+        return [clips(fields[0][a + 1], fields[1][a + 1], turned[0][a], turned[1][a]) for a in range(chunks)]
+
+    for p in range(2):
+        for a, (_, below_one) in enumerate(moved(p, -count)):
+            spill[p, a, 1 : 1 + count, :] = below_one
+
+    def block(i, carry):
+        at = pl.multiple_of(i * count, count)
+        for p in range(2):
+            shifted_clips = moved(p, at)
             for a in range(chunks):
-                lanes = slice(a * LANES, (a + 1) * LANES)
-                x = hs_ref[p, at : at + block, lanes]
-                down = pltpu.roll(x, block - 1, axis=0)
-                up = pltpu.roll(x, 1, axis=0)
-                mate = jnp.where(even_row, down, up)
-                total, gap = x + mate, x - mate
-                mirror = lambda t: jnp.where(even_lane, pltpu.roll(t, LANES - 1, axis=1), pltpu.roll(t, 1, axis=1))
-                plain.append(finish(total, gap, mirror(total), mirror(gap)))
-                after = hs_ref[p, at + block : at + block + 1, lanes] if at + block < side else bottom_ref[p, :, lanes]
-                ahead = hs_ref[p, at - 1 : at, lanes] if at > 0 else top_ref[p, :, lanes]
-                down = jnp.where(row == block - 1, after, down)
-                up = jnp.where(row == 0, ahead, up)
-                mate = jnp.where(even_row, up, down)
-                sums_of.append(x + mate)
-                gaps_of.append(x - mate)
-            rows = slice(at, at + block)
-
-            def beside(ref):
-                x, up, down = ref[p, 0, rows, :], ref[p, 1, rows, :], ref[p, 2, rows, :]
-                mate = jnp.where(even_row, up, down)
-                return x + mate, x - mate
-
-            left, right = beside(left_ref), beside(right_ref)
-            turned = [[(pltpu.roll(t, 1, axis=1), pltpu.roll(t, LANES - 1, axis=1)) for t in both] for both in (sums_of, gaps_of)]
+                upper = pl.ds(pad + 2 * at, count, stride=2)
+                lower = pl.ds(pad + 1 + 2 * at, count, stride=2)
+                high, low = cells[p, a + 1, upper, :], cells[p, a + 1, lower, :]
+                total, gap = high + low, high - low
+                total_x = jnp.where(even, sooner(total), later(total))
+                gap_x = jnp.where(even, sooner(gap), later(gap))
+                top_clip, low_clip = clips(total, gap, total_x, gap_x)
+                spill[p, a, pl.ds(at + count + 1, count), :] = shifted_clips[a][1]
+                top_clip += spill[p, a, pl.ds(at + count, count), :]
+                low_clip += shifted_clips[a][0]
+                result[p, a, pl.ds(2 * at, count, stride=2), :] = high - 0.125 * top_clip
+                result[p, a, pl.ds(2 * at + 1, count, stride=2), :] = low - 0.125 * low_clip
             for a in range(chunks):
-                other = []
-                for k in range(2):
-                    from_left = turned[k][a - 1][0] if a > 0 else left[k]
-                    from_right = turned[k][a + 1][1] if a + 1 < chunks else right[k]
-                    to_left = jnp.where(lane == 0, from_left, turned[k][a][0])
-                    to_right = jnp.where(lane == LANES - 1, from_right, turned[k][a][1])
-                    other.append(jnp.where(even_lane, to_left, to_right))
-                moved = finish(sums_of[a], gaps_of[a], other[0], other[1])
-                out[rows, a * LANES : (a + 1) * LANES] = 0.5 * (plain[a] + moved)
-
-
-def run_haar(hs, top, bottom, left, right):
-    side = hs.shape[1]
+                mine = pl.ds(2 * at, 2 * count)
+                (out_re, out_im)[p][mine, a * LANES : (a + 1) * LANES] = result[p, a, mine, :]
+        return carry
+
+    lax.fori_loop(0, side // (2 * count), block, 0)
+
+
+def run_finish(own, right, below, top, bottom, ring):
+    side = own.shape[1]
+    chunks = side // LANES
+    f32 = jnp.float32
     vmem = pl.BlockSpec(memory_space=pltpu.VMEM)
-    tile = jax.ShapeDtypeStruct((side, side), jnp.float32)
+    tile = jax.ShapeDtypeStruct((side, side), f32)
+    parts = [part.shape[1] for part in below]
     return pl.pallas_call(
-        haar_kernel,
+        functools.partial(finish_kernel, parts),
         out_shape=(tile, tile),
-        in_specs=[vmem] * 5,
+        in_specs=[vmem] * (5 + len(parts)),
         out_specs=[vmem] * 2,
-        name="haar",
-    )(hs, top, bottom, left, right)
+        scratch_shapes=[
+            pltpu.VMEM((2, chunks + 2, side + 32, LANES), f32),
+            pltpu.VMEM((2, chunks, side // 2 + 16, LANES), f32),
+            pltpu.VMEM((2, chunks, side, LANES), f32),
+        ],
+        compiler_params=pltpu.CompilerParams(vmem_limit_bytes=20 * 2**20),
+        name="finish",
+    )(own, right, *below, top, bottom, ring)
 
 
 def shifted(value, axis, steps):
@@ -340,32 +381,61 @@
     return lax.ppermute(value, axis, [(i, (i + steps) % count) for i in range(count)])
 
 
+def parts_of(side, weights):
+    unit = side // 32
+    sizes = [unit * weight for weight in weights]
+    assert sum(sizes) == side and unit % 16 == 0
+    return sizes
+
+
+def split_rows(value, sizes):
+    ends = np.cumsum(sizes)
+    return [value[:, end - size : end] for end, size in zip(ends, sizes)]
+
+
 def body(obj_re, obj_im, probe_re, probe_im, amplitude, offset_y, offset_x, counts):
     f32, bf16 = jnp.float32, jnp.bfloat16
     side = probe_re.shape[0]
+    in_parts, out_parts = parts_of(side, (16, 10, 6)), parts_of(side, (4, 12, 16))
     probe_power = jnp.mean(probe_re * probe_re + probe_im * probe_im) + epsilon
-    own = jnp.stack([obj_re, obj_im]).astype(bf16)
-    below = shifted(own, "row", -1)
-    right = shifted(own, "col", -1)
-    diag = shifted(below, "col", -1)
-    own_sum, right_sum, below_sum, diag_sum = run_slots(
-        counts, offset_y, offset_x, obj_re, obj_im, right, below, diag, probe_re, probe_im, amplitude
+    scale = (step_size / probe_power).reshape(1, 1)
+    own = jnp.stack([obj_re, obj_im])
+    pieces = [piece.astype(bf16) for piece in split_rows(own, in_parts)]
+    below = [shifted(piece, "row", -1) for piece in pieces]
+    right = shifted(own.astype(bf16), "col", -1)
+    diag = [shifted(piece, "col", -1) for piece in below]
+    own_sum, right_sum, edges, below_sum, diag_sum = run_slots(
+        counts, offset_y, offset_x, scale, obj_re, obj_im, right, below, diag, probe_re, probe_im, amplitude, out_parts
     )
-    diag_in = shifted(diag_sum, "col", 1)
+
+    diag_in = [shifted(piece, "col", 1) for piece in diag_sum]
     right_in = shifted(right_sum, "col", 1)
-    below_in = shifted((below_sum + diag_in.astype(f32)).astype(bf16), "row", 1)
-    total = own_sum + right_in.astype(f32) + below_in.astype(f32)
-    half_step = jnp.stack([obj_re, obj_im]) + step_size / probe_power * total
-    top = shifted(half_step[:, -1:, :], "row", 1)
-    bottom = shifted(half_step[:, :1, :], "row", -1)
-    edges = jnp.concatenate([top, half_step[:, :, :], bottom], axis=1)
-    left = shifted(edges[:, :, -1], "col", 1)
-    right = shifted(edges[:, :, 0], "col", -1)
-
-    def three(column):
-        return jnp.stack([column[:, 1:-1], column[:, :-2], column[:, 2:]], axis=1)[..., None]
-
-    return run_haar(half_step, top, bottom, three(left), three(right))
+    beside_right = shifted(edges[:, 0], "col", -1) + edges[:, 2]
+    beside_left = shifted(edges[:, 1], "col", 1) + shifted(edges[:, 3], "col", 2)
+    lower = [mine + theirs.astype(f32) for mine, theirs in zip(below_sum, diag_in)]
+    below_in = [shifted(piece.astype(bf16), "row", 1) for piece in lower]
+
+    def with_ends(row, at):
+        chunks = row.reshape(2, side // LANES, LANES)
+        ends = [jnp.broadcast_to(column[:, at, None, None], (2, 1, LANES)) for column in (beside_left, beside_right)]
+        return jnp.concatenate([ends[0], chunks, ends[1]], axis=1)
+
+    first = with_ends(own_sum[:, 0] + right_in[:, 0].astype(f32), 0)
+    last = with_ends(own_sum[:, -1] + right_in[:, -1].astype(f32), side - 1)
+    low_first = with_ends(lower[0][:, 0], side)
+    low_last = with_ends(lower[-1][:, -1], 2 * side - 1)
+    sides = jnp.concatenate([beside_left[:, side:], beside_right[:, side:]], axis=1)
+    sent_down = jnp.concatenate([last, sides.reshape(2, -1, LANES)], axis=1)
+    from_up = shifted(sent_down, "row", 1)
+    from_down = shifted(first, "row", -1)
+    from_far = shifted(low_last, "row", 2)
+    rows = side // LANES + 2
+    top = from_up[:, :rows] + from_far
+    bottom = from_down + low_first
+    spilled = from_up[:, rows:].reshape(2, 2, side)
+    ring = jnp.concatenate([beside_left[:, :side] + spilled[:, 0], beside_right[:, :side] + spilled[:, 1]], axis=0)
+    ring = jnp.concatenate([ring, jnp.zeros((4, side), f32)], axis=0)
+    return run_finish(own_sum, right_in, below_in, top, bottom, ring)
 
 
 def solution(mesh):

time: 138 us -> 132 us (0.957)
  starting transfers between devices: 12.8 us -> 39.5 us
  waiting for transfers between devices: 74.1 us -> 48.2 us
  Pallas kernels: 34.5 us -> 25.3 us
  local copies, waits for them, and re-layouts: 4.55 us -> 8.22 us
    ppermute x10 -> x20, starting transfers between devices: 12.8 us -> 39.5 us  [shifted(): lax.ppermute(value, axis, [(i, (i + steps) % count) for i in range(count)])]
    ppermute x10 -> x20, waiting for transfers between devices: 74.1 us -> 48.2 us  [shifted(): lax.ppermute(value, axis, [(i, (i + steps) % count) for i in range(count)])]
    pallas_call x2, Pallas kernels: 34.5 us -> 25.3 us  [the longest x1 16.8 us: run_slots(): pl.pallas_call(functools.partial(slots_kernel, side, in_parts, out_parts)...]
    slice x1 -> x11, local copies, waits for them, and re-layouts: 0.01 us -> 5.01 us  [the longest x3 3.19 us: split_rows(): return [value[:, end - size:end] for end, size in zip(ends, sizes)]]
    broadcast_in_dim x2 -> x9, local copies, waits for them, and re-layouts: 3.35 us -> 0.56 us  [the longest x8 0.56 us: with_ends(): jnp.broadcast_to(column[:, at, None, None], (2, 1, LANES))]
    add x1 -> x6, other arithmetic: 3.16 us -> 1.44 us  [the longest x1 0.72 us: body(): top = from_up[:, :rows] + from_far]
    concatenate x0 -> x4, other arithmetic: none -> 1.38 us  [the longest x1 0.75 us: body(): ring = jnp.concatenate([ring, jnp.zeros((4, side), f32)], axis=0)]
    convert_element_type x2 -> x4, other arithmetic: 4.74 us -> 5.38 us  [the longest x1 2.81 us: body(): right = shifted(own.astype(bf16), 'col', -1)]
  transfers between devices with their start and end apart: 10 -> 20, of which waited for: 8 -> 10; matrix products, arithmetic and copies ran while one was open for 4% -> 10% of each run, Pallas kernels for 0% -> 0%
where the time goes in v2:
time: 132 us; the launch traced here: 133 us
  waiting for transfers between devices  48.2 us (37%)
  starting transfers between devices  39.5 us (30%)
  Pallas kernels  25.3 us (19%)
  other arithmetic  9.13 us (7%)
  local copies, waits for them, and re-layouts  8.22 us (6%)
  between operations  2.22 us (2%)
    ppermute x20, waiting for transfers between devices, shifted(): lax.ppermute(value, axis, [(i, (i + steps) % count) for i in range(count)])  48.2 us
    ppermute x20, starting transfers between devices, shifted(): lax.ppermute(value, axis, [(i, (i + steps) % count) for i in range(count)])  39.5 us
    pallas_call x1, Pallas kernels, run_slots(): pl.pallas_call(functools.partial(slots_kernel, side, in_parts, out_parts)...  16.8 us
    pallas_call x1, Pallas kernels, run_finish(): pl.pallas_call(functools.partial(finish_kernel, parts), out_shape=(tile,...  8.54 us
    slice x3, local copies, waits for them, and re-layouts, split_rows(): return [value[:, end - size:end] for end, size in zip(ends, sizes)]  3.19 us
    convert_element_type x1, other arithmetic, body(): right = shifted(own.astype(bf16), 'col', -1)  2.81 us
  transfers between devices with their start and end apart: 20, of which 10 were waited for; matrix products, arithmetic and copies ran while one was open for 10% of the time, Pallas kernels for 0%

profile of v2, /device:TPU:0, one launch (start us, length us, event | category | flops | bytes accessed | tf_op | source)
XLA Modules:
  0.0 132.6 jit_solution(7391130876871728309)
XLA Ops:
  0.7 2.8 %maximum_convert_fusion = bf16[2,512,512]{2,1,0:T(8,128)(2,1)} fusion(f32[1,512,512]{2,1,0:T(8,128)} %bitcast.31, f32[1,512,512]{2,1,0:T(8,128)} %bitcast.30), kind=kLoop, calls=%fused_computation | loop fusion | flops 524288 | bytes 3145728 | tf_op jit(solution)/shard_map/convert_element_type | solution.py:405
  3.5 1.2 slice.119
  4.7 5.1 %collective-permute-start.1 = (bf16[2,256,512]{2,1,0:T(8,128)(2,1)S(1)}, bf16[2,256,512]{2,1,0:T(8,128)(2,1)S(1)}, u32[]{:S(2)}, u32[]{:S(2)}) collective-permute-start(bf16[2,256,512]{2,1,0:T(8,128)(2,1)S(1)} %slice.119), channel_id=1, source_target_pairs={{0,24},{8,0},{16,8},{24,16},{1,25},{9,1},{17,9},{25,17},{2,26},{10... | collective-permute-start | bytes 1572872 | tf_op jit(solution)/shard_map/ppermute | solution.py:381
  9.9 1.6 %collective-permute-start = (bf16[2,512,512]{2,1,0:T(8,128)(2,1)}, bf16[2,512,512]{2,1,0:T(8,128)(2,1)}, u32[]{:S(2)}, u32[]{:S(2)}) collective-permute-start(bf16[2,512,512]{2,1,0:T(8,128)(2,1)} %maximum_convert_fusion), channel_id=1, source_target_pairs={{0,7},{1,0},{2,1},{3,2},{4,3},{5,4},{6,5},{7,6},{8,15},{9,8},{10,9... | collective-permute-start | bytes 3145736 | tf_op jit(solution)/shard_map/ppermute | solution.py:381
  11.5 1.0 slice.120
  13.0 9.2 %collective-permute-done.1.refs_7_ = bf16[2,256,512]{2,1,0:T(8,128)(2,1)S(1)} collective-permute-done((bf16[2,256,512]{2,1,0:T(8,128)(2,1)S(1)}, bf16[2,256,512]{2,1,0:T(8,128)(2,1)S(1)}, u32[]{:S(2)}, u32[]{:S(2)}) %collective-permute-start.1) | collective-permute-done | bytes 524320 | tf_op jit(solution)/shard_map/ppermute | solution.py:381
  22.2 0.9 slice.121
  23.1 4.3 %collective-permute-start.3 = (bf16[2,96,512]{2,1,0:T(8,128)(2,1)S(1)}, bf16[2,96,512]{2,1,0:T(8,128)(2,1)}, u32[]{:S(2)}, u32[]{:S(2)}) collective-permute-start(bf16[2,96,512]{2,1,0:T(8,128)(2,1)S(1)} %slice.121), channel_id=1, source_target_pairs={{0,24},{8,0},{16,8},{24,16},{1,25},{9,1},{17,9},{25,17},{2,26},{10... | collective-permute-start | bytes 589832 | tf_op jit(solution)/shard_map/ppermute | solution.py:381
  28.1 1.7 %collective-permute-start.5 = (bf16[2,160,512]{2,1,0:T(8,128)(2,1)S(1)}, bf16[2,160,512]{2,1,0:T(8,128)(2,1)}, u32[]{:S(2)}, u32[]{:S(2)}) collective-permute-start(bf16[2,160,512]{2,1,0:T(8,128)(2,1)S(1)} %collective-permute-done.2.refs_8_), channel_id=1, source_target_pairs={{0,7},{1,0},{2,1},{3,2},{4,3},{5,4},{6,5},{7,6},{8,15},{9,8},{10,9... | collective-permute-start | bytes 983048 | tf_op jit(solution)/shard_map/ppermute | solution.py:381
  29.7 2.5 %collective-permute-done.3.refs_9_ = bf16[2,96,512]{2,1,0:T(8,128)(2,1)} collective-permute-done((bf16[2,96,512]{2,1,0:T(8,128)(2,1)S(1)}, bf16[2,96,512]{2,1,0:T(8,128)(2,1)}, u32[]{:S(2)}, u32[]{:S(2)}) %collective-permute-start.3) | collective-permute-done | bytes 196640 | tf_op jit(solution)/shard_map/ppermute | solution.py:381
  32.3 1.7 %collective-permute-start.6 = (bf16[2,96,512]{2,1,0:T(8,128)(2,1)}, bf16[2,96,512]{2,1,0:T(8,128)(2,1)}, u32[]{:S(2)}, u32[]{:S(2)}) collective-permute-start(bf16[2,96,512]{2,1,0:T(8,128)(2,1)} %collective-permute-done.3.refs_9_), channel_id=1, source_target_pairs={{0,7},{1,0},{2,1},{3,2},{4,3},{5,4},{6,5},{7,6},{8,15},{9,8},{10,9... | collective-permute-start | bytes 589832 | tf_op jit(solution)/shard_map/ppermute | solution.py:381
  34.7 0.9 add_reduce_fusion
  36.3 1.2 collective-permute-done.6.refs_12_
  37.6 16.8 %slots.1 = (f32[2,512,512]{2,1,0:T(8,128)}, bf16[2,512,512]{2,1,0:T(8,128)(2,1)S(1)}, f32[2,4,1024]{2,1,0:T(4,128)S(1)}, f32[2,64,512]{2,1,0:T(8,128)S(1)}, f32[...) custom-call(s32[1,1]{1,0:T(1,128)S(6)} %copy.36.refs_0_, ...), custom_call_target="tpu_custom_call" | custom-call | tf_op jit(solution)/shard_map/slots/pallas_call | solution.py:245
  54.4 6.3 %collective-permute-start.15 = (f32[2,1024]{1,0:T(2,128)S(1)}, f32[2,1024]{1,0:T(2,128)S(1)}, u32[]{:S(2)}, u32[]{:S(2)}) collective-permute-start(f32[2,1024]{1,0:T(2,128)S(1)} %get-tuple-element.34), channel_id=1, source_target_pairs={{0,2},{1,3},{2,4},{3,5},{4,6},{5,7},{6,0},{7,1},{8,10},{9,11},{10,... | collective-permute-start | bytes 24584 | tf_op jit(solution)/shard_map/ppermute | solution.py:381
  61.4 4.7 %collective-permute-start.16 = (f32[2,1024]{1,0:T(2,128)S(1)}, f32[2,1024]{1,0:T(2,128)S(1)}, u32[]{:S(2)}, u32[]{:S(2)}) collective-permute-start(f32[2,1024]{1,0:T(2,128)S(1)} %get-tuple-element.35), channel_id=1, source_target_pairs={{0,7},{1,0},{2,1},{3,2},{4,3},{5,4},{6,5},{7,6},{8,15},{9,8},{10,9... | collective-permute-start | bytes 24584 | tf_op jit(solution)/shard_map/ppermute | solution.py:381
  67.4 1.3 collective-permute-start.10
  69.3 13.4 %collective-permute-done.8 = bf16[2,64,512]{2,1,0:T(8,128)(2,1)S(1)} collective-permute-done((bf16[2,64,512]{2,1,0:T(8,128)(2,1)S(1)}, bf16[2,64,512]{2,1,0:T(8,128)(2,1)S(1)}, u32[]{:S(2)}, u32[]{:S(2)}) %collective-permute-start.8) | collective-permute-done | bytes 131104 | tf_op jit(solution)/shard_map/ppermute | solution.py:381
  83.4 9.1 %collective-permute-done.10 = bf16[2,192,512]{2,1,0:T(8,128)(2,1)S(1)} collective-permute-done((bf16[2,192,512]{2,1,0:T(8,128)(2,1)S(1)}, bf16[2,192,512]{2,1,0:T(8,128)(2,1)S(1)}, u32[]{:S(2)}, u32[]{:S(2)}) %collective-permute-start.10) | collective-permute-done | bytes 393248 | tf_op jit(solution)/shard_map/ppermute | solution.py:381
  92.5 0.9 add_convert_fusion
  93.4 1.0 fusion.3
  95.2 1.6 %collective-permute-start.18 = (f32[2,6,128]{2,1,0:T(8,128)}, f32[2,6,128]{2,1,0:T(8,128)}, u32[]{:S(2)}, u32[]{:S(2)}) collective-permute-start(f32[2,6,128]{2,1,0:T(8,128)} %pad_maximum_fusion.1), channel_id=1, source_target_pairs={{0,16},{8,24},{16,0},{24,8},{1,17},{9,25},{17,1},{25,9},{2,18},{10... | collective-permute-start | bytes 18440 | tf_op jit(solution)/shard_map/ppermute | solution.py:381
  96.8 2.8 %collective-permute-start.13 = (bf16[2,256,512]{2,1,0:T(8,128)(2,1)}, bf16[2,256,512]{2,1,0:T(8,128)(2,1)}, u32[]{:S(2)}, u32[]{:S(2)}) collective-permute-start(bf16[2,256,512]{2,1,0:T(8,128)(2,1)} %get-tuple-element.28), channel_id=1, source_target_pairs={{0,8},{8,16},{16,24},{24,0},{1,9},{9,17},{17,25},{25,1},{2,10},{10... | collective-permute-start | bytes 1572872 | tf_op jit(solution)/shard_map/ppermute | solution.py:381
  99.7 1.1 collective-permute-start.19
  101.0 9.5 %collective-permute-done.19 = f32[2,6,128]{2,1,0:T(8,128)S(1)} collective-permute-done((f32[2,6,128]{2,1,0:T(8,128)S(1)}, f32[2,6,128]{2,1,0:T(8,128)S(1)}, u32[]{:S(2)}, u32[]{:S(2)}) %collective-permute-start.19) | collective-permute-done | bytes 6176 | tf_op jit(solution)/shard_map/ppermute | solution.py:381
  110.5 6.6 %collective-permute-start.17 = (f32[2,14,128]{2,1,0:T(8,128)S(1)}, f32[2,14,128]{2,1,0:T(8,128)S(1)}, u32[]{:S(2)}, u32[]{:S(2)}) collective-permute-start(f32[2,14,128]{2,1,0:T(8,128)S(1)} %pad_maximum_fusion), channel_id=1, source_target_pairs={{0,8},{8,16},{16,24},{24,0},{1,9},{9,17},{17,25},{25,1},{2,10},{10... | collective-permute-start | bytes 43016 | tf_op jit(solution)/shard_map/ppermute | solution.py:381
  117.3 1.3 collective-permute-done.17
  119.8 1.3 reshape.49
  121.1 0.8 fusion.5
  122.5 0.7 slice_add_fusion.refs_5_
  123.3 0.8 maximum_maximum_fusion.refs_7_
  124.0 8.5 %finish.1 = (f32[512,512]{1,0:T(8,128)}, f32[512,512]{1,0:T(8,128)}) custom-call(f32[2,512,512]{2,1,0:T(8,128)S(1)} %copy-done, bf16[2,512,512]{2,1,0:T(8,128)(2,1)S(1)} %collective-permute-done.7.refs_1_, bf16[2,64,512]{2,1,0:T(8,128)(2,1)} %collective-permute-done.9.refs_2_, bf16[2,192,512]{2,1,0:T(8,128)(2,1)S(1)} %collective-permute-done.11.refs_3_, ...), custom_call_target="tpu_custom_call" | custom-call | tf_op jit(solution)/shard_map/finish/pallas_call | solution.py:364
  (75 shorter events, 7.5 us)
Async XLA Ops:
  0.6 34.0 %copy-start.7 = (f32[512,512]{1,0:T(8,128)S(1)}, f32[512,512]{1,0:T(8,128)}, u32[]{:S(2)}) copy-start(f32[512,512]{1,0:T(8,128)} %refs_14_.1) | copy-start | bytes 3145732
  0.6 34.0 %copy-start.8 = (f32[512,512]{1,0:T(8,128)S(1)}, f32[512,512]{1,0:T(8,128)}, u32[]{:S(2)}) copy-start(f32[512,512]{1,0:T(8,128)} %refs_13_.1) | copy-start | bytes 3145732
  3.5 34.0 %copy-start.1 = (bf16[4,256,256]{2,1,0:T(8,128)(2,1)S(1)}, bf16[4,256,256]{2,1,0:T(8,128)(2,1)}, u32[]{:S(2)}) copy-start(bf16[4,256,256]{2,1,0:T(8,128)(2,1)} %constant.20.clone.refs_16_) | copy-start | bytes 1572868
  3.5 34.0 %copy-start.2 = (bf16[512,512]{1,0:T(8,128)(2,1)S(1)}, bf16[512,512]{1,0:T(8,128)(2,1)}, u32[]{:S(2)}) copy-start(bf16[512,512]{1,0:T(8,128)(2,1)} %constant.21.clone.refs_17_) | copy-start | bytes 1572868
  3.5 34.1 %copy-start.3 = (bf16[4,256,256]{2,1,0:T(8,128)(2,1)S(1)}, bf16[4,256,256]{2,1,0:T(8,128)(2,1)}, u32[]{:S(2)}) copy-start(bf16[4,256,256]{2,1,0:T(8,128)(2,1)} %constant.23.clone.refs_19_) | copy-start | bytes 1572868
  3.5 34.1 %copy-start.4 = (bf16[512,512]{1,0:T(8,128)(2,1)S(1)}, bf16[512,512]{1,0:T(8,128)(2,1)}, u32[]{:S(2)}) copy-start(bf16[512,512]{1,0:T(8,128)(2,1)} %constant.24.clone.refs_20_) | copy-start | bytes 1572868
  3.5 34.1 %copy-start.5 = (s32[1,4]{1,0:T(1,128)S(1)}, s32[1,4]{1,0:T(1,128)}, u32[]{:S(2)}) copy-start(s32[1,4]{1,0:T(1,128)} %refs_1_.1) | copy-start | bytes 52
  3.5 34.1 %copy-start.6 = (s32[1,4]{1,0:T(1,128)S(1)}, s32[1,4]{1,0:T(1,128)}, u32[]{:S(2)}) copy-start(s32[1,4]{1,0:T(1,128)} %refs_2_.1) | copy-start | bytes 52
  4.7 17.4 %collective-permute-start.1 = (bf16[2,256,512]{2,1,0:T(8,128)(2,1)S(1)}, bf16[2,256,512]{2,1,0:T(8,128)(2,1)S(1)}, u32[]{:S(2)}, u32[]{:S(2)}) collective-permute-start(bf16[2,256,512]{2,1,0:T(8,128)(2,1)S(1)} %slice.119), channel_id=1, source_target_pairs={{0,24},{8,0},{16,8},{24,16},{1,25},{9,1},{17,9},{25,17},{2,26},{10... | collective-permute-start | bytes 1572872 | tf_op jit(solution)/shard_map/ppermute | solution.py:381
  9.9 27.6 %collective-permute-start = (bf16[2,512,512]{2,1,0:T(8,128)(2,1)}, bf16[2,512,512]{2,1,0:T(8,128)(2,1)}, u32[]{:S(2)}, u32[]{:S(2)}) collective-permute-start(bf16[2,512,512]{2,1,0:T(8,128)(2,1)} %maximum_convert_fusion), channel_id=1, source_target_pairs={{0,7},{1,0},{2,1},{3,2},{4,3},{5,4},{6,5},{7,6},{8,15},{9,8},{10,9... | collective-permute-start | bytes 3145736 | tf_op jit(solution)/shard_map/ppermute | solution.py:381
  12.5 15.6 %collective-permute-start.2 = (bf16[2,160,512]{2,1,0:T(8,128)(2,1)S(1)}, bf16[2,160,512]{2,1,0:T(8,128)(2,1)S(1)}, u32[]{:S(2)}, u32[]{:S(2)}) collective-permute-start(bf16[2,160,512]{2,1,0:T(8,128)(2,1)S(1)} %slice.120), channel_id=1, source_target_pairs={{0,24},{8,0},{16,8},{24,16},{1,25},{9,1},{17,9},{25,17},{2,26},{10... | collective-permute-start | bytes 983048 | tf_op jit(solution)/shard_map/ppermute | solution.py:381
  22.2 15.3 %collective-permute-start.4 = (bf16[2,256,512]{2,1,0:T(8,128)(2,1)S(1)}, bf16[2,256,512]{2,1,0:T(8,128)(2,1)S(1)}, u32[]{:S(2)}, u32[]{:S(2)}) collective-permute-start(bf16[2,256,512]{2,1,0:T(8,128)(2,1)S(1)} %collective-permute-done.1.refs_7_), channel_id=1, source_target_pairs={{0,7},{1,0},{2,1},{3,2},{4,3},{5,4},{6,5},{7,6},{8,15},{9,8},{10,9... | collective-permute-start | bytes 1572872 | tf_op jit(solution)/shard_map/ppermute | solution.py:381
  23.1 9.2 %collective-permute-start.3 = (bf16[2,96,512]{2,1,0:T(8,128)(2,1)S(1)}, bf16[2,96,512]{2,1,0:T(8,128)(2,1)}, u32[]{:S(2)}, u32[]{:S(2)}) collective-permute-start(bf16[2,96,512]{2,1,0:T(8,128)(2,1)S(1)} %slice.121), channel_id=1, source_target_pairs={{0,24},{8,0},{16,8},{24,16},{1,25},{9,1},{17,9},{25,17},{2,26},{10... | collective-permute-start | bytes 589832 | tf_op jit(solution)/shard_map/ppermute | solution.py:381
  28.1 9.4 %collective-permute-start.5 = (bf16[2,160,512]{2,1,0:T(8,128)(2,1)S(1)}, bf16[2,160,512]{2,1,0:T(8,128)(2,1)}, u32[]{:S(2)}, u32[]{:S(2)}) collective-permute-start(bf16[2,160,512]{2,1,0:T(8,128)(2,1)S(1)} %collective-permute-done.2.refs_8_), channel_id=1, source_target_pairs={{0,7},{1,0},{2,1},{3,2},{4,3},{5,4},{6,5},{7,6},{8,15},{9,8},{10,9... | collective-permute-start | bytes 983048 | tf_op jit(solution)/shard_map/ppermute | solution.py:381
  32.3 5.2 %collective-permute-start.6 = (bf16[2,96,512]{2,1,0:T(8,128)(2,1)}, bf16[2,96,512]{2,1,0:T(8,128)(2,1)}, u32[]{:S(2)}, u32[]{:S(2)}) collective-permute-start(bf16[2,96,512]{2,1,0:T(8,128)(2,1)} %collective-permute-done.3.refs_9_), channel_id=1, source_target_pairs={{0,7},{1,0},{2,1},{3,2},{4,3},{5,4},{6,5},{7,6},{8,15},{9,8},{10,9... | collective-permute-start | bytes 589832 | tf_op jit(solution)/shard_map/ppermute | solution.py:381
  54.3 39.1 %copy-start.9 = (f32[2,256,512]{2,1,0:T(8,128)S(1)}, f32[2,256,512]{2,1,0:T(8,128)}, u32[]{:S(2)}) copy-start(f32[2,256,512]{2,1,0:T(8,128)} %get-tuple-element.17) | copy-start | bytes 3145732
  54.4 12.4 %collective-permute-start.14 = (f32[2,1024]{1,0:T(2,128)S(1)}, f32[2,1024]{1,0:T(2,128)S(1)}, u32[]{:S(2)}, u32[]{:S(2)}) collective-permute-start(f32[2,1024]{1,0:T(2,128)S(1)} %get-tuple-element.36), channel_id=1, source_target_pairs={{0,1},{1,2},{2,3},{3,4},{4,5},{5,6},{6,7},{7,0},{8,9},{9,10},{10,1... | collective-permute-start | bytes 24584 | tf_op jit(solution)/shard_map/ppermute | solution.py:381
  54.4 13.0 %collective-permute-start.15 = (f32[2,1024]{1,0:T(2,128)S(1)}, f32[2,1024]{1,0:T(2,128)S(1)}, u32[]{:S(2)}, u32[]{:S(2)}) collective-permute-start(f32[2,1024]{1,0:T(2,128)S(1)} %get-tuple-element.34), channel_id=1, source_target_pairs={{0,2},{1,3},{2,4},{3,5},{4,6},{5,7},{6,0},{7,1},{8,10},{9,11},{10,... | collective-permute-start | bytes 24584 | tf_op jit(solution)/shard_map/ppermute | solution.py:381
  61.4 7.6 %collective-permute-start.16 = (f32[2,1024]{1,0:T(2,128)S(1)}, f32[2,1024]{1,0:T(2,128)S(1)}, u32[]{:S(2)}, u32[]{:S(2)}) collective-permute-start(f32[2,1024]{1,0:T(2,128)S(1)} %get-tuple-element.35), channel_id=1, source_target_pairs={{0,7},{1,0},{2,1},{3,2},{4,3},{5,4},{6,5},{7,6},{8,15},{9,8},{10,9... | collective-permute-start | bytes 24584 | tf_op jit(solution)/shard_map/ppermute | solution.py:381
  66.2 33.4 %collective-permute-start.7 = (bf16[2,512,512]{2,1,0:T(8,128)(2,1)S(1)}, bf16[2,512,512]{2,1,0:T(8,128)(2,1)S(1)}, u32[]{:S(2)}, u32[]{:S(2)}) collective-permute-start(bf16[2,512,512]{2,1,0:T(8,128)(2,1)S(1)} %get-tuple-element.12), channel_id=1, source_target_pairs={{0,1},{1,2},{2,3},{3,4},{4,5},{5,6},{6,7},{7,0},{8,9},{9,10},{10,1... | collective-permute-start | bytes 3145736 | tf_op jit(solution)/shard_map/ppermute | solution.py:381
  66.2 16.5 %collective-permute-start.8 = (bf16[2,64,512]{2,1,0:T(8,128)(2,1)S(1)}, bf16[2,64,512]{2,1,0:T(8,128)(2,1)S(1)}, u32[]{:S(2)}, u32[]{:S(2)}) collective-permute-start(bf16[2,64,512]{2,1,0:T(8,128)(2,1)S(1)} %get-tuple-element.14), channel_id=1, source_target_pairs={{0,1},{1,2},{2,3},{3,4},{4,5},{5,6},{6,7},{7,0},{8,9},{9,10},{10,1... | collective-permute-start | bytes 393224 | tf_op jit(solution)/shard_map/ppermute | solution.py:381
  66.7 26.7 %collective-permute-start.12 = (bf16[2,256,512]{2,1,0:T(8,128)(2,1)S(1)}, bf16[2,256,512]{2,1,0:T(8,128)(2,1)S(1)}, u32[]{:S(2)}, u32[]{:S(2)}) collective-permute-start(bf16[2,256,512]{2,1,0:T(8,128)(2,1)S(1)} %get-tuple-element.18), channel_id=1, source_target_pairs={{0,1},{1,2},{2,3},{3,4},{4,5},{5,6},{6,7},{7,0},{8,9},{9,10},{10,1... | collective-permute-start | bytes 1572872 | tf_op jit(solution)/shard_map/ppermute | solution.py:381
  67.4 25.1 %collective-permute-start.10 = (bf16[2,192,512]{2,1,0:T(8,128)(2,1)S(1)}, bf16[2,192,512]{2,1,0:T(8,128)(2,1)S(1)}, u32[]{:S(2)}, u32[]{:S(2)}) collective-permute-start(bf16[2,192,512]{2,1,0:T(8,128)(2,1)S(1)} %get-tuple-element.16), channel_id=1, source_target_pairs={{0,1},{1,2},{2,3},{3,4},{4,5},{5,6},{6,7},{7,0},{8,9},{9,10},{10,1... | collective-permute-start | bytes 1179656 | tf_op jit(solution)/shard_map/ppermute | solution.py:381
  69.0 13.7 %copy-start.10 = (f32[2,1024]{1,0:T(2,128)}, f32[2,1024]{1,0:T(2,128)S(1)}, u32[]{:S(2)}) copy-start(f32[2,1024]{1,0:T(2,128)S(1)} %fusion) | copy-start | bytes 24580
  83.4 40.6 %collective-permute-start.9 = (bf16[2,64,512]{2,1,0:T(8,128)(2,1)}, bf16[2,64,512]{2,1,0:T(8,128)(2,1)}, u32[]{:S(2)}, u32[]{:S(2)}) collective-permute-start(bf16[2,64,512]{2,1,0:T(8,128)(2,1)} %get-tuple-element.30), channel_id=1, source_target_pairs={{0,8},{8,16},{16,24},{24,0},{1,9},{9,17},{17,25},{25,1},{2,10},{10... | collective-permute-start | bytes 393224 | tf_op jit(solution)/shard_map/ppermute | solution.py:381
  92.5 7.0 %copy-start = (f32[2,512,512]{2,1,0:T(8,128)S(1)}, f32[2,512,512]{2,1,0:T(8,128)}, u32[]{:S(2)}) copy-start(f32[2,512,512]{2,1,0:T(8,128)} %get-tuple-element.11.refs_0_) | copy-start | bytes 6291460
  93.4 30.6 %collective-permute-start.11 = (bf16[2,192,512]{2,1,0:T(8,128)(2,1)}, bf16[2,192,512]{2,1,0:T(8,128)(2,1)S(1)}, u32[]{:S(2)}, u32[]{:S(2)}) collective-permute-start(bf16[2,192,512]{2,1,0:T(8,128)(2,1)} %add_convert_fusion), channel_id=1, source_target_pairs={{0,8},{8,16},{16,24},{24,0},{1,9},{9,17},{17,25},{25,1},{2,10},{10... | collective-permute-start | bytes 1179656 | tf_op jit(solution)/shard_map/ppermute | solution.py:381
  95.2 27.4 %collective-permute-start.18 = (f32[2,6,128]{2,1,0:T(8,128)}, f32[2,6,128]{2,1,0:T(8,128)}, u32[]{:S(2)}, u32[]{:S(2)}) collective-permute-start(f32[2,6,128]{2,1,0:T(8,128)} %pad_maximum_fusion.1), channel_id=1, source_target_pairs={{0,16},{8,24},{16,0},{24,8},{1,17},{9,25},{17,1},{25,9},{2,18},{10... | collective-permute-start | bytes 18440 | tf_op jit(solution)/shard_map/ppermute | solution.py:381
  96.8 27.3 %collective-permute-start.13 = (bf16[2,256,512]{2,1,0:T(8,128)(2,1)}, bf16[2,256,512]{2,1,0:T(8,128)(2,1)}, u32[]{:S(2)}, u32[]{:S(2)}) collective-permute-start(bf16[2,256,512]{2,1,0:T(8,128)(2,1)} %get-tuple-element.28), channel_id=1, source_target_pairs={{0,8},{8,16},{16,24},{24,0},{1,9},{9,17},{17,25},{25,1},{2,10},{10... | collective-permute-start | bytes 1572872 | tf_op jit(solution)/shard_map/ppermute | solution.py:381
  99.7 10.8 %collective-permute-start.19 = (f32[2,6,128]{2,1,0:T(8,128)S(1)}, f32[2,6,128]{2,1,0:T(8,128)S(1)}, u32[]{:S(2)}, u32[]{:S(2)}) collective-permute-start(f32[2,6,128]{2,1,0:T(8,128)S(1)} %pad_maximum_fusion.2), channel_id=1, source_target_pairs={{0,24},{8,0},{16,8},{24,16},{1,25},{9,1},{17,9},{25,17},{2,26},{10... | collective-permute-start | bytes 18440 | tf_op jit(solution)/shard_map/ppermute | solution.py:381
  110.5 8.1 %collective-permute-start.17 = (f32[2,14,128]{2,1,0:T(8,128)S(1)}, f32[2,14,128]{2,1,0:T(8,128)S(1)}, u32[]{:S(2)}, u32[]{:S(2)}) collective-permute-start(f32[2,14,128]{2,1,0:T(8,128)S(1)} %pad_maximum_fusion), channel_id=1, source_target_pairs={{0,8},{8,16},{16,24},{24,0},{1,9},{9,17},{17,25},{25,1},{2,10},{10... | collective-permute-start | bytes 43016 | tf_op jit(solution)/shard_map/ppermute | solution.py:381
  118.6 0.6 copy-start.11

commit v3 on v2

--- a/solution.py
+++ b/solution.py
@@ -8,6 +8,7 @@
 from jax.experimental import pallas as pl
 from jax.experimental.pallas import tpu as pltpu
 from jax.sharding import PartitionSpec as P
+
 
 modulus_floor = 0.5
 shrink_level = 0.2
@@ -51,7 +52,6 @@
     order = np.concatenate([frequency, mirrored])
     pick = np.zeros((side, side))
     pick[order, every] = 1.0
-    as_bf16 = lambda table: jnp.asarray(np.asarray(table, np.float32)).astype(bf16)
     return tuple(
         np.asarray(np.asarray(table, np.float32), dtype=bf16)
         for table in (np.stack(rows_in), cols_in, np.stack(cols_out), np.stack(rows_out), pick)
@@ -228,7 +228,7 @@
                 cells = scale * sums[p, a, r * LANES : (r + 1) * LANES, :]
                 if k < 2 and r < chunks:
                     cells += own[r * LANES : (r + 1) * LANES, a * LANES : (a + 1) * LANES]
-                edge_out[p, k : k + 1, r * LANES : (r + 1) * LANES] = cells.T[at : at + 1, :]
+                edge_out[k, p : p + 1, r * LANES : (r + 1) * LANES] = cells.T[at : at + 1, :]
 
 
 def run_slots(counts, offset_y, offset_x, scale, obj_re, obj_im, right, below, diag, probe_re, probe_im, amplitude, out_parts):
@@ -240,7 +240,7 @@
     smem = pl.BlockSpec(memory_space=pltpu.SMEM)
     vmem = pl.BlockSpec(memory_space=pltpu.VMEM)
     tile = lambda rows, kind: jax.ShapeDtypeStruct((2, rows, side), kind)
-    outs = [tile(side, f32), tile(side, bf16), jax.ShapeDtypeStruct((2, 4, 2 * side), f32)]
+    outs = [tile(side, f32), tile(side, bf16), jax.ShapeDtypeStruct((4, 2, 2 * side), f32)]
     outs += [tile(rows, f32) for rows in out_parts] + [tile(rows, bf16) for rows in out_parts]
     results = pl.pallas_call(
         functools.partial(slots_kernel, side, in_parts, out_parts),
@@ -258,7 +258,7 @@
             pltpu.VMEM((4, 2 * quarter, side), bf16),
             pltpu.VMEM((chunks, side, LANES), f32),
         ],
-        compiler_params=pltpu.CompilerParams(vmem_limit_bytes=46 * 2**20),
+        compiler_params=pltpu.CompilerParams(vmem_limit_bytes=40 * 2**20),
         name="slots",
     )(counts, offset_y, offset_x, scale, obj_re, obj_im, right, *below, *diag, probe_re, probe_im, amplitude, *tables)
     parts = len(out_parts)
@@ -268,11 +268,20 @@
 def finish_kernel(parts, *refs):
     own_ref, right_ref = refs[:2]
     below_refs = refs[2 : 2 + len(parts)]
-    top_ref, bottom_ref, ring_ref, out_re, out_im, cells, spill, result = refs[2 + len(parts) :]
+    up_ref, far_ref, down_ref, low_ref, left_ref, beside_ref, out_re, out_im, cells, spill, result, ring_ref = refs[
+        2 + len(parts) :
+    ]
     side = own_ref.shape[1]
     chunks = side // LANES
     f32 = jnp.float32
     pad, count = 16, 8
+    rows = chunks + 2
+    for p in range(2):
+        for k, column in enumerate((left_ref, beside_ref)):
+            for a in range(chunks):
+                lanes = slice(a * LANES, (a + 1) * LANES)
+                at = rows + k * chunks + a
+                ring_ref[2 * k + p : 2 * k + p + 1, lanes] = column[p : p + 1, lanes] + up_ref[p, at : at + 1, :]
     ring = ring_ref[...].T
     for p in range(2):
         for a in range(chunks):
@@ -288,8 +297,9 @@
             beside = jnp.broadcast_to(ring[:, 2 * k + p : 2 * k + p + 1], (side, LANES))
             cells[p, k * (chunks + 1), pad : pad + side, :] = beside
         for a in range(chunks + 2):
-            cells[p, a, pad - 1 : pad, :] = top_ref[p, a : a + 1, :]
-            cells[p, a, pad + side : pad + side + 1, :] = bottom_ref[p, a : a + 1, :]
+            one = slice(a, a + 1)
+            cells[p, a, pad - 1 : pad, :] = up_ref[p, one, :] + far_ref[p, one, :]
+            cells[p, a, pad + side : pad + side + 1, :] = down_ref[p, one, :] + low_ref[p, one, :]
 
     bound = 2.0 * shrink_level
     lane = lax.broadcasted_iota(jnp.int32, (count, LANES), 1)
@@ -354,7 +364,7 @@
     lax.fori_loop(0, side // (2 * count), block, 0)
 
 
-def run_finish(own, right, below, top, bottom, ring):
+def run_finish(own, right, below, *edges):
     side = own.shape[1]
     chunks = side // LANES
     f32 = jnp.float32
@@ -364,16 +374,17 @@
     return pl.pallas_call(
         functools.partial(finish_kernel, parts),
         out_shape=(tile, tile),
-        in_specs=[vmem] * (5 + len(parts)),
+        in_specs=[vmem] * (2 + len(parts) + len(edges)),
         out_specs=[vmem] * 2,
         scratch_shapes=[
             pltpu.VMEM((2, chunks + 2, side + 32, LANES), f32),
             pltpu.VMEM((2, chunks, side // 2 + 16, LANES), f32),
             pltpu.VMEM((2, chunks, side, LANES), f32),
+            pltpu.VMEM((8, side), f32),
         ],
         compiler_params=pltpu.CompilerParams(vmem_limit_bytes=20 * 2**20),
         name="finish",
-    )(own, right, *below, top, bottom, ring)
+    )(own, right, *below, *edges)
 
 
 def shifted(value, axis, steps):
@@ -393,55 +404,58 @@
     return [value[:, end - size : end] for end, size in zip(ends, sizes)]
 
 
-def body(obj_re, obj_im, probe_re, probe_im, amplitude, offset_y, offset_x, counts):
+def update(obj_re, obj_im, probe_re, probe_im, amplitude, offset_y, offset_x, counts):
     f32, bf16 = jnp.float32, jnp.bfloat16
     side = probe_re.shape[0]
-    in_parts, out_parts = parts_of(side, (16, 10, 6)), parts_of(side, (4, 12, 16))
+    in_parts, out_parts = parts_of(side, IN_SHARES), parts_of(side, OUT_SHARES)
+
+    head = in_parts[0]
+    piece = jnp.stack([obj_re[:head], obj_im[:head]]).astype(bf16)
+    piece, later_re, later_im = lax.optimization_barrier((piece, obj_re, obj_im))
+    below = [shifted(piece, "row", -1)]
+    own = jnp.stack([later_re, later_im]).astype(bf16)
+    right = shifted(own, "col", -1)
+    for rest in split_rows(own, in_parts)[1:]:
+        below.append(shifted(rest, "row", -1))
+    diag = [shifted(value, "col", -1) for value in below]
     probe_power = jnp.mean(probe_re * probe_re + probe_im * probe_im) + epsilon
     scale = (step_size / probe_power).reshape(1, 1)
-    own = jnp.stack([obj_re, obj_im])
-    pieces = [piece.astype(bf16) for piece in split_rows(own, in_parts)]
-    below = [shifted(piece, "row", -1) for piece in pieces]
-    right = shifted(own.astype(bf16), "col", -1)
-    diag = [shifted(piece, "col", -1) for piece in below]
     own_sum, right_sum, edges, below_sum, diag_sum = run_slots(
         counts, offset_y, offset_x, scale, obj_re, obj_im, right, below, diag, probe_re, probe_im, amplitude, out_parts
     )
 
-    diag_in = [shifted(piece, "col", 1) for piece in diag_sum]
+    diag_in = [shifted(value, "col", 1) for value in diag_sum]
+    beside_right = shifted(edges[0], "col", -1) + edges[2]
+    beside_left = shifted(edges[1], "col", 1) + shifted(edges[3], "col", 2)
     right_in = shifted(right_sum, "col", 1)
-    beside_right = shifted(edges[:, 0], "col", -1) + edges[:, 2]
-    beside_left = shifted(edges[:, 1], "col", 1) + shifted(edges[:, 3], "col", 2)
     lower = [mine + theirs.astype(f32) for mine, theirs in zip(below_sum, diag_in)]
-    below_in = [shifted(piece.astype(bf16), "row", 1) for piece in lower]
+    below_in = [shifted(value.astype(bf16), "row", 1) for value in lower]
 
     def with_ends(row, at):
         chunks = row.reshape(2, side // LANES, LANES)
         ends = [jnp.broadcast_to(column[:, at, None, None], (2, 1, LANES)) for column in (beside_left, beside_right)]
         return jnp.concatenate([ends[0], chunks, ends[1]], axis=1)
 
+    low_first = with_ends(lower[0][:, 0], side)
+    low_last = with_ends(lower[-1][:, -1], 2 * side - 1)
+    from_far = shifted(low_last, "row", 2)
     first = with_ends(own_sum[:, 0] + right_in[:, 0].astype(f32), 0)
     last = with_ends(own_sum[:, -1] + right_in[:, -1].astype(f32), side - 1)
-    low_first = with_ends(lower[0][:, 0], side)
-    low_last = with_ends(lower[-1][:, -1], 2 * side - 1)
     sides = jnp.concatenate([beside_left[:, side:], beside_right[:, side:]], axis=1)
     sent_down = jnp.concatenate([last, sides.reshape(2, -1, LANES)], axis=1)
     from_up = shifted(sent_down, "row", 1)
     from_down = shifted(first, "row", -1)
-    from_far = shifted(low_last, "row", 2)
-    rows = side // LANES + 2
-    top = from_up[:, :rows] + from_far
-    bottom = from_down + low_first
-    spilled = from_up[:, rows:].reshape(2, 2, side)
-    ring = jnp.concatenate([beside_left[:, :side] + spilled[:, 0], beside_right[:, :side] + spilled[:, 1]], axis=0)
-    ring = jnp.concatenate([ring, jnp.zeros((4, side), f32)], axis=0)
-    return run_finish(own_sum, right_in, below_in, top, bottom, ring)
+    return run_finish(own_sum, right_in, below_in, from_up, from_far, from_down, low_first, beside_left, beside_right)
+
+
+IN_SHARES = (16, 10, 6)
+OUT_SHARES = (4, 12, 16)
 
 
 def solution(mesh):
     split = P("row", "col")
     return jax.shard_map(
-        body,
+        update,
         mesh=mesh,
         in_specs=(split, split, P(), P(), P("row", "col", None, None), split, split, split),
         out_specs=(split, split),

time: 132 us -> 109 us (0.83)
  waiting for transfers between devices: 48.2 us -> 31.3 us
  other arithmetic: 9.13 us -> 2.69 us
  Pallas kernels: 25.3 us -> 18.9 us
  starting transfers between devices: 39.5 us -> 45.6 us
    ppermute x20, waiting for transfers between devices: 48.2 us -> 31.3 us  [shifted(): lax.ppermute(value, axis, [(i, (i + steps) % count) for i in range(count)])]
    ppermute x20, starting transfers between devices: 39.5 us -> 45.6 us  [shifted(): lax.ppermute(value, axis, [(i, (i + steps) % count) for i in range(count)])]
    pallas_call x1, Pallas kernels: 16.8 us -> 11.4 us  [run_slots(): pl.pallas_call(functools.partial(slots_kernel, side, in_parts, out_parts)...]
    convert_element_type x4 -> x3, other arithmetic: 5.38 us -> 0.38 us  [update(): below_in = [shifted(value.astype(bf16), 'row', 1) for value in lower]]
    unnamed x25, local copies, waits for them, and re-layouts: 0.65 us -> 5.42 us
    slice x9 -> x4, local copies, waits for them, and re-layouts: 4.58 us -> 0.01 us  [the longest x1 0.01 us: update(): low_last = with_ends(lower[-1][:, -1], 2 * side - 1)]
    add x6 -> x3, other arithmetic: 1.44 us -> 0.03 us  [the longest x1 0.01 us: update(): first = with_ends(own_sum[:, 0] + right_in[:, 0].astype(f32), 0)]
    another operation x0 -> x1, local copies, waits for them, and re-layouts: none -> 1.41 us  [update(): piece = jnp.stack([obj_re[:head], obj_im[:head]]).astype(bf16)]
  transfers between devices with their start and end apart: 20 -> 20, of which waited for: 10 -> 10; matrix products, arithmetic and copies ran while one was open for 10% -> 3% of each run, Pallas kernels for 0% -> 0%
where the time goes in v3:
time: 109 us
  starting transfers between devices  45.6 us (42%)
  waiting for transfers between devices  31.3 us (29%)
  Pallas kernels  18.9 us (17%)
  local copies, waits for them, and re-layouts  7.84 us (7%)
  other arithmetic  2.69 us (2%)
  between operations  2.23 us (2%)
    ppermute x20, starting transfers between devices, shifted(): lax.ppermute(value, axis, [(i, (i + steps) % count) for i in range(count)])  45.6 us
    ppermute x20, waiting for transfers between devices, shifted(): lax.ppermute(value, axis, [(i, (i + steps) % count) for i in range(count)])  31.3 us
    pallas_call x1, Pallas kernels, run_slots(): pl.pallas_call(functools.partial(slots_kernel, side, in_parts, out_parts)...  11.4 us
    pallas_call x1, Pallas kernels, run_finish(): pl.pallas_call(functools.partial(finish_kernel, parts), out_shape=(tile,...  7.48 us
    unnamed x25, local copies, waits for them, and re-layouts  5.42 us
  transfers between devices with their start and end apart: 20, of which 10 were waited for; matrix products, arithmetic and copies ran while one was open for 3% of the time, Pallas kernels for 0%

profile of v3, /device:TPU:0, one launch (start us, length us, event | category | flops | bytes accessed | tf_op | source)
XLA Modules:
  0.0 108.6 jit_solution(14818318183322547737)
XLA Ops:
  0.6 1.4 %fusion.1 = (bf16[1,256,512]{2,1,0:T(8,128)(2,1)S(1)}, bf16[1,256,512]{2,1,0:T(8,128)(2,1)S(1)}) fusion(f32[512,512]{1,0:T(8,128)} %refs_4_.1, f32[512,512]{1,0:T(8,128)} %refs_5_.1), kind=kLoop, calls=%fused_computation.14 | loop fusion | bytes 1048576 | tf_op jit(solution)/shard_map/stack | solution.py:413
  2.1 5.1 %collective-permute-start.1 = (bf16[2,256,512]{2,1,0:T(8,128)(2,1)S(1)}, bf16[2,256,512]{2,1,0:T(8,128)(2,1)}, u32[]{:S(2)}, u32[]{:S(2)}) collective-permute-start(bf16[2,256,512]{2,1,0:T(8,128)(2,1)S(1)} %pad_maximum_fusion.1), channel_id=1, source_target_pairs={{0,24},{8,0},{16,8},{24,16},{1,25},{9,1},{17,9},{25,17},{2,26},{10... | collective-permute-start | bytes 1572872 | tf_op jit(solution)/shard_map/ppermute | solution.py:392
  7.4 1.1 pad_maximum_fusion
  8.5 1.6 %collective-permute-start = (bf16[2,512,512]{2,1,0:T(8,128)(2,1)}, bf16[2,512,512]{2,1,0:T(8,128)(2,1)}, u32[]{:S(2)}, u32[]{:S(2)}) collective-permute-start(bf16[2,512,512]{2,1,0:T(8,128)(2,1)} %pad_maximum_fusion), channel_id=1, source_target_pairs={{0,7},{1,0},{2,1},{3,2},{4,3},{5,4},{6,5},{7,6},{8,15},{9,8},{10,9... | collective-permute-start | bytes 3145736 | tf_op jit(solution)/shard_map/ppermute | solution.py:392
  10.1 0.6 collective-permute-start.2
  10.7 8.9 %collective-permute-done.1.refs_7_ = bf16[2,256,512]{2,1,0:T(8,128)(2,1)} collective-permute-done((bf16[2,256,512]{2,1,0:T(8,128)(2,1)S(1)}, bf16[2,256,512]{2,1,0:T(8,128)(2,1)}, u32[]{:S(2)}, u32[]{:S(2)}) %collective-permute-start.1) | collective-permute-done | bytes 524320 | tf_op jit(solution)/shard_map/ppermute | solution.py:392
  19.6 4.4 %collective-permute-start.3 = (bf16[2,96,512]{2,1,0:T(8,128)(2,1)S(1)}, bf16[2,96,512]{2,1,0:T(8,128)(2,1)}, u32[]{:S(2)}, u32[]{:S(2)}) collective-permute-start(bf16[2,96,512]{2,1,0:T(8,128)(2,1)S(1)} %fusion.3), channel_id=1, source_target_pairs={{0,24},{8,0},{16,8},{24,16},{1,25},{9,1},{17,9},{25,17},{2,26},{10... | collective-permute-start | bytes 589832 | tf_op jit(solution)/shard_map/ppermute | solution.py:392
  24.0 2.2 %collective-permute-done.2.refs_8_ = bf16[2,160,512]{2,1,0:T(8,128)(2,1)S(1)} collective-permute-done((bf16[2,160,512]{2,1,0:T(8,128)(2,1)S(1)}, bf16[2,160,512]{2,1,0:T(8,128)(2,1)S(1)}, u32[]{:S(2)}, u32[]{:S(2)}) %collective-permute-start.2) | collective-permute-done | bytes 327712 | tf_op jit(solution)/shard_map/ppermute | solution.py:392
  26.5 3.2 %collective-permute-done.3.refs_9_ = bf16[2,96,512]{2,1,0:T(8,128)(2,1)} collective-permute-done((bf16[2,96,512]{2,1,0:T(8,128)(2,1)S(1)}, bf16[2,96,512]{2,1,0:T(8,128)(2,1)}, u32[]{:S(2)}, u32[]{:S(2)}) %collective-permute-start.3) | collective-permute-done | bytes 196640 | tf_op jit(solution)/shard_map/ppermute | solution.py:392
  29.7 1.4 %collective-permute-start.6 = (bf16[2,96,512]{2,1,0:T(8,128)(2,1)}, bf16[2,96,512]{2,1,0:T(8,128)(2,1)}, u32[]{:S(2)}, u32[]{:S(2)}) collective-permute-start(bf16[2,96,512]{2,1,0:T(8,128)(2,1)} %collective-permute-done.3.refs_9_), channel_id=1, source_target_pairs={{0,7},{1,0},{2,1},{3,2},{4,3},{5,4},{6,5},{7,6},{8,15},{9,8},{10,9... | collective-permute-start | bytes 589832 | tf_op jit(solution)/shard_map/ppermute | solution.py:392
  31.7 0.9 add_reduce_fusion
  33.3 1.2 %collective-permute-done.6.refs_12_ = bf16[2,96,512]{2,1,0:T(8,128)(2,1)} collective-permute-done((bf16[2,96,512]{2,1,0:T(8,128)(2,1)}, bf16[2,96,512]{2,1,0:T(8,128)(2,1)}, u32[]{:S(2)}, u32[]{:S(2)}) %collective-permute-start.6) | collective-permute-done | bytes 196640 | tf_op jit(solution)/shard_map/ppermute | solution.py:392
  34.6 1.2 %copy-done.4 = f32[512,512]{1,0:T(8,128)S(1)} copy-done((f32[512,512]{1,0:T(8,128)S(1)}, f32[512,512]{1,0:T(8,128)}, u32[]{:S(2)}) %copy-start.4) | copy-done | bytes 1048600
  35.8 1.0 copy-done.6
  36.8 1.0 copy-done.7
  37.9 1.0 copy-done.8
  38.9 1.0 copy-done.9
  40.0 11.4 %slots.1 = (f32[2,512,512]{2,1,0:T(8,128)}, bf16[2,512,512]{2,1,0:T(8,128)(2,1)S(1)}, f32[4,2,1024]{2,1,0:T(2,128)S(1)}, f32[2,64,512]{2,1,0:T(8,128)S(1)}, f32[...) custom-call(s32[1,1]{1,0:T(1,128)S(6)} %copy.18.refs_0_, ...), custom_call_target="tpu_custom_call" | custom-call | tf_op jit(solution)/shard_map/slots/pallas_call | solution.py:245
  51.4 2.9 %collective-permute-start.16 = (f32[2,1024]{1,0:T(2,128)S(1)}, f32[2,1024]{1,0:T(2,128)S(1)}, u32[]{:S(2)}, u32[]{:S(2)}) collective-permute-start(f32[2,1024]{1,0:T(2,128)S(1)} %get-tuple-element.41), channel_id=1, source_target_pairs={{0,7},{1,0},{2,1},{3,2},{4,3},{5,4},{6,5},{7,6},{8,15},{9,8},{10,9... | collective-permute-start | bytes 24584 | tf_op jit(solution)/shard_map/ppermute | solution.py:392
  54.3 3.3 %collective-permute-start.14 = (f32[2,1024]{1,0:T(2,128)S(1)}, f32[2,1024]{1,0:T(2,128)S(1)}, u32[]{:S(2)}, u32[]{:S(2)}) collective-permute-start(f32[2,1024]{1,0:T(2,128)S(1)} %get-tuple-element.42), channel_id=1, source_target_pairs={{0,1},{1,2},{2,3},{3,4},{4,5},{5,6},{6,7},{7,0},{8,9},{9,10},{10,1... | collective-permute-start | bytes 24584 | tf_op jit(solution)/shard_map/ppermute | solution.py:392
  57.6 8.3 %collective-permute-start.8 = (bf16[2,64,512]{2,1,0:T(8,128)(2,1)S(1)}, bf16[2,64,512]{2,1,0:T(8,128)(2,1)S(1)}, u32[]{:S(2)}, u32[]{:S(2)}) collective-permute-start(bf16[2,64,512]{2,1,0:T(8,128)(2,1)S(1)} %get-tuple-element.20), channel_id=1, source_target_pairs={{0,1},{1,2},{2,3},{3,4},{4,5},{5,6},{6,7},{7,0},{8,9},{9,10},{10,1... | collective-permute-start | bytes 393224 | tf_op jit(solution)/shard_map/ppermute | solution.py:392
  67.1 5.3 %collective-permute-start.9 = (bf16[2,64,512]{2,1,0:T(8,128)(2,1)S(1)}, bf16[2,64,512]{2,1,0:T(8,128)(2,1)S(1)}, u32[]{:S(2)}, u32[]{:S(2)}) collective-permute-start(bf16[2,64,512]{2,1,0:T(8,128)(2,1)S(1)} %get-tuple-element.36), channel_id=1, source_target_pairs={{0,8},{8,16},{16,24},{24,0},{1,9},{9,17},{17,25},{25,1},{2,10},{10... | collective-permute-start | bytes 393224 | tf_op jit(solution)/shard_map/ppermute | solution.py:392
  72.4 1.6 %collective-permute-done.10 = bf16[2,192,512]{2,1,0:T(8,128)(2,1)S(1)} collective-permute-done((bf16[2,192,512]{2,1,0:T(8,128)(2,1)S(1)}, bf16[2,192,512]{2,1,0:T(8,128)(2,1)S(1)}, u32[]{:S(2)}, u32[]{:S(2)}) %collective-permute-start.10) | collective-permute-done | bytes 393248 | tf_op jit(solution)/shard_map/ppermute | solution.py:392
  74.1 2.6 %collective-permute-start.11 = (bf16[2,192,512]{2,1,0:T(8,128)(2,1)S(1)}, bf16[2,192,512]{2,1,0:T(8,128)(2,1)S(1)}, u32[]{:S(2)}, u32[]{:S(2)}) collective-permute-start(bf16[2,192,512]{2,1,0:T(8,128)(2,1)S(1)} %add_convert_fusion), channel_id=1, source_target_pairs={{0,8},{8,16},{16,24},{24,0},{1,9},{9,17},{17,25},{25,1},{2,10},{10... | collective-permute-start | bytes 1179656 | tf_op jit(solution)/shard_map/ppermute | solution.py:392
  76.7 2.9 %collective-permute-done.12 = bf16[2,256,512]{2,1,0:T(8,128)(2,1)S(1)} collective-permute-done((bf16[2,256,512]{2,1,0:T(8,128)(2,1)S(1)}, bf16[2,256,512]{2,1,0:T(8,128)(2,1)S(1)}, u32[]{:S(2)}, u32[]{:S(2)}) %collective-permute-start.12) | collective-permute-done | bytes 524320 | tf_op jit(solution)/shard_map/ppermute | solution.py:392
  80.0 3.8 %collective-permute-start.18 = (f32[2,6,128]{2,1,0:T(8,128)S(1)}, f32[2,6,128]{2,1,0:T(8,128)S(1)}, u32[]{:S(2)}, u32[]{:S(2)}) collective-permute-start(f32[2,6,128]{2,1,0:T(8,128)S(1)} %pad_maximum_fusion.3), channel_id=1, source_target_pairs={{0,16},{8,24},{16,0},{24,8},{1,17},{9,25},{17,1},{25,9},{2,18},{10... | collective-permute-start | bytes 18440 | tf_op jit(solution)/shard_map/ppermute | solution.py:392
  83.8 1.1 %collective-permute-start.13 = (bf16[2,256,512]{2,1,0:T(8,128)(2,1)S(1)}, bf16[2,256,512]{2,1,0:T(8,128)(2,1)S(1)}, u32[]{:S(2)}, u32[]{:S(2)}) collective-permute-start(bf16[2,256,512]{2,1,0:T(8,128)(2,1)S(1)} %get-tuple-element.34), channel_id=1, source_target_pairs={{0,8},{8,16},{16,24},{24,0},{1,9},{9,17},{17,25},{25,1},{2,10},{10... | collective-permute-start | bytes 1572872 | tf_op jit(solution)/shard_map/ppermute | solution.py:392
  84.9 6.0 %collective-permute-done.7.refs_1_ = bf16[2,512,512]{2,1,0:T(8,128)(2,1)S(1)} collective-permute-done((bf16[2,512,512]{2,1,0:T(8,128)(2,1)S(1)}, bf16[2,512,512]{2,1,0:T(8,128)(2,1)S(1)}, u32[]{:S(2)}, u32[]{:S(2)}) %collective-permute-start.7) | collective-permute-done | bytes 1048608 | tf_op jit(solution)/shard_map/ppermute | solution.py:392
  91.0 4.3 %collective-permute-start.19 = (f32[2,6,128]{2,1,0:T(8,128)S(1)}, f32[2,6,128]{2,1,0:T(8,128)S(1)}, u32[]{:S(2)}, u32[]{:S(2)}) collective-permute-start(f32[2,6,128]{2,1,0:T(8,128)S(1)} %pad_maximum_fusion.4), channel_id=1, source_target_pairs={{0,24},{8,0},{16,8},{24,16},{1,25},{9,1},{17,9},{25,17},{2,26},{10... | collective-permute-start | bytes 18440 | tf_op jit(solution)/shard_map/ppermute | solution.py:392
  95.7 2.4 %collective-permute-done.18.refs_6_ = f32[2,6,128]{2,1,0:T(8,128)S(1)} collective-permute-done((f32[2,6,128]{2,1,0:T(8,128)S(1)}, f32[2,6,128]{2,1,0:T(8,128)S(1)}, u32[]{:S(2)}, u32[]{:S(2)}) %collective-permute-start.18) | collective-permute-done | bytes 6176 | tf_op jit(solution)/shard_map/ppermute | solution.py:392
  98.2 2.9 %collective-permute-done.17.refs_5_ = f32[2,14,128]{2,1,0:T(8,128)S(1)} collective-permute-done((f32[2,14,128]{2,1,0:T(8,128)S(1)}, f32[2,14,128]{2,1,0:T(8,128)S(1)}, u32[]{:S(2)}, u32[]{:S(2)}) %collective-permute-start.17) | collective-permute-done | bytes 14368 | tf_op jit(solution)/shard_map/ppermute | solution.py:392
  101.1 7.5 %finish.1 = (f32[512,512]{1,0:T(8,128)}, f32[512,512]{1,0:T(8,128)}) custom-call(f32[2,512,512]{2,1,0:T(8,128)S(1)} %copy-done.5, bf16[2,512,512]{2,1,0:T(8,128)(2,1)S(1)} %collective-permute-done.7.refs_1_, bf16[2,64,512]{2,1,0:T(8,128)(2,1)S(1)} %collective-permute-done.9.refs_2_, bf16[2,192,512]{2,1,0:T(8,128)(2,1)S(1)} %collective-permute-done.11.refs_3_, ...), custom_call_target="tpu_custom_call" | custom-call | tf_op jit(solution)/shard_map/finish/pallas_call | solution.py:374
  (69 shorter events, 2.8 us)
Async XLA Ops:
  0.6 6.7 %copy-start.1 = (f32[512,512]{1,0:T(8,128)S(1)}, f32[512,512]{1,0:T(8,128)}, u32[]{:S(2)}) copy-start(f32[512,512]{1,0:T(8,128)} %refs_5_.1) | copy-start | bytes 3145732
  0.6 6.6 %copy-start = (f32[512,512]{1,0:T(8,128)S(1)}, f32[512,512]{1,0:T(8,128)}, u32[]{:S(2)}) copy-start(f32[512,512]{1,0:T(8,128)} %refs_4_.1) | copy-start | bytes 3145732
  2.1 17.4 %collective-permute-start.1 = (bf16[2,256,512]{2,1,0:T(8,128)(2,1)S(1)}, bf16[2,256,512]{2,1,0:T(8,128)(2,1)}, u32[]{:S(2)}, u32[]{:S(2)}) collective-permute-start(bf16[2,256,512]{2,1,0:T(8,128)(2,1)S(1)} %pad_maximum_fusion.1), channel_id=1, source_target_pairs={{0,24},{8,0},{16,8},{24,16},{1,25},{9,1},{17,9},{25,17},{2,26},{10... | collective-permute-start | bytes 1572872 | tf_op jit(solution)/shard_map/ppermute | solution.py:392
  7.4 24.3 %copy-start.2 = (f32[512,512]{1,0:T(8,128)S(1)}, f32[512,512]{1,0:T(8,128)}, u32[]{:S(2)}) copy-start(f32[512,512]{1,0:T(8,128)} %refs_14_.1) | copy-start | bytes 3145732
  7.4 24.3 %copy-start.3 = (f32[512,512]{1,0:T(8,128)S(1)}, f32[512,512]{1,0:T(8,128)}, u32[]{:S(2)}) copy-start(f32[512,512]{1,0:T(8,128)} %refs_13_.1) | copy-start | bytes 3145732
  8.5 26.0 %copy-start.10 = (s32[1,4]{1,0:T(1,128)S(1)}, s32[1,4]{1,0:T(1,128)}, u32[]{:S(2)}) copy-start(s32[1,4]{1,0:T(1,128)} %refs_1_.1) | copy-start | bytes 52
  8.5 26.1 %copy-start.11 = (s32[1,4]{1,0:T(1,128)S(1)}, s32[1,4]{1,0:T(1,128)}, u32[]{:S(2)}) copy-start(s32[1,4]{1,0:T(1,128)} %refs_2_.1) | copy-start | bytes 52
  8.5 26.0 %collective-permute-start = (bf16[2,512,512]{2,1,0:T(8,128)(2,1)}, bf16[2,512,512]{2,1,0:T(8,128)(2,1)}, u32[]{:S(2)}, u32[]{:S(2)}) collective-permute-start(bf16[2,512,512]{2,1,0:T(8,128)(2,1)} %pad_maximum_fusion), channel_id=1, source_target_pairs={{0,7},{1,0},{2,1},{3,2},{4,3},{5,4},{6,5},{7,6},{8,15},{9,8},{10,9... | collective-permute-start | bytes 3145736 | tf_op jit(solution)/shard_map/ppermute | solution.py:392
  10.1 16.1 %collective-permute-start.2 = (bf16[2,160,512]{2,1,0:T(8,128)(2,1)S(1)}, bf16[2,160,512]{2,1,0:T(8,128)(2,1)S(1)}, u32[]{:S(2)}, u32[]{:S(2)}) collective-permute-start(bf16[2,160,512]{2,1,0:T(8,128)(2,1)S(1)} %fusion), channel_id=1, source_target_pairs={{0,24},{8,0},{16,8},{24,16},{1,25},{9,1},{17,9},{25,17},{2,26},{10... | collective-permute-start | bytes 983048 | tf_op jit(solution)/shard_map/ppermute | solution.py:392
  19.6 15.0 %collective-permute-start.4 = (bf16[2,256,512]{2,1,0:T(8,128)(2,1)}, bf16[2,256,512]{2,1,0:T(8,128)(2,1)}, u32[]{:S(2)}, u32[]{:S(2)}) collective-permute-start(bf16[2,256,512]{2,1,0:T(8,128)(2,1)} %collective-permute-done.1.refs_7_), channel_id=1, source_target_pairs={{0,7},{1,0},{2,1},{3,2},{4,3},{5,4},{6,5},{7,6},{8,15},{9,8},{10,9... | collective-permute-start | bytes 1572872 | tf_op jit(solution)/shard_map/ppermute | solution.py:392
  19.6 10.1 %collective-permute-start.3 = (bf16[2,96,512]{2,1,0:T(8,128)(2,1)S(1)}, bf16[2,96,512]{2,1,0:T(8,128)(2,1)}, u32[]{:S(2)}, u32[]{:S(2)}) collective-permute-start(bf16[2,96,512]{2,1,0:T(8,128)(2,1)S(1)} %fusion.3), channel_id=1, source_target_pairs={{0,24},{8,0},{16,8},{24,16},{1,25},{9,1},{17,9},{25,17},{2,26},{10... | collective-permute-start | bytes 589832 | tf_op jit(solution)/shard_map/ppermute | solution.py:392
  26.3 8.3 %collective-permute-start.5 = (bf16[2,160,512]{2,1,0:T(8,128)(2,1)S(1)}, bf16[2,160,512]{2,1,0:T(8,128)(2,1)}, u32[]{:S(2)}, u32[]{:S(2)}) collective-permute-start(bf16[2,160,512]{2,1,0:T(8,128)(2,1)S(1)} %collective-permute-done.2.refs_8_), channel_id=1, source_target_pairs={{0,7},{1,0},{2,1},{3,2},{4,3},{5,4},{6,5},{7,6},{8,15},{9,8},{10,9... | collective-permute-start | bytes 983048 | tf_op jit(solution)/shard_map/ppermute | solution.py:392
  29.7 4.9 %collective-permute-start.6 = (bf16[2,96,512]{2,1,0:T(8,128)(2,1)}, bf16[2,96,512]{2,1,0:T(8,128)(2,1)}, u32[]{:S(2)}, u32[]{:S(2)}) collective-permute-start(bf16[2,96,512]{2,1,0:T(8,128)(2,1)} %collective-permute-done.3.refs_9_), channel_id=1, source_target_pairs={{0,7},{1,0},{2,1},{3,2},{4,3},{5,4},{6,5},{7,6},{8,15},{9,8},{10,9... | collective-permute-start | bytes 589832 | tf_op jit(solution)/shard_map/ppermute | solution.py:392
  34.6 1.2 %copy-start.4 = (f32[512,512]{1,0:T(8,128)S(1)}, f32[512,512]{1,0:T(8,128)}, u32[]{:S(2)}) copy-start(f32[512,512]{1,0:T(8,128)} %refs_13_.1) | copy-start | bytes 3145732
  35.8 1.0 copy-start.6
  36.8 1.0 copy-start.7
  37.9 1.0 copy-start.8
  38.9 1.0 copy-start.9
  51.4 14.7 %collective-permute-start.16 = (f32[2,1024]{1,0:T(2,128)S(1)}, f32[2,1024]{1,0:T(2,128)S(1)}, u32[]{:S(2)}, u32[]{:S(2)}) collective-permute-start(f32[2,1024]{1,0:T(2,128)S(1)} %get-tuple-element.41), channel_id=1, source_target_pairs={{0,7},{1,0},{2,1},{3,2},{4,3},{5,4},{6,5},{7,6},{8,15},{9,8},{10,9... | collective-permute-start | bytes 24584 | tf_op jit(solution)/shard_map/ppermute | solution.py:392
  54.3 12.1 %collective-permute-start.15 = (f32[2,1024]{1,0:T(2,128)S(1)}, f32[2,1024]{1,0:T(2,128)S(1)}, u32[]{:S(2)}, u32[]{:S(2)}) collective-permute-start(f32[2,1024]{1,0:T(2,128)S(1)} %get-tuple-element.40), channel_id=1, source_target_pairs={{0,2},{1,3},{2,4},{3,5},{4,6},{5,7},{6,0},{7,1},{8,10},{9,11},{10,... | collective-permute-start | bytes 24584 | tf_op jit(solution)/shard_map/ppermute | solution.py:392
  54.3 12.5 %collective-permute-start.14 = (f32[2,1024]{1,0:T(2,128)S(1)}, f32[2,1024]{1,0:T(2,128)S(1)}, u32[]{:S(2)}, u32[]{:S(2)}) collective-permute-start(f32[2,1024]{1,0:T(2,128)S(1)} %get-tuple-element.42), channel_id=1, source_target_pairs={{0,1},{1,2},{2,3},{3,4},{4,5},{5,6},{6,7},{7,0},{8,9},{9,10},{10,1... | collective-permute-start | bytes 24584 | tf_op jit(solution)/shard_map/ppermute | solution.py:392
  57.6 9.4 %collective-permute-start.8 = (bf16[2,64,512]{2,1,0:T(8,128)(2,1)S(1)}, bf16[2,64,512]{2,1,0:T(8,128)(2,1)S(1)}, u32[]{:S(2)}, u32[]{:S(2)}) collective-permute-start(bf16[2,64,512]{2,1,0:T(8,128)(2,1)S(1)} %get-tuple-element.20), channel_id=1, source_target_pairs={{0,1},{1,2},{2,3},{3,4},{4,5},{5,6},{6,7},{7,0},{8,9},{9,10},{10,1... | collective-permute-start | bytes 393224 | tf_op jit(solution)/shard_map/ppermute | solution.py:392
  65.9 8.1 %collective-permute-start.10 = (bf16[2,192,512]{2,1,0:T(8,128)(2,1)S(1)}, bf16[2,192,512]{2,1,0:T(8,128)(2,1)S(1)}, u32[]{:S(2)}, u32[]{:S(2)}) collective-permute-start(bf16[2,192,512]{2,1,0:T(8,128)(2,1)S(1)} %get-tuple-element.22), channel_id=1, source_target_pairs={{0,1},{1,2},{2,3},{3,4},{4,5},{5,6},{6,7},{7,0},{8,9},{9,10},{10,1... | collective-permute-start | bytes 1179656 | tf_op jit(solution)/shard_map/ppermute | solution.py:392
  66.1 13.5 %collective-permute-start.12 = (bf16[2,256,512]{2,1,0:T(8,128)(2,1)S(1)}, bf16[2,256,512]{2,1,0:T(8,128)(2,1)S(1)}, u32[]{:S(2)}, u32[]{:S(2)}) collective-permute-start(bf16[2,256,512]{2,1,0:T(8,128)(2,1)S(1)} %get-tuple-element.24), channel_id=1, source_target_pairs={{0,1},{1,2},{2,3},{3,4},{4,5},{5,6},{6,7},{7,0},{8,9},{9,10},{10,1... | collective-permute-start | bytes 1572872 | tf_op jit(solution)/shard_map/ppermute | solution.py:392
  66.3 24.5 %collective-permute-start.7 = (bf16[2,512,512]{2,1,0:T(8,128)(2,1)S(1)}, bf16[2,512,512]{2,1,0:T(8,128)(2,1)S(1)}, u32[]{:S(2)}, u32[]{:S(2)}) collective-permute-start(bf16[2,512,512]{2,1,0:T(8,128)(2,1)S(1)} %get-tuple-element.18), channel_id=1, source_target_pairs={{0,1},{1,2},{2,3},{3,4},{4,5},{5,6},{6,7},{7,0},{8,9},{9,10},{10,1... | collective-permute-start | bytes 3145736 | tf_op jit(solution)/shard_map/ppermute | solution.py:392
  67.1 28.4 %collective-permute-start.9 = (bf16[2,64,512]{2,1,0:T(8,128)(2,1)S(1)}, bf16[2,64,512]{2,1,0:T(8,128)(2,1)S(1)}, u32[]{:S(2)}, u32[]{:S(2)}) collective-permute-start(bf16[2,64,512]{2,1,0:T(8,128)(2,1)S(1)} %get-tuple-element.36), channel_id=1, source_target_pairs={{0,8},{8,16},{16,24},{24,0},{1,9},{9,17},{17,25},{25,1},{2,10},{10... | collective-permute-start | bytes 393224 | tf_op jit(solution)/shard_map/ppermute | solution.py:392
  74.0 16.9 %copy-start.5 = (f32[2,512,512]{2,1,0:T(8,128)S(1)}, f32[2,512,512]{2,1,0:T(8,128)}, u32[]{:S(2)}) copy-start(f32[2,512,512]{2,1,0:T(8,128)} %get-tuple-element.17.refs_0_) | copy-start | bytes 6291460
  74.1 24.0 %collective-permute-start.11 = (bf16[2,192,512]{2,1,0:T(8,128)(2,1)S(1)}, bf16[2,192,512]{2,1,0:T(8,128)(2,1)S(1)}, u32[]{:S(2)}, u32[]{:S(2)}) collective-permute-start(bf16[2,192,512]{2,1,0:T(8,128)(2,1)S(1)} %add_convert_fusion), channel_id=1, source_target_pairs={{0,8},{8,16},{16,24},{24,0},{1,9},{9,17},{17,25},{25,1},{2,10},{10... | collective-permute-start | bytes 1179656 | tf_op jit(solution)/shard_map/ppermute | solution.py:392
  80.0 18.1 %collective-permute-start.18 = (f32[2,6,128]{2,1,0:T(8,128)S(1)}, f32[2,6,128]{2,1,0:T(8,128)S(1)}, u32[]{:S(2)}, u32[]{:S(2)}) collective-permute-start(f32[2,6,128]{2,1,0:T(8,128)S(1)} %pad_maximum_fusion.3), channel_id=1, source_target_pairs={{0,16},{8,24},{16,0},{24,8},{1,17},{9,25},{17,1},{25,9},{2,18},{10... | collective-permute-start | bytes 18440 | tf_op jit(solution)/shard_map/ppermute | solution.py:392
  83.8 14.4 %collective-permute-start.13 = (bf16[2,256,512]{2,1,0:T(8,128)(2,1)S(1)}, bf16[2,256,512]{2,1,0:T(8,128)(2,1)S(1)}, u32[]{:S(2)}, u32[]{:S(2)}) collective-permute-start(bf16[2,256,512]{2,1,0:T(8,128)(2,1)S(1)} %get-tuple-element.34), channel_id=1, source_target_pairs={{0,8},{8,16},{16,24},{24,0},{1,9},{9,17},{17,25},{25,1},{2,10},{10... | collective-permute-start | bytes 1572872 | tf_op jit(solution)/shard_map/ppermute | solution.py:392
  91.0 7.2 %collective-permute-start.19 = (f32[2,6,128]{2,1,0:T(8,128)S(1)}, f32[2,6,128]{2,1,0:T(8,128)S(1)}, u32[]{:S(2)}, u32[]{:S(2)}) collective-permute-start(f32[2,6,128]{2,1,0:T(8,128)S(1)} %pad_maximum_fusion.4), channel_id=1, source_target_pairs={{0,24},{8,0},{16,8},{24,16},{1,25},{9,1},{17,9},{25,17},{2,26},{10... | collective-permute-start | bytes 18440 | tf_op jit(solution)/shard_map/ppermute | solution.py:392
  95.5 5.6 %collective-permute-start.17 = (f32[2,14,128]{2,1,0:T(8,128)S(1)}, f32[2,14,128]{2,1,0:T(8,128)S(1)}, u32[]{:S(2)}, u32[]{:S(2)}) collective-permute-start(f32[2,14,128]{2,1,0:T(8,128)S(1)} %pad_maximum_fusion.2), channel_id=1, source_target_pairs={{0,8},{8,16},{16,24},{24,0},{1,9},{9,17},{17,25},{25,1},{2,10},{10... | collective-permute-start | bytes 43016 | tf_op jit(solution)/shard_map/ppermute | solution.py:392

commit v4 on v3

--- a/solution.py
+++ b/solution.py
@@ -76,23 +76,56 @@
     rows_in, cols_in, cols_out, rows_out, pick = take(5)
     own_out, right_out, edge_out = take(3)
     below_outs, diag_outs = take(len(out_parts)), take(len(out_parts))
-    region, sums, probe, exits, wide, half, delta, back, amp = refs
+    region, sums, probe, exits, wide, half, delta, back, amp, held, amp_held = refs[:11]
+    table_held, sems, amp_sems, table_sems = refs[11:16], refs[16], refs[17], refs[18]
     quarter, chunks = side // 4, side // LANES
     f32, bf16 = jnp.float32, jnp.bfloat16
+
+    def fetches(sources, target, at):
+        return [
+            pltpu.make_async_copy(
+                sources[p].at[:, a * LANES : (a + 1) * LANES], target.at[p, a], sems.at[at + p * chunks + a]
+            )
+            for p in range(2)
+            for a in range(chunks)
+        ]
+
+    def amp_fetch(s):
+        return pltpu.make_async_copy(amp_ref.at[0, s], amp_held.at[s], amp_sems.at[s])
+
+    own_copies = fetches((own_re, own_im), held, 0)
+    late_copies = fetches((probe_re, probe_im), probe, 2 * chunks)
+    tables = (rows_in, pick, cols_in, cols_out, rows_out)
+    late_copies += [
+        pltpu.make_async_copy(table, target, table_sems.at[k]) for k, (table, target) in enumerate(zip(tables, table_held))
+    ]
+    for copy in own_copies + late_copies:
+        copy.start()
+
+    def start_amp(s, carry):
+        amp_fetch(s).start()
+        return carry
+
+    lax.fori_loop(0, count_ref[0, 0], start_amp, 0)
+    rows_in, pick, cols_in, cols_out, rows_out = table_held
+    sums[...] = jnp.zeros_like(sums)
 
     for p in range(2):
         for a in range(chunks):
             lanes = slice(a * LANES, (a + 1) * LANES)
-            own = (own_re, own_im)[p]
-            region[p, a, :side, :] = own[:, lanes].astype(bf16).astype(f32)
             region[p, chunks + a, :side, :] = right_ref[p, :, lanes].astype(f32)
             at = side
             for rows, below_ref, diag_ref in zip(in_parts, below_refs, diag_refs):
                 region[p, a, at : at + rows, :] = below_ref[p, :, lanes].astype(f32)
                 region[p, chunks + a, at : at + rows, :] = diag_ref[p, :, lanes].astype(f32)
                 at += rows
-            probe[p, a] = (probe_re, probe_im)[p][:, lanes]
-    sums[...] = jnp.zeros_like(sums)
+    for copy in own_copies:
+        copy.wait()
+    for p in range(2):
+        for a in range(chunks):
+            region[p, a, :side, :] = held[p, a].astype(bf16).astype(f32)
+    for copy in late_copies:
+        copy.wait()
 
     lane = lax.broadcasted_iota(jnp.int32, (1, LANES), 1)
 
@@ -104,6 +137,8 @@
         inward = (LANES - b) % LANES
         keep = lane < LANES - b
         placed = lane >= b
+
+        amp_fetch(s).wait()
 
         for c in range(4):
             rows = pl.ds(oy + c, quarter, stride=4)
@@ -138,7 +173,7 @@
                     half[cc, m * step : (m + 1) * step, lanes] = o_re.astype(bf16)
                     half[cc, quarter + m * step : quarter + (m + 1) * step, lanes] = o_im.astype(bf16)
 
-        ordered = dot(amp_ref[0, s], pick[...])
+        ordered = dot(amp_held[s], pick[...])
         for a in range(chunks):
             amp[a] = ordered[:, a * LANES : (a + 1) * LANES]
 
@@ -213,11 +248,10 @@
 
     scale = scale_ref[0, 0]
     for p in range(2):
-        own = (own_re, own_im)[p]
         for a in range(chunks):
             lanes = slice(a * LANES, (a + 1) * LANES)
             right_out[p, :, lanes] = (scale * sums[p, chunks + a, :side, :]).astype(bf16)
-            own_out[p, :, lanes] = own[:, lanes] + scale * sums[p, a, :side, :]
+            own_out[p, :, lanes] = held[p, a] + scale * sums[p, a, :side, :]
             at = side
             for rows, below_out, diag_out in zip(out_parts, below_outs, diag_outs):
                 below_out[p, :, lanes] = scale * sums[p, a, at : at + rows, :]
@@ -227,7 +261,7 @@
             for r in range(2 * side // LANES):
                 cells = scale * sums[p, a, r * LANES : (r + 1) * LANES, :]
                 if k < 2 and r < chunks:
-                    cells += own[r * LANES : (r + 1) * LANES, a * LANES : (a + 1) * LANES]
+                    cells += held[p, a, r * LANES : (r + 1) * LANES, :]
                 edge_out[k, p : p + 1, r * LANES : (r + 1) * LANES] = cells.T[at : at + 1, :]
 
 
@@ -239,13 +273,15 @@
     in_parts = [part.shape[1] for part in below]
     smem = pl.BlockSpec(memory_space=pltpu.SMEM)
     vmem = pl.BlockSpec(memory_space=pltpu.VMEM)
+    here = pl.BlockSpec(memory_space=pl.ANY)
+    slots = amplitude.shape[1]
     tile = lambda rows, kind: jax.ShapeDtypeStruct((2, rows, side), kind)
     outs = [tile(side, f32), tile(side, bf16), jax.ShapeDtypeStruct((4, 2, 2 * side), f32)]
     outs += [tile(rows, f32) for rows in out_parts] + [tile(rows, bf16) for rows in out_parts]
     results = pl.pallas_call(
         functools.partial(slots_kernel, side, in_parts, out_parts),
         out_shape=outs,
-        in_specs=[smem] * 4 + [vmem] * (11 + 2 * len(in_parts)),
+        in_specs=[smem] * 4 + [here] * 2 + [vmem] * (1 + 2 * len(in_parts)) + [here] * 8,
         out_specs=[vmem] * len(outs),
         scratch_shapes=[
             pltpu.VMEM((2, 2 * chunks, 2 * side, LANES), f32),
@@ -257,8 +293,14 @@
             pltpu.VMEM((2, side, side), bf16),
             pltpu.VMEM((4, 2 * quarter, side), bf16),
             pltpu.VMEM((chunks, side, LANES), f32),
+            pltpu.VMEM((2, chunks, side, LANES), f32),
+            pltpu.VMEM((slots, side, side), bf16),
+            *[pltpu.VMEM(tables[k].shape, bf16) for k in (0, 4, 1, 2, 3)],
+            pltpu.SemaphoreType.DMA((4 * chunks,)),
+            pltpu.SemaphoreType.DMA((slots,)),
+            pltpu.SemaphoreType.DMA((5,)),
         ],
-        compiler_params=pltpu.CompilerParams(vmem_limit_bytes=40 * 2**20),
+        compiler_params=pltpu.CompilerParams(vmem_limit_bytes=44 * 2**20),
         name="slots",
     )(counts, offset_y, offset_x, scale, obj_re, obj_im, right, *below, *diag, probe_re, probe_im, amplitude, *tables)
     parts = len(out_parts)
@@ -425,11 +467,16 @@
     )
 
     diag_in = [shifted(value, "col", 1) for value in diag_sum]
-    beside_right = shifted(edges[0], "col", -1) + edges[2]
-    beside_left = shifted(edges[1], "col", 1) + shifted(edges[3], "col", 2)
+    from_beside = shifted(edges[0], "col", -1)
+    from_left, from_second = shifted(edges[1], "col", 1), shifted(edges[3], "col", 2)
+    beside_right = from_beside + edges[2]
+    beside_left = from_left + from_second
     right_in = shifted(right_sum, "col", 1)
-    lower = [mine + theirs.astype(f32) for mine, theirs in zip(below_sum, diag_in)]
-    below_in = [shifted(value.astype(bf16), "row", 1) for value in lower]
+    lower, below_in = [], []
+    for mine, theirs in zip(below_sum, diag_in):
+        lower.append(mine + theirs.astype(f32))
+        sent = lower[-1].astype(bf16)
+        below_in.append(shifted(sent, "row", 1))
 
     def with_ends(row, at):
         chunks = row.reshape(2, side // LANES, LANES)
@@ -448,7 +495,7 @@
     return run_finish(own_sum, right_in, below_in, from_up, from_far, from_down, low_first, beside_left, beside_right)
 
 
-IN_SHARES = (16, 10, 6)
+IN_SHARES = (16, 12, 4)
 OUT_SHARES = (4, 12, 16)
 
 

time: 109 us -> 108 us (level)
  waiting for transfers between devices: 31.3 us -> 38.1 us
  local copies, waits for them, and re-layouts: 7.84 us -> 2.48 us
  starting transfers between devices: 45.6 us -> 43.4 us
    ppermute x20, waiting for transfers between devices: 31.3 us -> 38.1 us  [shifted(): lax.ppermute(value, axis, [(i, (i + steps) % count) for i in range(count)])]
    unnamed x25 -> x23, local copies, waits for them, and re-layouts: 5.42 us -> 0.06 us
    ppermute x20, starting transfers between devices: 45.6 us -> 43.4 us  [shifted(): lax.ppermute(value, axis, [(i, (i + steps) % count) for i in range(count)])]
where the time goes in v4:
time: 108 us
  starting transfers between devices  43.4 us (40%)
  waiting for transfers between devices  38.1 us (35%)
  Pallas kernels  19.4 us (18%)
  other arithmetic  2.68 us (2%)
  local copies, waits for them, and re-layouts  2.48 us (2%)
  between operations  2.27 us (2%)
    ppermute x20, starting transfers between devices, shifted(): lax.ppermute(value, axis, [(i, (i + steps) % count) for i in range(count)])  43.4 us
    ppermute x20, waiting for transfers between devices, shifted(): lax.ppermute(value, axis, [(i, (i + steps) % count) for i in range(count)])  38.1 us
    pallas_call x1, Pallas kernels, run_slots(): pl.pallas_call(functools.partial(slots_kernel, side, in_parts, out_parts)...  11.9 us
    pallas_call x1, Pallas kernels, run_finish(): pl.pallas_call(functools.partial(finish_kernel, parts), out_shape=(tile,...  7.48 us
  transfers between devices with their start and end apart: 20, of which 10 were waited for; matrix products, arithmetic and copies ran while one was open for 3% of the time, Pallas kernels for 0%

profile of v4, /device:TPU:0, one launch (start us, length us, event | category | flops | bytes accessed | tf_op | source)
XLA Modules:
  0.0 108.3 jit_solution(1288825301181758532)
XLA Ops:
  0.7 1.4 %fusion.1 = (bf16[1,256,512]{2,1,0:T(8,128)(2,1)S(1)}, bf16[1,256,512]{2,1,0:T(8,128)(2,1)S(1)}) fusion(f32[512,512]{1,0:T(8,128)} %refs_4_.1, f32[512,512]{1,0:T(8,128)} %refs_5_.1), kind=kLoop, calls=%fused_computation.14 | loop fusion | bytes 1048576 | tf_op jit(solution)/shard_map/stack | solution.py:455
  2.1 5.1 %collective-permute-start.1 = (bf16[2,256,512]{2,1,0:T(8,128)(2,1)S(1)}, bf16[2,256,512]{2,1,0:T(8,128)(2,1)}, u32[]{:S(2)}, u32[]{:S(2)}) collective-permute-start(bf16[2,256,512]{2,1,0:T(8,128)(2,1)S(1)} %pad_maximum_fusion.1), channel_id=1, source_target_pairs={{0,24},{8,0},{16,8},{24,16},{1,25},{9,1},{17,9},{25,17},{2,26},{10... | collective-permute-start | bytes 1572872 | tf_op jit(solution)/shard_map/ppermute | solution.py:434
  7.4 1.1 pad_maximum_fusion
  8.5 1.7 %collective-permute-start = (bf16[2,512,512]{2,1,0:T(8,128)(2,1)}, bf16[2,512,512]{2,1,0:T(8,128)(2,1)}, u32[]{:S(2)}, u32[]{:S(2)}) collective-permute-start(bf16[2,512,512]{2,1,0:T(8,128)(2,1)} %pad_maximum_fusion), channel_id=1, source_target_pairs={{0,7},{1,0},{2,1},{3,2},{4,3},{5,4},{6,5},{7,6},{8,15},{9,8},{10,9... | collective-permute-start | bytes 3145736 | tf_op jit(solution)/shard_map/ppermute | solution.py:434
  10.2 0.6 collective-permute-start.2
  10.8 8.8 %collective-permute-done.1.refs_7_ = bf16[2,256,512]{2,1,0:T(8,128)(2,1)} collective-permute-done((bf16[2,256,512]{2,1,0:T(8,128)(2,1)S(1)}, bf16[2,256,512]{2,1,0:T(8,128)(2,1)}, u32[]{:S(2)}, u32[]{:S(2)}) %collective-permute-start.1) | collective-permute-done | bytes 524320 | tf_op jit(solution)/shard_map/ppermute | solution.py:434
  19.6 7.3 %collective-permute-done.2.refs_8_ = bf16[2,192,512]{2,1,0:T(8,128)(2,1)S(1)} collective-permute-done((bf16[2,192,512]{2,1,0:T(8,128)(2,1)S(1)}, bf16[2,192,512]{2,1,0:T(8,128)(2,1)S(1)}, u32[]{:S(2)}, u32[]{:S(2)}) %collective-permute-start.2) | collective-permute-done | bytes 393248 | tf_op jit(solution)/shard_map/ppermute | solution.py:434
  26.9 1.0 collective-permute-start.5
  27.9 4.3 %collective-permute-start.3 = (bf16[2,64,512]{2,1,0:T(8,128)(2,1)S(1)}, bf16[2,64,512]{2,1,0:T(8,128)(2,1)}, u32[]{:S(2)}, u32[]{:S(2)}) collective-permute-start(bf16[2,64,512]{2,1,0:T(8,128)(2,1)S(1)} %fusion.3), channel_id=1, source_target_pairs={{0,24},{8,0},{16,8},{24,16},{1,25},{9,1},{17,9},{25,17},{2,26},{10... | collective-permute-start | bytes 393224 | tf_op jit(solution)/shard_map/ppermute | solution.py:434
  32.9 1.9 %collective-permute-done.3.refs_9_ = bf16[2,64,512]{2,1,0:T(8,128)(2,1)} collective-permute-done((bf16[2,64,512]{2,1,0:T(8,128)(2,1)S(1)}, bf16[2,64,512]{2,1,0:T(8,128)(2,1)}, u32[]{:S(2)}, u32[]{:S(2)}) %collective-permute-start.3) | collective-permute-done | bytes 131104 | tf_op jit(solution)/shard_map/ppermute | solution.py:434
  34.8 1.6 %collective-permute-start.6 = (bf16[2,64,512]{2,1,0:T(8,128)(2,1)}, bf16[2,64,512]{2,1,0:T(8,128)(2,1)}, u32[]{:S(2)}, u32[]{:S(2)}) collective-permute-start(bf16[2,64,512]{2,1,0:T(8,128)(2,1)} %collective-permute-done.3.refs_9_), channel_id=1, source_target_pairs={{0,7},{1,0},{2,1},{3,2},{4,3},{5,4},{6,5},{7,6},{8,15},{9,8},{10,9... | collective-permute-start | bytes 393224 | tf_op jit(solution)/shard_map/ppermute | solution.py:434
  36.4 0.9 add_reduce_fusion
  38.0 1.2 %collective-permute-done.6.refs_12_ = bf16[2,64,512]{2,1,0:T(8,128)(2,1)} collective-permute-done((bf16[2,64,512]{2,1,0:T(8,128)(2,1)}, bf16[2,64,512]{2,1,0:T(8,128)(2,1)}, u32[]{:S(2)}, u32[]{:S(2)}) %collective-permute-start.6) | collective-permute-done | bytes 131104 | tf_op jit(solution)/shard_map/ppermute | solution.py:434
  39.3 11.9 %slots.1 = (f32[2,512,512]{2,1,0:T(8,128)}, bf16[2,512,512]{2,1,0:T(8,128)(2,1)S(1)}, f32[4,2,1024]{2,1,0:T(2,128)S(1)}, f32[2,64,512]{2,1,0:T(8,128)S(1)}, f32[...) custom-call(s32[1,1]{1,0:T(1,128)S(6)} %copy.18.refs_0_, ...), custom_call_target="tpu_custom_call" | custom-call | tf_op jit(solution)/shard_map/slots/pallas_call | solution.py:281
  51.2 2.9 %collective-permute-start.16 = (f32[2,1024]{1,0:T(2,128)S(1)}, f32[2,1024]{1,0:T(2,128)S(1)}, u32[]{:S(2)}, u32[]{:S(2)}) collective-permute-start(f32[2,1024]{1,0:T(2,128)S(1)} %get-tuple-element.41), channel_id=1, source_target_pairs={{0,7},{1,0},{2,1},{3,2},{4,3},{5,4},{6,5},{7,6},{8,15},{9,8},{10,9... | collective-permute-start | bytes 24584 | tf_op jit(solution)/shard_map/ppermute | solution.py:434
  54.0 3.3 %collective-permute-start.14 = (f32[2,1024]{1,0:T(2,128)S(1)}, f32[2,1024]{1,0:T(2,128)S(1)}, u32[]{:S(2)}, u32[]{:S(2)}) collective-permute-start(f32[2,1024]{1,0:T(2,128)S(1)} %get-tuple-element.42), channel_id=1, source_target_pairs={{0,1},{1,2},{2,3},{3,4},{4,5},{5,6},{6,7},{7,0},{8,9},{9,10},{10,1... | collective-permute-start | bytes 24584 | tf_op jit(solution)/shard_map/ppermute | solution.py:434
  57.3 8.3 %collective-permute-start.8 = (bf16[2,64,512]{2,1,0:T(8,128)(2,1)S(1)}, bf16[2,64,512]{2,1,0:T(8,128)(2,1)S(1)}, u32[]{:S(2)}, u32[]{:S(2)}) collective-permute-start(bf16[2,64,512]{2,1,0:T(8,128)(2,1)S(1)} %get-tuple-element.20), channel_id=1, source_target_pairs={{0,1},{1,2},{2,3},{3,4},{4,5},{5,6},{6,7},{7,0},{8,9},{9,10},{10,1... | collective-permute-start | bytes 393224 | tf_op jit(solution)/shard_map/ppermute | solution.py:434
  65.8 0.2 slice_reduce_fusion
  66.0 0.4 collective-permute-start.7
  66.5 0.2 slice_reduce_fusion.1
  66.8 3.8 %collective-permute-start.9 = (bf16[2,64,512]{2,1,0:T(8,128)(2,1)S(1)}, bf16[2,64,512]{2,1,0:T(8,128)(2,1)S(1)}, u32[]{:S(2)}, u32[]{:S(2)}) collective-permute-start(bf16[2,64,512]{2,1,0:T(8,128)(2,1)S(1)} %get-tuple-element.36), channel_id=1, source_target_pairs={{0,8},{8,16},{16,24},{24,0},{1,9},{9,17},{17,25},{25,1},{2,10},{10... | collective-permute-start | bytes 393224 | tf_op jit(solution)/shard_map/ppermute | solution.py:434
  70.6 3.1 %collective-permute-done.10 = bf16[2,192,512]{2,1,0:T(8,128)(2,1)S(1)} collective-permute-done((bf16[2,192,512]{2,1,0:T(8,128)(2,1)S(1)}, bf16[2,192,512]{2,1,0:T(8,128)(2,1)S(1)}, u32[]{:S(2)}, u32[]{:S(2)}) %collective-permute-start.10) | collective-permute-done | bytes 393248 | tf_op jit(solution)/shard_map/ppermute | solution.py:434
  73.9 1.0 collective-permute-start.11
  74.9 4.4 %collective-permute-done.12 = bf16[2,256,512]{2,1,0:T(8,128)(2,1)S(1)} collective-permute-done((bf16[2,256,512]{2,1,0:T(8,128)(2,1)S(1)}, bf16[2,256,512]{2,1,0:T(8,128)(2,1)S(1)}, u32[]{:S(2)}, u32[]{:S(2)}) %collective-permute-start.12) | collective-permute-done | bytes 524320 | tf_op jit(solution)/shard_map/ppermute | solution.py:434
  79.3 0.2 fusion.6
  79.7 4.0 %collective-permute-start.18 = (f32[2,6,128]{2,1,0:T(8,128)S(1)}, f32[2,6,128]{2,1,0:T(8,128)S(1)}, u32[]{:S(2)}, u32[]{:S(2)}) collective-permute-start(f32[2,6,128]{2,1,0:T(8,128)S(1)} %pad_maximum_fusion.3), channel_id=1, source_target_pairs={{0,16},{8,24},{16,0},{24,8},{1,17},{9,25},{17,1},{25,9},{2,18},{10... | collective-permute-start | bytes 18440 | tf_op jit(solution)/shard_map/ppermute | solution.py:434
  83.8 0.8 collective-permute-start.13
  84.6 6.0 %collective-permute-done.7.refs_1_ = bf16[2,512,512]{2,1,0:T(8,128)(2,1)S(1)} collective-permute-done((bf16[2,512,512]{2,1,0:T(8,128)(2,1)S(1)}, bf16[2,512,512]{2,1,0:T(8,128)(2,1)S(1)}, u32[]{:S(2)}, u32[]{:S(2)}) %collective-permute-start.7) | collective-permute-done | bytes 1048608 | tf_op jit(solution)/shard_map/ppermute | solution.py:434
  90.8 4.3 %collective-permute-start.19 = (f32[2,6,128]{2,1,0:T(8,128)S(1)}, f32[2,6,128]{2,1,0:T(8,128)S(1)}, u32[]{:S(2)}, u32[]{:S(2)}) collective-permute-start(f32[2,6,128]{2,1,0:T(8,128)S(1)} %pad_maximum_fusion.4), channel_id=1, source_target_pairs={{0,24},{8,0},{16,8},{24,16},{1,25},{9,1},{17,9},{25,17},{2,26},{10... | collective-permute-start | bytes 18440 | tf_op jit(solution)/shard_map/ppermute | solution.py:434
  95.4 2.4 %collective-permute-done.18.refs_6_ = f32[2,6,128]{2,1,0:T(8,128)S(1)} collective-permute-done((f32[2,6,128]{2,1,0:T(8,128)S(1)}, f32[2,6,128]{2,1,0:T(8,128)S(1)}, u32[]{:S(2)}, u32[]{:S(2)}) %collective-permute-start.18) | collective-permute-done | bytes 6176 | tf_op jit(solution)/shard_map/ppermute | solution.py:434
  97.9 2.9 %collective-permute-done.17.refs_5_ = f32[2,14,128]{2,1,0:T(8,128)S(1)} collective-permute-done((f32[2,14,128]{2,1,0:T(8,128)S(1)}, f32[2,14,128]{2,1,0:T(8,128)S(1)}, u32[]{:S(2)}, u32[]{:S(2)}) %collective-permute-start.17) | collective-permute-done | bytes 14368 | tf_op jit(solution)/shard_map/ppermute | solution.py:434
  100.8 7.5 %finish.1 = (f32[512,512]{1,0:T(8,128)}, f32[512,512]{1,0:T(8,128)}) custom-call(f32[2,512,512]{2,1,0:T(8,128)S(1)} %copy-done.1, bf16[2,512,512]{2,1,0:T(8,128)(2,1)S(1)} %collective-permute-done.7.refs_1_, bf16[2,64,512]{2,1,0:T(8,128)(2,1)S(1)} %collective-permute-done.9.refs_2_, bf16[2,192,512]{2,1,0:T(8,128)(2,1)S(1)} %collective-permute-done.11.refs_3_, ...), custom_call_target="tpu_custom_call" | custom-call | tf_op jit(solution)/shard_map/finish/pallas_call | solution.py:416
  (67 shorter events, 1.5 us)
Async XLA Ops:
  0.6 6.7 %copy-start.8 = (f32[512,512]{1,0:T(8,128)S(1)}, f32[512,512]{1,0:T(8,128)}, u32[]{:S(2)}) copy-start(f32[512,512]{1,0:T(8,128)} %refs_5_.1) | copy-start | bytes 3145732
  0.6 6.6 %copy-start = (f32[512,512]{1,0:T(8,128)S(1)}, f32[512,512]{1,0:T(8,128)}, u32[]{:S(2)}) copy-start(f32[512,512]{1,0:T(8,128)} %refs_4_.1) | copy-start | bytes 3145732
  2.1 17.4 %collective-permute-start.1 = (bf16[2,256,512]{2,1,0:T(8,128)(2,1)S(1)}, bf16[2,256,512]{2,1,0:T(8,128)(2,1)}, u32[]{:S(2)}, u32[]{:S(2)}) collective-permute-start(bf16[2,256,512]{2,1,0:T(8,128)(2,1)S(1)} %pad_maximum_fusion.1), channel_id=1, source_target_pairs={{0,24},{8,0},{16,8},{24,16},{1,25},{9,1},{17,9},{25,17},{2,26},{10... | collective-permute-start | bytes 1572872 | tf_op jit(solution)/shard_map/ppermute | solution.py:434
  7.4 28.9 %copy-start.9 = (f32[512,512]{1,0:T(8,128)S(1)}, f32[512,512]{1,0:T(8,128)}, u32[]{:S(2)}) copy-start(f32[512,512]{1,0:T(8,128)} %refs_14_.1) | copy-start | bytes 3145732
  7.4 28.9 %copy-start.10 = (f32[512,512]{1,0:T(8,128)S(1)}, f32[512,512]{1,0:T(8,128)}, u32[]{:S(2)}) copy-start(f32[512,512]{1,0:T(8,128)} %refs_13_.1) | copy-start | bytes 3145732
  8.5 30.7 %copy-start.2 = (bf16[512,512]{1,0:T(8,128)(2,1)S(1)}, bf16[512,512]{1,0:T(8,128)(2,1)}, u32[]{:S(2)}) copy-start(bf16[512,512]{1,0:T(8,128)(2,1)} %constant.23.clone.refs_20_) | copy-start | bytes 1572868
  8.5 30.7 %copy-start.3 = (bf16[4,256,256]{2,1,0:T(8,128)(2,1)S(1)}, bf16[4,256,256]{2,1,0:T(8,128)(2,1)}, u32[]{:S(2)}) copy-start(bf16[4,256,256]{2,1,0:T(8,128)(2,1)} %constant.22.clone.refs_19_) | copy-start | bytes 1572868
  8.5 30.7 %copy-start.4 = (bf16[512,512]{1,0:T(8,128)(2,1)S(1)}, bf16[512,512]{1,0:T(8,128)(2,1)}, u32[]{:S(2)}) copy-start(bf16[512,512]{1,0:T(8,128)(2,1)} %constant.20.clone.refs_17_) | copy-start | bytes 1572868
  8.5 30.7 %copy-start.5 = (bf16[4,256,256]{2,1,0:T(8,128)(2,1)S(1)}, bf16[4,256,256]{2,1,0:T(8,128)(2,1)}, u32[]{:S(2)}) copy-start(bf16[4,256,256]{2,1,0:T(8,128)(2,1)} %constant.19.clone.refs_16_) | copy-start | bytes 1572868
  8.5 30.7 %copy-start.6 = (s32[1,4]{1,0:T(1,128)S(1)}, s32[1,4]{1,0:T(1,128)}, u32[]{:S(2)}) copy-start(s32[1,4]{1,0:T(1,128)} %refs_1_.1) | copy-start | bytes 52
  8.5 30.7 %copy-start.7 = (s32[1,4]{1,0:T(1,128)S(1)}, s32[1,4]{1,0:T(1,128)}, u32[]{:S(2)}) copy-start(s32[1,4]{1,0:T(1,128)} %refs_2_.1) | copy-start | bytes 52
  8.5 30.7 %collective-permute-start = (bf16[2,512,512]{2,1,0:T(8,128)(2,1)}, bf16[2,512,512]{2,1,0:T(8,128)(2,1)}, u32[]{:S(2)}, u32[]{:S(2)}) collective-permute-start(bf16[2,512,512]{2,1,0:T(8,128)(2,1)} %pad_maximum_fusion), channel_id=1, source_target_pairs={{0,7},{1,0},{2,1},{3,2},{4,3},{5,4},{6,5},{7,6},{8,15},{9,8},{10,9... | collective-permute-start | bytes 3145736 | tf_op jit(solution)/shard_map/ppermute | solution.py:434
  10.2 16.6 %collective-permute-start.2 = (bf16[2,192,512]{2,1,0:T(8,128)(2,1)S(1)}, bf16[2,192,512]{2,1,0:T(8,128)(2,1)S(1)}, u32[]{:S(2)}, u32[]{:S(2)}) collective-permute-start(bf16[2,192,512]{2,1,0:T(8,128)(2,1)S(1)} %fusion), channel_id=1, source_target_pairs={{0,24},{8,0},{16,8},{24,16},{1,25},{9,1},{17,9},{25,17},{2,26},{10... | collective-permute-start | bytes 1179656 | tf_op jit(solution)/shard_map/ppermute | solution.py:434
  19.6 19.6 %collective-permute-start.4 = (bf16[2,256,512]{2,1,0:T(8,128)(2,1)}, bf16[2,256,512]{2,1,0:T(8,128)(2,1)}, u32[]{:S(2)}, u32[]{:S(2)}) collective-permute-start(bf16[2,256,512]{2,1,0:T(8,128)(2,1)} %collective-permute-done.1.refs_7_), channel_id=1, source_target_pairs={{0,7},{1,0},{2,1},{3,2},{4,3},{5,4},{6,5},{7,6},{8,15},{9,8},{10,9... | collective-permute-start | bytes 1572872 | tf_op jit(solution)/shard_map/ppermute | solution.py:434
  26.9 12.3 %collective-permute-start.5 = (bf16[2,192,512]{2,1,0:T(8,128)(2,1)S(1)}, bf16[2,192,512]{2,1,0:T(8,128)(2,1)}, u32[]{:S(2)}, u32[]{:S(2)}) collective-permute-start(bf16[2,192,512]{2,1,0:T(8,128)(2,1)S(1)} %collective-permute-done.2.refs_8_), channel_id=1, source_target_pairs={{0,7},{1,0},{2,1},{3,2},{4,3},{5,4},{6,5},{7,6},{8,15},{9,8},{10,9... | collective-permute-start | bytes 1179656 | tf_op jit(solution)/shard_map/ppermute | solution.py:434
  27.9 6.9 %collective-permute-start.3 = (bf16[2,64,512]{2,1,0:T(8,128)(2,1)S(1)}, bf16[2,64,512]{2,1,0:T(8,128)(2,1)}, u32[]{:S(2)}, u32[]{:S(2)}) collective-permute-start(bf16[2,64,512]{2,1,0:T(8,128)(2,1)S(1)} %fusion.3), channel_id=1, source_target_pairs={{0,24},{8,0},{16,8},{24,16},{1,25},{9,1},{17,9},{25,17},{2,26},{10... | collective-permute-start | bytes 393224 | tf_op jit(solution)/shard_map/ppermute | solution.py:434
  34.8 4.4 %collective-permute-start.6 = (bf16[2,64,512]{2,1,0:T(8,128)(2,1)}, bf16[2,64,512]{2,1,0:T(8,128)(2,1)}, u32[]{:S(2)}, u32[]{:S(2)}) collective-permute-start(bf16[2,64,512]{2,1,0:T(8,128)(2,1)} %collective-permute-done.3.refs_9_), channel_id=1, source_target_pairs={{0,7},{1,0},{2,1},{3,2},{4,3},{5,4},{6,5},{7,6},{8,15},{9,8},{10,9... | collective-permute-start | bytes 393224 | tf_op jit(solution)/shard_map/ppermute | solution.py:434
  51.2 14.6 %collective-permute-start.16 = (f32[2,1024]{1,0:T(2,128)S(1)}, f32[2,1024]{1,0:T(2,128)S(1)}, u32[]{:S(2)}, u32[]{:S(2)}) collective-permute-start(f32[2,1024]{1,0:T(2,128)S(1)} %get-tuple-element.41), channel_id=1, source_target_pairs={{0,7},{1,0},{2,1},{3,2},{4,3},{5,4},{6,5},{7,6},{8,15},{9,8},{10,9... | collective-permute-start | bytes 24584 | tf_op jit(solution)/shard_map/ppermute | solution.py:434
  54.0 12.0 %collective-permute-start.15 = (f32[2,1024]{1,0:T(2,128)S(1)}, f32[2,1024]{1,0:T(2,128)S(1)}, u32[]{:S(2)}, u32[]{:S(2)}) collective-permute-start(f32[2,1024]{1,0:T(2,128)S(1)} %get-tuple-element.40), channel_id=1, source_target_pairs={{0,2},{1,3},{2,4},{3,5},{4,6},{5,7},{6,0},{7,1},{8,10},{9,11},{10,... | collective-permute-start | bytes 24584 | tf_op jit(solution)/shard_map/ppermute | solution.py:434
  54.0 12.4 %collective-permute-start.14 = (f32[2,1024]{1,0:T(2,128)S(1)}, f32[2,1024]{1,0:T(2,128)S(1)}, u32[]{:S(2)}, u32[]{:S(2)}) collective-permute-start(f32[2,1024]{1,0:T(2,128)S(1)} %get-tuple-element.42), channel_id=1, source_target_pairs={{0,1},{1,2},{2,3},{3,4},{4,5},{5,6},{6,7},{7,0},{8,9},{9,10},{10,1... | collective-permute-start | bytes 24584 | tf_op jit(solution)/shard_map/ppermute | solution.py:434
  57.3 9.4 %collective-permute-start.8 = (bf16[2,64,512]{2,1,0:T(8,128)(2,1)S(1)}, bf16[2,64,512]{2,1,0:T(8,128)(2,1)S(1)}, u32[]{:S(2)}, u32[]{:S(2)}) collective-permute-start(bf16[2,64,512]{2,1,0:T(8,128)(2,1)S(1)} %get-tuple-element.20), channel_id=1, source_target_pairs={{0,1},{1,2},{2,3},{3,4},{4,5},{5,6},{6,7},{7,0},{8,9},{9,10},{10,1... | collective-permute-start | bytes 393224 | tf_op jit(solution)/shard_map/ppermute | solution.py:434
  65.6 8.1 %collective-permute-start.10 = (bf16[2,192,512]{2,1,0:T(8,128)(2,1)S(1)}, bf16[2,192,512]{2,1,0:T(8,128)(2,1)S(1)}, u32[]{:S(2)}, u32[]{:S(2)}) collective-permute-start(bf16[2,192,512]{2,1,0:T(8,128)(2,1)S(1)} %get-tuple-element.22), channel_id=1, source_target_pairs={{0,1},{1,2},{2,3},{3,4},{4,5},{5,6},{6,7},{7,0},{8,9},{9,10},{10,1... | collective-permute-start | bytes 1179656 | tf_op jit(solution)/shard_map/ppermute | solution.py:434
  65.8 13.6 %collective-permute-start.12 = (bf16[2,256,512]{2,1,0:T(8,128)(2,1)S(1)}, bf16[2,256,512]{2,1,0:T(8,128)(2,1)S(1)}, u32[]{:S(2)}, u32[]{:S(2)}) collective-permute-start(bf16[2,256,512]{2,1,0:T(8,128)(2,1)S(1)} %get-tuple-element.24), channel_id=1, source_target_pairs={{0,1},{1,2},{2,3},{3,4},{4,5},{5,6},{6,7},{7,0},{8,9},{9,10},{10,1... | collective-permute-start | bytes 1572872 | tf_op jit(solution)/shard_map/ppermute | solution.py:434
  66.0 24.5 %collective-permute-start.7 = (bf16[2,512,512]{2,1,0:T(8,128)(2,1)S(1)}, bf16[2,512,512]{2,1,0:T(8,128)(2,1)S(1)}, u32[]{:S(2)}, u32[]{:S(2)}) collective-permute-start(bf16[2,512,512]{2,1,0:T(8,128)(2,1)S(1)} %get-tuple-element.18), channel_id=1, source_target_pairs={{0,1},{1,2},{2,3},{3,4},{4,5},{5,6},{6,7},{7,0},{8,9},{9,10},{10,1... | collective-permute-start | bytes 3145736 | tf_op jit(solution)/shard_map/ppermute | solution.py:434
  66.8 28.4 %collective-permute-start.9 = (bf16[2,64,512]{2,1,0:T(8,128)(2,1)S(1)}, bf16[2,64,512]{2,1,0:T(8,128)(2,1)S(1)}, u32[]{:S(2)}, u32[]{:S(2)}) collective-permute-start(bf16[2,64,512]{2,1,0:T(8,128)(2,1)S(1)} %get-tuple-element.36), channel_id=1, source_target_pairs={{0,8},{8,16},{16,24},{24,0},{1,9},{9,17},{17,25},{25,1},{2,10},{10... | collective-permute-start | bytes 393224 | tf_op jit(solution)/shard_map/ppermute | solution.py:434
  73.7 16.9 %copy-start.1 = (f32[2,512,512]{2,1,0:T(8,128)S(1)}, f32[2,512,512]{2,1,0:T(8,128)}, u32[]{:S(2)}) copy-start(f32[2,512,512]{2,1,0:T(8,128)} %get-tuple-element.17.refs_0_) | copy-start | bytes 6291460
  73.9 24.0 %collective-permute-start.11 = (bf16[2,192,512]{2,1,0:T(8,128)(2,1)S(1)}, bf16[2,192,512]{2,1,0:T(8,128)(2,1)S(1)}, u32[]{:S(2)}, u32[]{:S(2)}) collective-permute-start(bf16[2,192,512]{2,1,0:T(8,128)(2,1)S(1)} %add_convert_fusion), channel_id=1, source_target_pairs={{0,8},{8,16},{16,24},{24,0},{1,9},{9,17},{17,25},{25,1},{2,10},{10... | collective-permute-start | bytes 1179656 | tf_op jit(solution)/shard_map/ppermute | solution.py:434
  79.7 18.1 %collective-permute-start.18 = (f32[2,6,128]{2,1,0:T(8,128)S(1)}, f32[2,6,128]{2,1,0:T(8,128)S(1)}, u32[]{:S(2)}, u32[]{:S(2)}) collective-permute-start(f32[2,6,128]{2,1,0:T(8,128)S(1)} %pad_maximum_fusion.3), channel_id=1, source_target_pairs={{0,16},{8,24},{16,0},{24,8},{1,17},{9,25},{17,1},{25,9},{2,18},{10... | collective-permute-start | bytes 18440 | tf_op jit(solution)/shard_map/ppermute | solution.py:434
  83.8 14.1 %collective-permute-start.13 = (bf16[2,256,512]{2,1,0:T(8,128)(2,1)S(1)}, bf16[2,256,512]{2,1,0:T(8,128)(2,1)S(1)}, u32[]{:S(2)}, u32[]{:S(2)}) collective-permute-start(bf16[2,256,512]{2,1,0:T(8,128)(2,1)S(1)} %get-tuple-element.34), channel_id=1, source_target_pairs={{0,8},{8,16},{16,24},{24,0},{1,9},{9,17},{17,25},{25,1},{2,10},{10... | collective-permute-start | bytes 1572872 | tf_op jit(solution)/shard_map/ppermute | solution.py:434
  90.8 7.2 %collective-permute-start.19 = (f32[2,6,128]{2,1,0:T(8,128)S(1)}, f32[2,6,128]{2,1,0:T(8,128)S(1)}, u32[]{:S(2)}, u32[]{:S(2)}) collective-permute-start(f32[2,6,128]{2,1,0:T(8,128)S(1)} %pad_maximum_fusion.4), channel_id=1, source_target_pairs={{0,24},{8,0},{16,8},{24,16},{1,25},{9,1},{17,9},{25,17},{2,26},{10... | collective-permute-start | bytes 18440 | tf_op jit(solution)/shard_map/ppermute | solution.py:434
  95.2 5.6 %collective-permute-start.17 = (f32[2,14,128]{2,1,0:T(8,128)S(1)}, f32[2,14,128]{2,1,0:T(8,128)S(1)}, u32[]{:S(2)}, u32[]{:S(2)}) collective-permute-start(f32[2,14,128]{2,1,0:T(8,128)S(1)} %pad_maximum_fusion.2), channel_id=1, source_target_pairs={{0,8},{8,16},{16,24},{24,0},{1,9},{9,17},{17,25},{25,1},{2,10},{10... | collective-permute-start | bytes 43016 | tf_op jit(solution)/shard_map/ppermute | solution.py:434

commit v5 on v4

--- a/solution.py
+++ b/solution.py
@@ -15,6 +15,7 @@
 step_size = 0.5
 epsilon = 1e-05
 LANES = 128
+UNROLL = 4
 
 
 def transform_tables(side):
@@ -74,7 +75,7 @@
     below_refs, diag_refs = take(len(in_parts)), take(len(in_parts))
     probe_re, probe_im, amp_ref = take(3)
     rows_in, cols_in, cols_out, rows_out, pick = take(5)
-    own_out, right_out, edge_out = take(3)
+    own_out, right_out, left_out, beside_out, kept_out, second_out = take(6)
     below_outs, diag_outs = take(len(out_parts)), take(len(out_parts))
     region, sums, probe, exits, wide, half, delta, back, amp, held, amp_held = refs[:11]
     table_held, sems, amp_sems, table_sems = refs[11:16], refs[16], refs[17], refs[18]
@@ -257,12 +258,28 @@
                 below_out[p, :, lanes] = scale * sums[p, a, at : at + rows, :]
                 diag_out[p, :, lanes] = (scale * sums[p, chunks + a, at : at + rows, :]).astype(bf16)
                 at += rows
-        for k, (a, at) in enumerate(((0, 0), (chunks - 1, LANES - 1), (chunks, 0), (2 * chunks - 1, LANES - 1))):
-            for r in range(2 * side // LANES):
-                cells = scale * sums[p, a, r * LANES : (r + 1) * LANES, :]
-                if k < 2 and r < chunks:
-                    cells += held[p, a, r * LANES : (r + 1) * LANES, :]
-                edge_out[k, p : p + 1, r * LANES : (r + 1) * LANES] = cells.T[at : at + 1, :]
+        here = slice(p, p + 1)
+        columns = (
+            (left_out, 0, 0, True),
+            (beside_out, chunks - 1, LANES - 1, True),
+            (kept_out, chunks, 0, False),
+            (second_out, 2 * chunks - 1, LANES - 1, False),
+        )
+        for target, a, at, with_own in columns:
+            cells = scale * sums[p, a]
+            turned = jnp.concatenate([cells[r * LANES : (r + 1) * LANES, :].T[at : at + 1, :] for r in range(2 * chunks)], axis=1)
+            if with_own:
+                own_turned = [held[p, a, r * LANES : (r + 1) * LANES, :].T[at : at + 1, :] for r in range(chunks)]
+                turned += jnp.concatenate(own_turned + [jnp.zeros((1, side), f32)], axis=1)
+            target[here, : 2 * side] = turned
+        for k, row in enumerate((0, side - 1, side, 2 * side - 1)):
+            for a in range(chunks):
+                at = 2 * side + k * side + a * LANES
+                mine = scale * sums[p, a, row : row + 1, :]
+                if k < 2:
+                    mine += held[p, a, row : row + 1, :]
+                kept_out[here, at : at + LANES] = mine
+                beside_out[here, at : at + LANES] = scale * sums[p, chunks + a, row : row + 1, :]
 
 
 def run_slots(counts, offset_y, offset_x, scale, obj_re, obj_im, right, below, diag, probe_re, probe_im, amplitude, out_parts):
@@ -276,7 +293,7 @@
     here = pl.BlockSpec(memory_space=pl.ANY)
     slots = amplitude.shape[1]
     tile = lambda rows, kind: jax.ShapeDtypeStruct((2, rows, side), kind)
-    outs = [tile(side, f32), tile(side, bf16), jax.ShapeDtypeStruct((4, 2, 2 * side), f32)]
+    outs = [tile(side, f32), tile(side, bf16)] + [jax.ShapeDtypeStruct((2, n * side), f32) for n in (2, 6, 6, 2)]
     outs += [tile(rows, f32) for rows in out_parts] + [tile(rows, bf16) for rows in out_parts]
     results = pl.pallas_call(
         functools.partial(slots_kernel, side, in_parts, out_parts),
@@ -304,7 +321,7 @@
         name="slots",
     )(counts, offset_y, offset_x, scale, obj_re, obj_im, right, *below, *diag, probe_re, probe_im, amplitude, *tables)
     parts = len(out_parts)
-    return results[0], results[1], results[2], results[3 : 3 + parts], results[3 + parts :]
+    return results[0], results[1], results[2:6], results[6 : 6 + parts], results[6 + parts :]
 
 
 def finish_kernel(parts, *refs):
@@ -403,7 +420,7 @@
                 (out_re, out_im)[p][mine, a * LANES : (a + 1) * LANES] = result[p, a, mine, :]
         return carry
 
-    lax.fori_loop(0, side // (2 * count), block, 0)
+    lax.fori_loop(0, side // (2 * count), block, 0, unroll=UNROLL)
 
 
 def run_finish(own, right, below, *edges):
@@ -429,6 +446,44 @@
     )(own, right, *below, *edges)
 
 
+def ring_kernel(right_ref, left_ref, second_ref, kept_ref, far_out, down_out, up_out, low_out, beside_left, beside_right):
+    side = right_ref.shape[1] // 2
+    chunks = side // LANES
+    both = slice(0, 2 * side)
+    beside_left[...] = left_ref[:, both] + second_ref[...]
+    beside_right[...] = right_ref[...] + kept_ref[:, both]
+    for k, (target, at) in enumerate(((up_out, 0), (down_out, side - 1), (low_out, side), (far_out, 2 * side - 1))):
+        for p in range(2):
+            here = slice(p, p + 1)
+            for row, column in ((0, beside_left), (chunks + 1, beside_right)):
+                target[p, row : row + 1, :] = jnp.broadcast_to(column[here, at : at + 1], (1, LANES))
+            for a in range(chunks):
+                lanes = slice(2 * side + k * side + a * LANES, 2 * side + k * side + (a + 1) * LANES)
+                target[p, a + 1 : a + 2, :] = kept_ref[here, lanes] + left_ref[here, lanes]
+    for p in range(2):
+        for k, column in enumerate((beside_left, beside_right)):
+            for a in range(chunks):
+                row = chunks + 2 + k * chunks + a
+                lanes = slice(side + a * LANES, side + (a + 1) * LANES)
+                down_out[p, row : row + 1, :] = column[p : p + 1, lanes]
+
+
+def run_ring(right, left, second, kept):
+    wide = right.shape[1]
+    chunks = wide // 2 // LANES
+    vmem = pl.BlockSpec(memory_space=pltpu.VMEM)
+    rows = [chunks + 2, 3 * chunks + 2, chunks + 2, chunks + 2]
+    shapes = [(2, n, LANES) for n in rows] + [(2, wide)] * 2
+    return pl.pallas_call(
+        ring_kernel,
+        out_shape=[jax.ShapeDtypeStruct(shape, jnp.float32) for shape in shapes],
+        in_specs=[vmem] * 4,
+        out_specs=[vmem] * 6,
+        compiler_params=pltpu.CompilerParams(vmem_limit_bytes=2 * 2**20),
+        name="ring",
+    )(right, left, second, kept)
+
+
 def shifted(value, axis, steps):
     count = lax.axis_size(axis)
     return lax.ppermute(value, axis, [(i, (i + steps) % count) for i in range(count)])
@@ -466,36 +521,22 @@
         counts, offset_y, offset_x, scale, obj_re, obj_im, right, below, diag, probe_re, probe_im, amplitude, out_parts
     )
 
+    to_left, to_right, kept, to_second = edges
     diag_in = [shifted(value, "col", 1) for value in diag_sum]
-    from_beside = shifted(edges[0], "col", -1)
-    from_left, from_second = shifted(edges[1], "col", 1), shifted(edges[3], "col", 2)
-    beside_right = from_beside + edges[2]
-    beside_left = from_left + from_second
+    ring_parts = (shifted(to_left, "col", -1), shifted(to_right, "col", 1), shifted(to_second, "col", 2))
     right_in = shifted(right_sum, "col", 1)
-    lower, below_in = [], []
+    below_in = []
     for mine, theirs in zip(below_sum, diag_in):
-        lower.append(mine + theirs.astype(f32))
-        sent = lower[-1].astype(bf16)
+        sent = (mine + theirs.astype(f32)).astype(bf16)
         below_in.append(shifted(sent, "row", 1))
-
-    def with_ends(row, at):
-        chunks = row.reshape(2, side // LANES, LANES)
-        ends = [jnp.broadcast_to(column[:, at, None, None], (2, 1, LANES)) for column in (beside_left, beside_right)]
-        return jnp.concatenate([ends[0], chunks, ends[1]], axis=1)
-
-    low_first = with_ends(lower[0][:, 0], side)
-    low_last = with_ends(lower[-1][:, -1], 2 * side - 1)
+    low_last, sent_down, first, low_first, beside_left, beside_right = run_ring(*ring_parts, kept)
     from_far = shifted(low_last, "row", 2)
-    first = with_ends(own_sum[:, 0] + right_in[:, 0].astype(f32), 0)
-    last = with_ends(own_sum[:, -1] + right_in[:, -1].astype(f32), side - 1)
-    sides = jnp.concatenate([beside_left[:, side:], beside_right[:, side:]], axis=1)
-    sent_down = jnp.concatenate([last, sides.reshape(2, -1, LANES)], axis=1)
     from_up = shifted(sent_down, "row", 1)
     from_down = shifted(first, "row", -1)
     return run_finish(own_sum, right_in, below_in, from_up, from_far, from_down, low_first, beside_left, beside_right)
 
 
-IN_SHARES = (16, 12, 4)
+IN_SHARES = (16, 8, 5, 3)
 OUT_SHARES = (4, 12, 16)
 
 

time: 108 us -> 119 us (1.10)
  starting transfers between devices: 43.4 us -> 63.5 us
  waiting for transfers between devices: 38.1 us -> 31.4 us
  Pallas kernels: 19.4 us -> 18 us
    ppermute x20 -> x22, starting transfers between devices: 43.4 us -> 63.5 us  [shifted(): lax.ppermute(value, axis, [(i, (i + steps) % count) for i in range(count)])]
    ppermute x20 -> x22, waiting for transfers between devices: 38.1 us -> 31.4 us  [shifted(): lax.ppermute(value, axis, [(i, (i + steps) % count) for i in range(count)])]
    pallas_call x1, Pallas kernels: 7.48 us -> 5.72 us  [run_finish(): pl.pallas_call(functools.partial(finish_kernel, parts), out_shape=(tile,...]
  transfers between devices with their start and end apart: 20 -> 22, of which waited for: 10 -> 10; matrix products, arithmetic and copies ran while one was open for 3% -> 2% of each run, Pallas kernels for 0% -> 0%
where the time goes in v5:
time: 119 us
  starting transfers between devices  63.5 us (53%)
  waiting for transfers between devices  31.4 us (26%)
  Pallas kernels  18 us (15%)
  other arithmetic  2.56 us (2%)
  between operations  2.2 us (2%)
  local copies, waits for them, and re-layouts  1.47 us (1%)
    ppermute x22, starting transfers between devices, shifted(): lax.ppermute(value, axis, [(i, (i + steps) % count) for i in range(count)])  63.5 us
    ppermute x22, waiting for transfers between devices, shifted(): lax.ppermute(value, axis, [(i, (i + steps) % count) for i in range(count)])  31.4 us
    pallas_call x1, Pallas kernels, run_slots(): pl.pallas_call(functools.partial(slots_kernel, side, in_parts, out_parts)...  12.2 us
    pallas_call x1, Pallas kernels, run_finish(): pl.pallas_call(functools.partial(finish_kernel, parts), out_shape=(tile,...  5.72 us
  transfers between devices with their start and end apart: 22, of which 10 were waited for; matrix products, arithmetic and copies ran while one was open for 2% of the time, Pallas kernels for 0%

profile of v5, /device:TPU:0, one launch (start us, length us, event | category | flops | bytes accessed | tf_op | source)
XLA Modules:
  0.0 119.2 jit_solution(11511258316563957755)
XLA Ops:
  0.7 1.4 %fusion = (bf16[1,256,512]{2,1,0:T(8,128)(2,1)S(1)}, bf16[1,256,512]{2,1,0:T(8,128)(2,1)S(1)}) fusion(f32[512,512]{1,0:T(8,128)} %refs_4_.1, f32[512,512]{1,0:T(8,128)} %refs_5_.1), kind=kLoop, calls=%fused_computation.15 | loop fusion | bytes 1048576 | tf_op jit(solution)/shard_map/stack | solution.py:510
  2.1 5.1 %collective-permute-start.1 = (bf16[2,256,512]{2,1,0:T(8,128)(2,1)S(1)}, bf16[2,256,512]{2,1,0:T(8,128)(2,1)}, u32[]{:S(2)}, u32[]{:S(2)}) collective-permute-start(bf16[2,256,512]{2,1,0:T(8,128)(2,1)S(1)} %pad_maximum_fusion.1), channel_id=1, source_target_pairs={{0,24},{8,0},{16,8},{24,16},{1,25},{9,1},{17,9},{25,17},{2,26},{10... | collective-permute-start | bytes 1572872 | tf_op jit(solution)/shard_map/ppermute | solution.py:489
  7.4 1.1 pad_maximum_fusion
  8.5 1.6 %collective-permute-start = (bf16[2,512,512]{2,1,0:T(8,128)(2,1)}, bf16[2,512,512]{2,1,0:T(8,128)(2,1)}, u32[]{:S(2)}, u32[]{:S(2)}) collective-permute-start(bf16[2,512,512]{2,1,0:T(8,128)(2,1)} %pad_maximum_fusion), channel_id=1, source_target_pairs={{0,7},{1,0},{2,1},{3,2},{4,3},{5,4},{6,5},{7,6},{8,15},{9,8},{10,9... | collective-permute-start | bytes 3145736 | tf_op jit(solution)/shard_map/ppermute | solution.py:489
  10.2 0.6 collective-permute-start.2
  10.7 8.8 %collective-permute-done.1.refs_7_ = bf16[2,256,512]{2,1,0:T(8,128)(2,1)} collective-permute-done((bf16[2,256,512]{2,1,0:T(8,128)(2,1)S(1)}, bf16[2,256,512]{2,1,0:T(8,128)(2,1)}, u32[]{:S(2)}, u32[]{:S(2)}) %collective-permute-start.1) | collective-permute-done | bytes 524320 | tf_op jit(solution)/shard_map/ppermute | solution.py:489
  19.6 4.4 %collective-permute-start.3 = (bf16[2,80,512]{2,1,0:T(8,128)(2,1)S(1)}, bf16[2,80,512]{2,1,0:T(8,128)(2,1)}, u32[]{:S(2)}, u32[]{:S(2)}) collective-permute-start(bf16[2,80,512]{2,1,0:T(8,128)(2,1)S(1)} %fusion.3), channel_id=1, source_target_pairs={{0,24},{8,0},{16,8},{24,16},{1,25},{9,1},{17,9},{25,17},{2,26},{10... | collective-permute-start | bytes 491528 | tf_op jit(solution)/shard_map/ppermute | solution.py:489
  24.1 2.3 %collective-permute-start.6 = (bf16[2,128,512]{2,1,0:T(8,128)(2,1)S(1)}, bf16[2,128,512]{2,1,0:T(8,128)(2,1)}, u32[]{:S(2)}, u32[]{:S(2)}) collective-permute-start(bf16[2,128,512]{2,1,0:T(8,128)(2,1)S(1)} %collective-permute-done.2.refs_8_), channel_id=1, source_target_pairs={{0,7},{1,0},{2,1},{3,2},{4,3},{5,4},{6,5},{7,6},{8,15},{9,8},{10,9... | collective-permute-start | bytes 786440 | tf_op jit(solution)/shard_map/ppermute | solution.py:489
  27.1 3.2 %collective-permute-done.4.refs_10_ = bf16[2,48,512]{2,1,0:T(8,128)(2,1)S(1)} collective-permute-done((bf16[2,48,512]{2,1,0:T(8,128)(2,1)S(1)}, bf16[2,48,512]{2,1,0:T(8,128)(2,1)S(1)}, u32[]{:S(2)}, u32[]{:S(2)}) %collective-permute-start.4) | collective-permute-done | bytes 98336 | tf_op jit(solution)/shard_map/ppermute | solution.py:489
  30.3 1.7 %collective-permute-start.8 = (bf16[2,48,512]{2,1,0:T(8,128)(2,1)S(1)}, bf16[2,48,512]{2,1,0:T(8,128)(2,1)}, u32[]{:S(2)}, u32[]{:S(2)}) collective-permute-start(bf16[2,48,512]{2,1,0:T(8,128)(2,1)S(1)} %collective-permute-done.4.refs_10_), channel_id=1, source_target_pairs={{0,7},{1,0},{2,1},{3,2},{4,3},{5,4},{6,5},{7,6},{8,15},{9,8},{10,9... | collective-permute-start | bytes 294920 | tf_op jit(solution)/shard_map/ppermute | solution.py:489
  32.0 0.9 collective-permute-start.7
  32.8 0.9 add_reduce_fusion
  34.5 1.5 %collective-permute-done.7.refs_13_ = bf16[2,80,512]{2,1,0:T(8,128)(2,1)} collective-permute-done((bf16[2,80,512]{2,1,0:T(8,128)(2,1)}, bf16[2,80,512]{2,1,0:T(8,128)(2,1)}, u32[]{:S(2)}, u32[]{:S(2)}) %collective-permute-start.7) | collective-permute-done | bytes 163872 | tf_op jit(solution)/shard_map/ppermute | solution.py:489
  36.1 12.2 %slots.1 = (f32[2,512,512]{2,1,0:T(8,128)}, bf16[2,512,512]{2,1,0:T(8,128)(2,1)S(1)}, f32[2,1024]{1,0:T(2,128)S(1)}, f32[2,3072]{1,0:T(2,128)S(1)}, f32[2,3072]{...) custom-call(s32[1,1]{1,0:T(1,128)S(6)} %copy.15.refs_0_, ...), custom_call_target="tpu_custom_call" | custom-call | tf_op jit(solution)/shard_map/slots/pallas_call | solution.py:298
  48.3 0.1 collective-permute-start.14
  48.5 6.3 %collective-permute-start.9 = (bf16[2,512,512]{2,1,0:T(8,128)(2,1)S(1)}, bf16[2,512,512]{2,1,0:T(8,128)(2,1)S(1)}, u32[]{:S(2)}, u32[]{:S(2)}) collective-permute-start(bf16[2,512,512]{2,1,0:T(8,128)(2,1)S(1)} %get-tuple-element.27), channel_id=1, source_target_pairs={{0,1},{1,2},{2,3},{3,4},{4,5},{5,6},{6,7},{7,0},{8,9},{9,10},{10,1... | collective-permute-start | bytes 3145736 | tf_op jit(solution)/shard_map/ppermute | solution.py:489
  54.8 8.0 %collective-permute-start.10 = (bf16[2,64,512]{2,1,0:T(8,128)(2,1)S(1)}, bf16[2,64,512]{2,1,0:T(8,128)(2,1)S(1)}, u32[]{:S(2)}, u32[]{:S(2)}) collective-permute-start(bf16[2,64,512]{2,1,0:T(8,128)(2,1)S(1)} %get-tuple-element.29), channel_id=1, source_target_pairs={{0,1},{1,2},{2,3},{3,4},{4,5},{5,6},{6,7},{7,0},{8,9},{9,10},{10,1... | collective-permute-start | bytes 393224 | tf_op jit(solution)/shard_map/ppermute | solution.py:489
  62.8 0.2 add_convert_fusion
  63.0 7.4 %collective-permute-start.15 = (bf16[2,256,512]{2,1,0:T(8,128)(2,1)S(1)}, bf16[2,256,512]{2,1,0:T(8,128)(2,1)S(1)}, u32[]{:S(2)}, u32[]{:S(2)}) collective-permute-start(bf16[2,256,512]{2,1,0:T(8,128)(2,1)S(1)} %add_convert_fusion), channel_id=1, source_target_pairs={{0,8},{8,16},{16,24},{24,0},{1,9},{9,17},{17,25},{25,1},{2,10},{10... | collective-permute-start | bytes 1572872 | tf_op jit(solution)/shard_map/ppermute | solution.py:489
  70.5 4.0 %collective-permute-start.13 = (bf16[2,192,512]{2,1,0:T(8,128)(2,1)S(1)}, bf16[2,192,512]{2,1,0:T(8,128)(2,1)S(1)}, u32[]{:S(2)}, u32[]{:S(2)}) collective-permute-start(bf16[2,192,512]{2,1,0:T(8,128)(2,1)S(1)} %add_convert_fusion.1), channel_id=1, source_target_pairs={{0,8},{8,16},{16,24},{24,0},{1,9},{9,17},{17,25},{25,1},{2,10},{10... | collective-permute-start | bytes 1179656 | tf_op jit(solution)/shard_map/ppermute | solution.py:489
  74.6 0.3 collective-permute-done.10
  74.9 12.2 %collective-permute-start.11 = (bf16[2,64,512]{2,1,0:T(8,128)(2,1)S(1)}, bf16[2,64,512]{2,1,0:T(8,128)(2,1)S(1)}, u32[]{:S(2)}, u32[]{:S(2)}) collective-permute-start(bf16[2,64,512]{2,1,0:T(8,128)(2,1)S(1)} %add_convert_fusion.2), channel_id=1, source_target_pairs={{0,8},{8,16},{16,24},{24,0},{1,9},{9,17},{17,25},{25,1},{2,10},{10... | collective-permute-start | bytes 393224 | tf_op jit(solution)/shard_map/ppermute | solution.py:489
  87.1 1.4 %collective-permute-done.16.right_ref = f32[2,1024]{1,0:T(2,128)S(1)} collective-permute-done((f32[2,1024]{1,0:T(2,128)S(1)}, f32[2,1024]{1,0:T(2,128)S(1)}, u32[]{:S(2)}, u32[]{:S(2)}) %collective-permute-start.16) | collective-permute-done | bytes 8224 | tf_op jit(solution)/shard_map/ppermute | solution.py:489
  88.5 4.5 %collective-permute-done.18.second_ref = f32[2,1024]{1,0:T(2,128)S(1)} collective-permute-done((f32[2,1024]{1,0:T(2,128)S(1)}, f32[2,1024]{1,0:T(2,128)S(1)}, u32[]{:S(2)}, u32[]{:S(2)}) %collective-permute-start.18) | collective-permute-done | bytes 8224 | tf_op jit(solution)/shard_map/ppermute | solution.py:489
  93.0 4.1 %collective-permute-done.17.left_ref = f32[2,3072]{1,0:T(2,128)S(1)} collective-permute-done((f32[2,3072]{1,0:T(2,128)S(1)}, f32[2,3072]{1,0:T(2,128)S(1)}, u32[]{:S(2)}, u32[]{:S(2)}) %collective-permute-start.17) | collective-permute-done | bytes 24608 | tf_op jit(solution)/shard_map/ppermute | solution.py:489
  97.3 4.9 %collective-permute-start.20 = (f32[2,6,128]{2,1,0:T(8,128)S(1)}, f32[2,6,128]{2,1,0:T(8,128)S(1)}, u32[]{:S(2)}, u32[]{:S(2)}) collective-permute-start(f32[2,6,128]{2,1,0:T(8,128)S(1)} %get-tuple-element.39), channel_id=1, source_target_pairs={{0,16},{8,24},{16,0},{24,8},{1,17},{9,25},{17,1},{25,9},{2,18},{10... | collective-permute-start | bytes 18440 | tf_op jit(solution)/shard_map/ppermute | solution.py:489
  102.2 1.6 %collective-permute-done.20.refs_6_ = f32[2,6,128]{2,1,0:T(8,128)S(1)} collective-permute-done((f32[2,6,128]{2,1,0:T(8,128)S(1)}, f32[2,6,128]{2,1,0:T(8,128)S(1)}, u32[]{:S(2)}, u32[]{:S(2)}) %collective-permute-start.20) | collective-permute-done | bytes 6176 | tf_op jit(solution)/shard_map/ppermute | solution.py:489
  103.8 2.4 %collective-permute-start.21 = (f32[2,6,128]{2,1,0:T(8,128)S(1)}, f32[2,6,128]{2,1,0:T(8,128)S(1)}, u32[]{:S(2)}, u32[]{:S(2)}) collective-permute-start(f32[2,6,128]{2,1,0:T(8,128)S(1)} %get-tuple-element.40), channel_id=1, source_target_pairs={{0,24},{8,0},{16,8},{24,16},{1,25},{9,1},{17,9},{25,17},{2,26},{10... | collective-permute-start | bytes 18440 | tf_op jit(solution)/shard_map/ppermute | solution.py:489
  106.3 1.4 %collective-permute-done.21.refs_7_ = f32[2,6,128]{2,1,0:T(8,128)S(1)} collective-permute-done((f32[2,6,128]{2,1,0:T(8,128)S(1)}, f32[2,6,128]{2,1,0:T(8,128)S(1)}, u32[]{:S(2)}, u32[]{:S(2)}) %collective-permute-start.21) | collective-permute-done | bytes 6176 | tf_op jit(solution)/shard_map/ppermute | solution.py:489
  107.6 1.3 %collective-permute-start.19 = (f32[2,14,128]{2,1,0:T(8,128)S(1)}, f32[2,14,128]{2,1,0:T(8,128)S(1)}, u32[]{:S(2)}, u32[]{:S(2)}) collective-permute-start(f32[2,14,128]{2,1,0:T(8,128)S(1)} %get-tuple-element.38), channel_id=1, source_target_pairs={{0,8},{8,16},{16,24},{24,0},{1,9},{9,17},{17,25},{25,1},{2,10},{10... | collective-permute-start | bytes 43016 | tf_op jit(solution)/shard_map/ppermute | solution.py:489
  109.0 4.5 %collective-permute-done.19.refs_5_ = f32[2,14,128]{2,1,0:T(8,128)S(1)} collective-permute-done((f32[2,14,128]{2,1,0:T(8,128)S(1)}, f32[2,14,128]{2,1,0:T(8,128)S(1)}, u32[]{:S(2)}, u32[]{:S(2)}) %collective-permute-start.19) | collective-permute-done | bytes 14368 | tf_op jit(solution)/shard_map/ppermute | solution.py:489
  113.5 5.7 %finish.1 = (f32[512,512]{1,0:T(8,128)}, f32[512,512]{1,0:T(8,128)}) custom-call(f32[2,512,512]{2,1,0:T(8,128)S(1)} %copy-done.1, bf16[2,512,512]{2,1,0:T(8,128)(2,1)S(1)} %collective-permute-done.9.refs_1_, bf16[2,64,512]{2,1,0:T(8,128)(2,1)S(1)} %collective-permute-done.11.refs_2_, bf16[2,192,512]{2,1,0:T(8,128)(2,1)S(1)} %collective-permute-done.13.refs_3_, ...), custom_call_target="tpu_custom_call" | custom-call | tf_op jit(solution)/shard_map/finish/pallas_call | solution.py:433
  (49 shorter events, 0.8 us)
Async XLA Ops:
  0.6 6.7 %copy-start.8 = (f32[512,512]{1,0:T(8,128)S(1)}, f32[512,512]{1,0:T(8,128)}, u32[]{:S(2)}) copy-start(f32[512,512]{1,0:T(8,128)} %refs_5_.1) | copy-start | bytes 3145732
  2.1 17.4 %collective-permute-start.1 = (bf16[2,256,512]{2,1,0:T(8,128)(2,1)S(1)}, bf16[2,256,512]{2,1,0:T(8,128)(2,1)}, u32[]{:S(2)}, u32[]{:S(2)}) collective-permute-start(bf16[2,256,512]{2,1,0:T(8,128)(2,1)S(1)} %pad_maximum_fusion.1), channel_id=1, source_target_pairs={{0,24},{8,0},{16,8},{24,16},{1,25},{9,1},{17,9},{25,17},{2,26},{10... | collective-permute-start | bytes 1572872 | tf_op jit(solution)/shard_map/ppermute | solution.py:489
  8.5 24.4 %copy-start.9 = (f32[512,512]{1,0:T(8,128)S(1)}, f32[512,512]{1,0:T(8,128)}, u32[]{:S(2)}) copy-start(f32[512,512]{1,0:T(8,128)} %refs_16_.1) | copy-start | bytes 3145732
  8.5 24.4 %copy-start.10 = (f32[512,512]{1,0:T(8,128)S(1)}, f32[512,512]{1,0:T(8,128)}, u32[]{:S(2)}) copy-start(f32[512,512]{1,0:T(8,128)} %refs_15_.1) | copy-start | bytes 3145732
  8.5 27.5 %collective-permute-start = (bf16[2,512,512]{2,1,0:T(8,128)(2,1)}, bf16[2,512,512]{2,1,0:T(8,128)(2,1)}, u32[]{:S(2)}, u32[]{:S(2)}) collective-permute-start(bf16[2,512,512]{2,1,0:T(8,128)(2,1)} %pad_maximum_fusion), channel_id=1, source_target_pairs={{0,7},{1,0},{2,1},{3,2},{4,3},{5,4},{6,5},{7,6},{8,15},{9,8},{10,9... | collective-permute-start | bytes 3145736 | tf_op jit(solution)/shard_map/ppermute | solution.py:489
  10.1 25.9 %copy-start.2 = (bf16[512,512]{1,0:T(8,128)(2,1)S(1)}, bf16[512,512]{1,0:T(8,128)(2,1)}, u32[]{:S(2)}) copy-start(bf16[512,512]{1,0:T(8,128)(2,1)} %constant.23.clone.refs_22_) | copy-start | bytes 1572868
  10.1 25.9 %copy-start.3 = (bf16[4,256,256]{2,1,0:T(8,128)(2,1)S(1)}, bf16[4,256,256]{2,1,0:T(8,128)(2,1)}, u32[]{:S(2)}) copy-start(bf16[4,256,256]{2,1,0:T(8,128)(2,1)} %constant.22.clone.refs_21_) | copy-start | bytes 1572868
  10.1 25.9 %copy-start.4 = (bf16[512,512]{1,0:T(8,128)(2,1)S(1)}, bf16[512,512]{1,0:T(8,128)(2,1)}, u32[]{:S(2)}) copy-start(bf16[512,512]{1,0:T(8,128)(2,1)} %constant.20.clone.refs_19_) | copy-start | bytes 1572868
  10.2 25.9 %copy-start.5 = (bf16[4,256,256]{2,1,0:T(8,128)(2,1)S(1)}, bf16[4,256,256]{2,1,0:T(8,128)(2,1)}, u32[]{:S(2)}) copy-start(bf16[4,256,256]{2,1,0:T(8,128)(2,1)} %constant.19.clone.refs_18_) | copy-start | bytes 1572868
  10.2 25.9 %copy-start.6 = (s32[1,4]{1,0:T(1,128)S(1)}, s32[1,4]{1,0:T(1,128)}, u32[]{:S(2)}) copy-start(s32[1,4]{1,0:T(1,128)} %refs_1_.1) | copy-start | bytes 52
  10.2 25.9 %copy-start.7 = (s32[1,4]{1,0:T(1,128)S(1)}, s32[1,4]{1,0:T(1,128)}, u32[]{:S(2)}) copy-start(s32[1,4]{1,0:T(1,128)} %refs_2_.1) | copy-start | bytes 52
  10.2 13.9 %collective-permute-start.2 = (bf16[2,128,512]{2,1,0:T(8,128)(2,1)S(1)}, bf16[2,128,512]{2,1,0:T(8,128)(2,1)S(1)}, u32[]{:S(2)}, u32[]{:S(2)}) collective-permute-start(bf16[2,128,512]{2,1,0:T(8,128)(2,1)S(1)} %fusion.2), channel_id=1, source_target_pairs={{0,24},{8,0},{16,8},{24,16},{1,25},{9,1},{17,9},{25,17},{2,26},{10... | collective-permute-start | bytes 786440 | tf_op jit(solution)/shard_map/ppermute | solution.py:489
  19.6 16.4 %collective-permute-start.5 = (bf16[2,256,512]{2,1,0:T(8,128)(2,1)}, bf16[2,256,512]{2,1,0:T(8,128)(2,1)}, u32[]{:S(2)}, u32[]{:S(2)}) collective-permute-start(bf16[2,256,512]{2,1,0:T(8,128)(2,1)} %collective-permute-done.1.refs_7_), channel_id=1, source_target_pairs={{0,7},{1,0},{2,1},{3,2},{4,3},{5,4},{6,5},{7,6},{8,15},{9,8},{10,9... | collective-permute-start | bytes 1572872 | tf_op jit(solution)/shard_map/ppermute | solution.py:489
  19.6 12.4 %collective-permute-start.3 = (bf16[2,80,512]{2,1,0:T(8,128)(2,1)S(1)}, bf16[2,80,512]{2,1,0:T(8,128)(2,1)}, u32[]{:S(2)}, u32[]{:S(2)}) collective-permute-start(bf16[2,80,512]{2,1,0:T(8,128)(2,1)S(1)} %fusion.3), channel_id=1, source_target_pairs={{0,24},{8,0},{16,8},{24,16},{1,25},{9,1},{17,9},{25,17},{2,26},{10... | collective-permute-start | bytes 491528 | tf_op jit(solution)/shard_map/ppermute | solution.py:489
  24.0 6.2 %collective-permute-start.4 = (bf16[2,48,512]{2,1,0:T(8,128)(2,1)S(1)}, bf16[2,48,512]{2,1,0:T(8,128)(2,1)S(1)}, u32[]{:S(2)}, u32[]{:S(2)}) collective-permute-start(bf16[2,48,512]{2,1,0:T(8,128)(2,1)S(1)} %fusion.4), channel_id=1, source_target_pairs={{0,24},{8,0},{16,8},{24,16},{1,25},{9,1},{17,9},{25,17},{2,26},{10... | collective-permute-start | bytes 294920 | tf_op jit(solution)/shard_map/ppermute | solution.py:489
  24.1 11.9 %collective-permute-start.6 = (bf16[2,128,512]{2,1,0:T(8,128)(2,1)S(1)}, bf16[2,128,512]{2,1,0:T(8,128)(2,1)}, u32[]{:S(2)}, u32[]{:S(2)}) collective-permute-start(bf16[2,128,512]{2,1,0:T(8,128)(2,1)S(1)} %collective-permute-done.2.refs_8_), channel_id=1, source_target_pairs={{0,7},{1,0},{2,1},{3,2},{4,3},{5,4},{6,5},{7,6},{8,15},{9,8},{10,9... | collective-permute-start | bytes 786440 | tf_op jit(solution)/shard_map/ppermute | solution.py:489
  30.3 4.2 %collective-permute-start.8 = (bf16[2,48,512]{2,1,0:T(8,128)(2,1)S(1)}, bf16[2,48,512]{2,1,0:T(8,128)(2,1)}, u32[]{:S(2)}, u32[]{:S(2)}) collective-permute-start(bf16[2,48,512]{2,1,0:T(8,128)(2,1)S(1)} %collective-permute-done.4.refs_10_), channel_id=1, source_target_pairs={{0,7},{1,0},{2,1},{3,2},{4,3},{5,4},{6,5},{7,6},{8,15},{9,8},{10,9... | collective-permute-start | bytes 294920 | tf_op jit(solution)/shard_map/ppermute | solution.py:489
  32.0 4.0 %collective-permute-start.7 = (bf16[2,80,512]{2,1,0:T(8,128)(2,1)}, bf16[2,80,512]{2,1,0:T(8,128)(2,1)}, u32[]{:S(2)}, u32[]{:S(2)}) collective-permute-start(bf16[2,80,512]{2,1,0:T(8,128)(2,1)} %collective-permute-done.3.refs_9_), channel_id=1, source_target_pairs={{0,7},{1,0},{2,1},{3,2},{4,3},{5,4},{6,5},{7,6},{8,15},{9,8},{10,9... | collective-permute-start | bytes 491528 | tf_op jit(solution)/shard_map/ppermute | solution.py:489
  48.3 14.5 %collective-permute-start.14 = (bf16[2,256,512]{2,1,0:T(8,128)(2,1)S(1)}, bf16[2,256,512]{2,1,0:T(8,128)(2,1)S(1)}, u32[]{:S(2)}, u32[]{:S(2)}) collective-permute-start(bf16[2,256,512]{2,1,0:T(8,128)(2,1)S(1)} %get-tuple-element.33), channel_id=1, source_target_pairs={{0,1},{1,2},{2,3},{3,4},{4,5},{5,6},{6,7},{7,0},{8,9},{9,10},{10,1... | collective-permute-start | bytes 1572872 | tf_op jit(solution)/shard_map/ppermute | solution.py:489
  48.4 22.0 %collective-permute-start.12 = (bf16[2,192,512]{2,1,0:T(8,128)(2,1)S(1)}, bf16[2,192,512]{2,1,0:T(8,128)(2,1)S(1)}, u32[]{:S(2)}, u32[]{:S(2)}) collective-permute-start(bf16[2,192,512]{2,1,0:T(8,128)(2,1)S(1)} %get-tuple-element.31), channel_id=1, source_target_pairs={{0,1},{1,2},{2,3},{3,4},{4,5},{5,6},{6,7},{7,0},{8,9},{9,10},{10,1... | collective-permute-start | bytes 1179656 | tf_op jit(solution)/shard_map/ppermute | solution.py:489
  48.5 65.0 %collective-permute-start.9 = (bf16[2,512,512]{2,1,0:T(8,128)(2,1)S(1)}, bf16[2,512,512]{2,1,0:T(8,128)(2,1)S(1)}, u32[]{:S(2)}, u32[]{:S(2)}) collective-permute-start(bf16[2,512,512]{2,1,0:T(8,128)(2,1)S(1)} %get-tuple-element.27), channel_id=1, source_target_pairs={{0,1},{1,2},{2,3},{3,4},{4,5},{5,6},{6,7},{7,0},{8,9},{9,10},{10,1... | collective-permute-start | bytes 3145736 | tf_op jit(solution)/shard_map/ppermute | solution.py:489
  54.8 20.1 %collective-permute-start.10 = (bf16[2,64,512]{2,1,0:T(8,128)(2,1)S(1)}, bf16[2,64,512]{2,1,0:T(8,128)(2,1)S(1)}, u32[]{:S(2)}, u32[]{:S(2)}) collective-permute-start(bf16[2,64,512]{2,1,0:T(8,128)(2,1)S(1)} %get-tuple-element.29), channel_id=1, source_target_pairs={{0,1},{1,2},{2,3},{3,4},{4,5},{5,6},{6,7},{7,0},{8,9},{9,10},{10,1... | collective-permute-start | bytes 393224 | tf_op jit(solution)/shard_map/ppermute | solution.py:489
  62.8 50.7 %copy-start.1 = (f32[2,512,512]{2,1,0:T(8,128)S(1)}, f32[2,512,512]{2,1,0:T(8,128)}, u32[]{:S(2)}) copy-start(f32[2,512,512]{2,1,0:T(8,128)} %get-tuple-element.26.refs_0_) | copy-start | bytes 6291460
  63.0 50.5 %collective-permute-start.15 = (bf16[2,256,512]{2,1,0:T(8,128)(2,1)S(1)}, bf16[2,256,512]{2,1,0:T(8,128)(2,1)S(1)}, u32[]{:S(2)}, u32[]{:S(2)}) collective-permute-start(bf16[2,256,512]{2,1,0:T(8,128)(2,1)S(1)} %add_convert_fusion), channel_id=1, source_target_pairs={{0,8},{8,16},{16,24},{24,0},{1,9},{9,17},{17,25},{25,1},{2,10},{10... | collective-permute-start | bytes 1572872 | tf_op jit(solution)/shard_map/ppermute | solution.py:489
  70.5 42.9 %collective-permute-start.13 = (bf16[2,192,512]{2,1,0:T(8,128)(2,1)S(1)}, bf16[2,192,512]{2,1,0:T(8,128)(2,1)S(1)}, u32[]{:S(2)}, u32[]{:S(2)}) collective-permute-start(bf16[2,192,512]{2,1,0:T(8,128)(2,1)S(1)} %add_convert_fusion.1), channel_id=1, source_target_pairs={{0,8},{8,16},{16,24},{24,0},{1,9},{9,17},{17,25},{25,1},{2,10},{10... | collective-permute-start | bytes 1179656 | tf_op jit(solution)/shard_map/ppermute | solution.py:489
  74.9 38.5 %collective-permute-start.11 = (bf16[2,64,512]{2,1,0:T(8,128)(2,1)S(1)}, bf16[2,64,512]{2,1,0:T(8,128)(2,1)S(1)}, u32[]{:S(2)}, u32[]{:S(2)}) collective-permute-start(bf16[2,64,512]{2,1,0:T(8,128)(2,1)S(1)} %add_convert_fusion.2), channel_id=1, source_target_pairs={{0,8},{8,16},{16,24},{24,0},{1,9},{9,17},{17,25},{25,1},{2,10},{10... | collective-permute-start | bytes 393224 | tf_op jit(solution)/shard_map/ppermute | solution.py:489
  87.1 1.4 %collective-permute-start.16 = (f32[2,1024]{1,0:T(2,128)S(1)}, f32[2,1024]{1,0:T(2,128)S(1)}, u32[]{:S(2)}, u32[]{:S(2)}) collective-permute-start(f32[2,1024]{1,0:T(2,128)S(1)} %get-tuple-element.34), channel_id=1, source_target_pairs={{0,7},{1,0},{2,1},{3,2},{4,3},{5,4},{6,5},{7,6},{8,15},{9,8},{10,9... | collective-permute-start | bytes 24584 | tf_op jit(solution)/shard_map/ppermute | solution.py:489
  88.5 4.5 %collective-permute-start.18 = (f32[2,1024]{1,0:T(2,128)S(1)}, f32[2,1024]{1,0:T(2,128)S(1)}, u32[]{:S(2)}, u32[]{:S(2)}) collective-permute-start(f32[2,1024]{1,0:T(2,128)S(1)} %get-tuple-element.36), channel_id=1, source_target_pairs={{0,2},{1,3},{2,4},{3,5},{4,6},{5,7},{6,0},{7,1},{8,10},{9,11},{10,... | collective-permute-start | bytes 24584 | tf_op jit(solution)/shard_map/ppermute | solution.py:489
  93.0 4.2 %collective-permute-start.17 = (f32[2,3072]{1,0:T(2,128)S(1)}, f32[2,3072]{1,0:T(2,128)S(1)}, u32[]{:S(2)}, u32[]{:S(2)}) collective-permute-start(f32[2,3072]{1,0:T(2,128)S(1)} %get-tuple-element.35), channel_id=1, source_target_pairs={{0,1},{1,2},{2,3},{3,4},{4,5},{5,6},{6,7},{7,0},{8,9},{9,10},{10,1... | collective-permute-start | bytes 73736 | tf_op jit(solution)/shard_map/ppermute | solution.py:489
  97.3 6.6 %collective-permute-start.20 = (f32[2,6,128]{2,1,0:T(8,128)S(1)}, f32[2,6,128]{2,1,0:T(8,128)S(1)}, u32[]{:S(2)}, u32[]{:S(2)}) collective-permute-start(f32[2,6,128]{2,1,0:T(8,128)S(1)} %get-tuple-element.39), channel_id=1, source_target_pairs={{0,16},{8,24},{16,0},{24,8},{1,17},{9,25},{17,1},{25,9},{2,18},{10... | collective-permute-start | bytes 18440 | tf_op jit(solution)/shard_map/ppermute | solution.py:489
  103.8 3.8 %collective-permute-start.21 = (f32[2,6,128]{2,1,0:T(8,128)S(1)}, f32[2,6,128]{2,1,0:T(8,128)S(1)}, u32[]{:S(2)}, u32[]{:S(2)}) collective-permute-start(f32[2,6,128]{2,1,0:T(8,128)S(1)} %get-tuple-element.40), channel_id=1, source_target_pairs={{0,24},{8,0},{16,8},{24,16},{1,25},{9,1},{17,9},{25,17},{2,26},{10... | collective-permute-start | bytes 18440 | tf_op jit(solution)/shard_map/ppermute | solution.py:489
  107.6 5.8 %collective-permute-start.19 = (f32[2,14,128]{2,1,0:T(8,128)S(1)}, f32[2,14,128]{2,1,0:T(8,128)S(1)}, u32[]{:S(2)}, u32[]{:S(2)}) collective-permute-start(f32[2,14,128]{2,1,0:T(8,128)S(1)} %get-tuple-element.38), channel_id=1, source_target_pairs={{0,8},{8,16},{16,24},{24,0},{1,9},{9,17},{17,25},{25,1},{2,10},{10... | collective-permute-start | bytes 43016 | tf_op jit(solution)/shard_map/ppermute | solution.py:489
  (1 other events, 6.6 us)

commit v6 on v5

--- a/solution.py
+++ b/solution.py
@@ -77,8 +77,8 @@
     rows_in, cols_in, cols_out, rows_out, pick = take(5)
     own_out, right_out, left_out, beside_out, kept_out, second_out = take(6)
     below_outs, diag_outs = take(len(out_parts)), take(len(out_parts))
-    region, sums, probe, exits, wide, half, delta, back, amp, held, amp_held = refs[:11]
-    table_held, sems, amp_sems, table_sems = refs[11:16], refs[16], refs[17], refs[18]
+    region, sums, probe, exits, wide, half, delta, back, amp, held, amp_held, wave = refs[:12]
+    table_held, sems, amp_sems, table_sems = refs[12:17], refs[17], refs[18], refs[19]
     quarter, chunks = side // 4, side // LANES
     f32, bf16 = jnp.float32, jnp.bfloat16
 
@@ -130,30 +130,57 @@
 
     lane = lax.broadcasted_iota(jnp.int32, (1, LANES), 1)
 
+    def corner(s):
+        return oy_ref[0, s], ox_ref[0, s] // LANES, ox_ref[0, s] % LANES
+
+    def take_patch(s, c):
+        oy, q, b = corner(s)
+        rows = pl.ds(oy + c, quarter, stride=4)
+        mine = pl.ds(c, quarter, stride=4)
+        before = None
+        for a in range(chunks + 1):
+            now = [pltpu.roll(region[p, q + a, rows, :], (LANES - b) % LANES, axis=1) for p in range(2)]
+            if a > 0:
+                o_re, o_im = (jnp.where(lane < LANES - b, before[p], now[p]) for p in range(2))
+                p_re, p_im = probe[0, a - 1, mine, :], probe[1, a - 1, mine, :]
+                lanes = slice((a - 1) * LANES, a * LANES)
+                exits[c, :quarter, lanes] = (p_re * o_re - p_im * o_im).astype(bf16)
+                exits[c, quarter:, lanes] = (p_re * o_im + p_im * o_re).astype(bf16)
+            before = now
+
+    rows_at = 16
+
+    def place_term(s, r):
+        oy, q, b = corner(s)
+        at = r * rows_at
+        before = [jnp.zeros((rows_at, LANES), f32)] * 8
+        for a in range(chunks + 1):
+            now = [jnp.zeros((rows_at, LANES), f32)] * 8
+            if a < chunks:
+                lanes = slice(a * LANES, (a + 1) * LANES)
+                re = [wave[c, at : at + rows_at, lanes] for c in range(4)]
+                im = [wave[c, quarter + at : quarter + at + rows_at, lanes] for c in range(4)]
+                er, ei, fr, fi = re[0] + re[2], im[0] + im[2], re[0] - re[2], im[0] - im[2]
+                gr, gi, hr, hi = re[1] + re[3], im[1] + im[3], re[1] - re[3], im[1] - im[3]
+                outs = ((er + gr, ei + gi), (fr - hi, fi + hr), (er - gr, ei - gi), (fr + hi, fi - hr))
+                for m, (w_re, w_im) in enumerate(outs):
+                    mine = slice(m * quarter + at, m * quarter + at + rows_at)
+                    p_re, p_im = probe[0, a, mine, :], probe[1, a, mine, :]
+                    now[2 * m] = pltpu.roll(p_re * w_re + p_im * w_im, b, axis=1)
+                    now[2 * m + 1] = pltpu.roll(p_re * w_im - p_im * w_re, b, axis=1)
+            for k in range(8):
+                rows = pl.ds(oy + (k // 2) * quarter + at, rows_at)
+                sums[k % 2, q + a, rows, :] += jnp.where(lane >= b, now[k], before[k])
+            before = now
+
+    blocks = quarter // rows_at
+    wave[...] = jnp.zeros_like(wave)
+    for c in range(4):
+        take_patch(0, c)
+
     def one_slot(s, carry):
-        oy = oy_ref[0, s]
-        ox = ox_ref[0, s]
-        q = ox // LANES
-        b = ox % LANES
-        inward = (LANES - b) % LANES
-        keep = lane < LANES - b
-        placed = lane >= b
-
+        later, earlier = jnp.minimum(s + 1, amp_held.shape[0] - 1), jnp.maximum(s - 1, 0)
         amp_fetch(s).wait()
-
-        for c in range(4):
-            rows = pl.ds(oy + c, quarter, stride=4)
-            before = None
-            for a in range(chunks + 1):
-                now = [pltpu.roll(region[p, q + a, rows, :], inward, axis=1) for p in range(2)]
-                if a > 0:
-                    o_re, o_im = (jnp.where(keep, before[p], now[p]) for p in range(2))
-                    mine = pl.ds(c, quarter, stride=4)
-                    p_re, p_im = probe[0, a - 1, mine, :], probe[1, a - 1, mine, :]
-                    lanes = slice((a - 1) * LANES, a * LANES)
-                    exits[c, :quarter, lanes] = (p_re * o_re - p_im * o_im).astype(bf16)
-                    exits[c, quarter:, lanes] = (p_re * o_im + p_im * o_re).astype(bf16)
-                before = now
         for c in range(4):
             wide[c] = dot(rows_in[c], exits[c])
         step = quarter // 4
@@ -180,6 +207,7 @@
 
         for cc in range(4):
             wide[cc] = dot(half[cc], cols_in[...])
+            take_patch(later, cc)
         mid = chunks // 2
         for cc in range(4):
             for part in range(mid):
@@ -202,6 +230,8 @@
         for part in range(2):
             for r in range(2):
                 wide[2 * part + r] = dot(delta[part, r * side // 2 : (r + 1) * side // 2, :], cols_out[part])
+                for block in range(blocks // 4):
+                    place_term(earlier, (2 * part + r) * (blocks // 4) + block)
         for cc in range(4):
             for k in range(2):
                 for a in range(mid):
@@ -213,39 +243,12 @@
                     back[cc, put, (mid + a) * LANES : (mid + a + 1) * LANES] = (even - odd).astype(bf16)
 
         for c in range(4):
-            wide[c] = dot(rows_out[c], back[c])
-        rows_at = 16
-        for r in range(quarter // rows_at):
-            before = [None] * 8
-            for a in range(chunks + 1):
-                now = [None] * 8
-                if a < chunks:
-                    lanes = slice(a * LANES, (a + 1) * LANES)
-                    at = r * rows_at
-                    re = [wide[c, at : at + rows_at, lanes] for c in range(4)]
-                    im = [wide[c, quarter + at : quarter + at + rows_at, lanes] for c in range(4)]
-                    er, ei, fr, fi = re[0] + re[2], im[0] + im[2], re[0] - re[2], im[0] - im[2]
-                    gr, gi, hr, hi = re[1] + re[3], im[1] + im[3], re[1] - re[3], im[1] - im[3]
-                    outs = (
-                        (er + gr, ei + gi),
-                        (fr - hi, fi + hr),
-                        (er - gr, ei - gi),
-                        (fr + hi, fi - hr),
-                    )
-                    for m, (w_re, w_im) in enumerate(outs):
-                        mine = slice(m * quarter + at, m * quarter + at + rows_at)
-                        p_re, p_im = probe[0, a, mine, :], probe[1, a, mine, :]
-                        now[2 * m] = pltpu.roll(p_re * w_re + p_im * w_im, b, axis=1)
-                        now[2 * m + 1] = pltpu.roll(p_re * w_im - p_im * w_re, b, axis=1)
-                for k in range(8):
-                    one = jnp.zeros((rows_at, LANES), f32) if now[k] is None else now[k]
-                    two = jnp.zeros((rows_at, LANES), f32) if before[k] is None else before[k]
-                    rows = pl.ds(oy + (k // 2) * quarter + r * rows_at, rows_at)
-                    sums[k % 2, q + a, rows, :] += jnp.where(placed, one, two)
-                before = now
+            wave[c] = dot(rows_out[c], back[c])
         return carry
 
     lax.fori_loop(0, count_ref[0, 0], one_slot, 0)
+    for r in range(blocks):
+        place_term(count_ref[0, 0] - 1, r)
 
     scale = scale_ref[0, 0]
     for p in range(2):
@@ -312,12 +315,13 @@
             pltpu.VMEM((chunks, side, LANES), f32),
             pltpu.VMEM((2, chunks, side, LANES), f32),
             pltpu.VMEM((slots, side, side), bf16),
+            pltpu.VMEM((4, 2 * quarter, side), f32),
             *[pltpu.VMEM(tables[k].shape, bf16) for k in (0, 4, 1, 2, 3)],
             pltpu.SemaphoreType.DMA((4 * chunks,)),
             pltpu.SemaphoreType.DMA((slots,)),
             pltpu.SemaphoreType.DMA((5,)),
         ],
-        compiler_params=pltpu.CompilerParams(vmem_limit_bytes=44 * 2**20),
+        compiler_params=pltpu.CompilerParams(vmem_limit_bytes=46 * 2**20),
         name="slots",
     )(counts, offset_y, offset_x, scale, obj_re, obj_im, right, *below, *diag, probe_re, probe_im, amplitude, *tables)
     parts = len(out_parts)
@@ -537,7 +541,7 @@
 
 
 IN_SHARES = (16, 8, 5, 3)
-OUT_SHARES = (4, 12, 16)
+OUT_SHARES = (5, 9, 18)
 
 
 def solution(mesh):

time: 119 us -> 118 us (level)
  starting transfers between devices: 63.5 us -> 60.6 us
  other arithmetic: 2.56 us -> 3.96 us
    ppermute x22, starting transfers between devices: 63.5 us -> 60.6 us  [shifted(): lax.ppermute(value, axis, [(i, (i + steps) % count) for i in range(count)])]
    convert_element_type x3, other arithmetic: 0.34 us -> 1.74 us  [update(): sent = (mine + theirs.astype(f32)).astype(bf16)]
  transfers between devices with their start and end apart: 22 -> 22, of which waited for: 10 -> 10; matrix products, arithmetic and copies ran while one was open for 2% -> 3% of each run, Pallas kernels for 0% -> 0%
where the time goes in v6:
time: 118 us
  starting transfers between devices  60.6 us (51%)
  waiting for transfers between devices  31.6 us (27%)
  Pallas kernels  18.2 us (15%)
  other arithmetic  3.96 us (3%)
  between operations  2.21 us (2%)
  local copies, waits for them, and re-layouts  1.42 us (1%)
    ppermute x22, starting transfers between devices, shifted(): lax.ppermute(value, axis, [(i, (i + steps) % count) for i in range(count)])  60.6 us
    ppermute x22, waiting for transfers between devices, shifted(): lax.ppermute(value, axis, [(i, (i + steps) % count) for i in range(count)])  31.6 us
    pallas_call x1, Pallas kernels, run_slots(): pl.pallas_call(functools.partial(slots_kernel, side, in_parts, out_parts)...  12.4 us
    pallas_call x1, Pallas kernels, run_finish(): pl.pallas_call(functools.partial(finish_kernel, parts), out_shape=(tile,...  5.73 us
  transfers between devices with their start and end apart: 22, of which 10 were waited for; matrix products, arithmetic and copies ran while one was open for 3% of the time, Pallas kernels for 0%

profile of v6, /device:TPU:0, one launch (start us, length us, event | category | flops | bytes accessed | tf_op | source)
XLA Modules:
  0.0 118.1 jit_solution(293268305542132809)
XLA Ops:
  0.6 1.4 %fusion = (bf16[1,256,512]{2,1,0:T(8,128)(2,1)S(1)}, bf16[1,256,512]{2,1,0:T(8,128)(2,1)S(1)}) fusion(f32[512,512]{1,0:T(8,128)} %refs_4_.1, f32[512,512]{1,0:T(8,128)} %refs_5_.1), kind=kLoop, calls=%fused_computation.16 | loop fusion | bytes 1048576 | tf_op jit(solution)/shard_map/stack | solution.py:514
  2.1 5.1 %collective-permute-start.1 = (bf16[2,256,512]{2,1,0:T(8,128)(2,1)S(1)}, bf16[2,256,512]{2,1,0:T(8,128)(2,1)S(1)}, u32[]{:S(2)}, u32[]{:S(2)}) collective-permute-start(bf16[2,256,512]{2,1,0:T(8,128)(2,1)S(1)} %pad_maximum_fusion.1), channel_id=1, source_target_pairs={{0,24},{8,0},{16,8},{24,16},{1,25},{9,1},{17,9},{25,17},{2,26},{10... | collective-permute-start | bytes 1572872 | tf_op jit(solution)/shard_map/ppermute | solution.py:493
  7.4 1.1 pad_maximum_fusion
  8.4 1.6 %collective-permute-start = (bf16[2,512,512]{2,1,0:T(8,128)(2,1)}, bf16[2,512,512]{2,1,0:T(8,128)(2,1)}, u32[]{:S(2)}, u32[]{:S(2)}) collective-permute-start(bf16[2,512,512]{2,1,0:T(8,128)(2,1)} %pad_maximum_fusion), channel_id=1, source_target_pairs={{0,7},{1,0},{2,1},{3,2},{4,3},{5,4},{6,5},{7,6},{8,15},{9,8},{10,9... | collective-permute-start | bytes 3145736 | tf_op jit(solution)/shard_map/ppermute | solution.py:493
  10.1 1.4 %collective-permute-start.2 = (bf16[2,128,512]{2,1,0:T(8,128)(2,1)S(1)}, bf16[2,128,512]{2,1,0:T(8,128)(2,1)S(1)}, u32[]{:S(2)}, u32[]{:S(2)}) collective-permute-start(bf16[2,128,512]{2,1,0:T(8,128)(2,1)S(1)} %fusion.2), channel_id=1, source_target_pairs={{0,24},{8,0},{16,8},{24,16},{1,25},{9,1},{17,9},{25,17},{2,26},{10... | collective-permute-start | bytes 786440 | tf_op jit(solution)/shard_map/ppermute | solution.py:493
  11.5 8.0 %collective-permute-done.1.refs_7_ = bf16[2,256,512]{2,1,0:T(8,128)(2,1)S(1)} collective-permute-done((bf16[2,256,512]{2,1,0:T(8,128)(2,1)S(1)}, bf16[2,256,512]{2,1,0:T(8,128)(2,1)S(1)}, u32[]{:S(2)}, u32[]{:S(2)}) %collective-permute-start.1) | collective-permute-done | bytes 524320 | tf_op jit(solution)/shard_map/ppermute | solution.py:493
  19.5 4.3 %collective-permute-start.3 = (bf16[2,80,512]{2,1,0:T(8,128)(2,1)S(1)}, bf16[2,80,512]{2,1,0:T(8,128)(2,1)}, u32[]{:S(2)}, u32[]{:S(2)}) collective-permute-start(bf16[2,80,512]{2,1,0:T(8,128)(2,1)S(1)} %fusion.3), channel_id=1, source_target_pairs={{0,24},{8,0},{16,8},{24,16},{1,25},{9,1},{17,9},{25,17},{2,26},{10... | collective-permute-start | bytes 491528 | tf_op jit(solution)/shard_map/ppermute | solution.py:493
  24.0 2.3 %collective-permute-start.6 = (bf16[2,128,512]{2,1,0:T(8,128)(2,1)S(1)}, bf16[2,128,512]{2,1,0:T(8,128)(2,1)}, u32[]{:S(2)}, u32[]{:S(2)}) collective-permute-start(bf16[2,128,512]{2,1,0:T(8,128)(2,1)S(1)} %collective-permute-done.2.refs_8_), channel_id=1, source_target_pairs={{0,7},{1,0},{2,1},{3,2},{4,3},{5,4},{6,5},{7,6},{8,15},{9,8},{10,9... | collective-permute-start | bytes 786440 | tf_op jit(solution)/shard_map/ppermute | solution.py:493
  27.0 3.1 %collective-permute-done.4.refs_10_ = bf16[2,48,512]{2,1,0:T(8,128)(2,1)S(1)} collective-permute-done((bf16[2,48,512]{2,1,0:T(8,128)(2,1)S(1)}, bf16[2,48,512]{2,1,0:T(8,128)(2,1)S(1)}, u32[]{:S(2)}, u32[]{:S(2)}) %collective-permute-start.4) | collective-permute-done | bytes 98336 | tf_op jit(solution)/shard_map/ppermute | solution.py:493
  30.1 1.7 %collective-permute-start.8 = (bf16[2,48,512]{2,1,0:T(8,128)(2,1)S(1)}, bf16[2,48,512]{2,1,0:T(8,128)(2,1)}, u32[]{:S(2)}, u32[]{:S(2)}) collective-permute-start(bf16[2,48,512]{2,1,0:T(8,128)(2,1)S(1)} %collective-permute-done.4.refs_10_), channel_id=1, source_target_pairs={{0,7},{1,0},{2,1},{3,2},{4,3},{5,4},{6,5},{7,6},{8,15},{9,8},{10,9... | collective-permute-start | bytes 294920 | tf_op jit(solution)/shard_map/ppermute | solution.py:493
  31.8 0.9 collective-permute-start.7
  32.7 0.9 add_reduce_fusion
  34.3 1.5 %collective-permute-done.7.refs_13_ = bf16[2,80,512]{2,1,0:T(8,128)(2,1)} collective-permute-done((bf16[2,80,512]{2,1,0:T(8,128)(2,1)}, bf16[2,80,512]{2,1,0:T(8,128)(2,1)}, u32[]{:S(2)}, u32[]{:S(2)}) %collective-permute-start.7) | collective-permute-done | bytes 163872 | tf_op jit(solution)/shard_map/ppermute | solution.py:493
  35.9 12.4 %slots.1 = (f32[2,512,512]{2,1,0:T(8,128)}, bf16[2,512,512]{2,1,0:T(8,128)(2,1)S(1)}, f32[2,1024]{1,0:T(2,128)S(1)}, f32[2,3072]{1,0:T(2,128)S(1)}, f32[2,3072]{...) custom-call(s32[1,1]{1,0:T(1,128)S(6)} %copy.15.refs_0_, ...), custom_call_target="tpu_custom_call" | custom-call | tf_op jit(solution)/shard_map/slots/pallas_call | solution.py:301
  48.3 0.2 collective-permute-start.14
  48.6 5.9 %collective-permute-start.12 = (bf16[2,144,512]{2,1,0:T(8,128)(2,1)S(1)}, bf16[2,144,512]{2,1,0:T(8,128)(2,1)S(1)}, u32[]{:S(2)}, u32[]{:S(2)}) collective-permute-start(bf16[2,144,512]{2,1,0:T(8,128)(2,1)S(1)} %get-tuple-element.31), channel_id=1, source_target_pairs={{0,1},{1,2},{2,3},{3,4},{4,5},{5,6},{6,7},{7,0},{8,9},{9,10},{10,1... | collective-permute-start | bytes 884744 | tf_op jit(solution)/shard_map/ppermute | solution.py:493
  54.6 7.0 %collective-permute-start.10 = (bf16[2,80,512]{2,1,0:T(8,128)(2,1)S(1)}, bf16[2,80,512]{2,1,0:T(8,128)(2,1)S(1)}, u32[]{:S(2)}, u32[]{:S(2)}) collective-permute-start(bf16[2,80,512]{2,1,0:T(8,128)(2,1)S(1)} %get-tuple-element.29), channel_id=1, source_target_pairs={{0,1},{1,2},{2,3},{3,4},{4,5},{5,6},{6,7},{7,0},{8,9},{9,10},{10,1... | collective-permute-start | bytes 491528 | tf_op jit(solution)/shard_map/ppermute | solution.py:493
  61.6 1.6 %add_convert_fusion = bf16[2,288,512]{2,1,0:T(8,128)(2,1)S(1)} fusion(f32[2,288,512]{2,1,0:T(8,128)} %get-tuple-element.32, bf16[2,288,512]{2,1,0:T(8,128)(2,1)S(1)} %collective-permute-done.14), kind=kLoop, calls=%fused_computation.7 | loop fusion | flops 884736 | bytes 2359296 | tf_op jit(solution)/shard_map/convert_element_type | solution.py:534
  63.2 8.3 %collective-permute-start.15 = (bf16[2,288,512]{2,1,0:T(8,128)(2,1)S(1)}, bf16[2,288,512]{2,1,0:T(8,128)(2,1)S(1)}, u32[]{:S(2)}, u32[]{:S(2)}) collective-permute-start(bf16[2,288,512]{2,1,0:T(8,128)(2,1)S(1)} %add_convert_fusion), channel_id=1, source_target_pairs={{0,8},{8,16},{16,24},{24,0},{1,9},{9,17},{17,25},{25,1},{2,10},{10... | collective-permute-start | bytes 1769480 | tf_op jit(solution)/shard_map/ppermute | solution.py:493
  71.5 1.8 %collective-permute-done.12 = bf16[2,144,512]{2,1,0:T(8,128)(2,1)S(1)} collective-permute-done((bf16[2,144,512]{2,1,0:T(8,128)(2,1)S(1)}, bf16[2,144,512]{2,1,0:T(8,128)(2,1)S(1)}, u32[]{:S(2)}, u32[]{:S(2)}) %collective-permute-start.12) | collective-permute-done | bytes 294944 | tf_op jit(solution)/shard_map/ppermute | solution.py:493
  73.4 11.0 %collective-permute-start.13 = (bf16[2,144,512]{2,1,0:T(8,128)(2,1)S(1)}, bf16[2,144,512]{2,1,0:T(8,128)(2,1)S(1)}, u32[]{:S(2)}, u32[]{:S(2)}) collective-permute-start(bf16[2,144,512]{2,1,0:T(8,128)(2,1)S(1)} %add_convert_fusion.1), channel_id=1, source_target_pairs={{0,8},{8,16},{16,24},{24,0},{1,9},{9,17},{17,25},{25,1},{2,10},{10... | collective-permute-start | bytes 884744 | tf_op jit(solution)/shard_map/ppermute | solution.py:493
  84.4 2.3 %collective-permute-start.11 = (bf16[2,80,512]{2,1,0:T(8,128)(2,1)S(1)}, bf16[2,80,512]{2,1,0:T(8,128)(2,1)S(1)}, u32[]{:S(2)}, u32[]{:S(2)}) collective-permute-start(bf16[2,80,512]{2,1,0:T(8,128)(2,1)S(1)} %add_convert_fusion.2), channel_id=1, source_target_pairs={{0,8},{8,16},{16,24},{24,0},{1,9},{9,17},{17,25},{25,1},{2,10},{10... | collective-permute-start | bytes 491528 | tf_op jit(solution)/shard_map/ppermute | solution.py:493
  86.7 1.4 %collective-permute-done.16.right_ref = f32[2,1024]{1,0:T(2,128)S(1)} collective-permute-done((f32[2,1024]{1,0:T(2,128)S(1)}, f32[2,1024]{1,0:T(2,128)S(1)}, u32[]{:S(2)}, u32[]{:S(2)}) %collective-permute-start.16) | collective-permute-done | bytes 8224 | tf_op jit(solution)/shard_map/ppermute | solution.py:493
  88.1 4.5 %collective-permute-done.18.second_ref = f32[2,1024]{1,0:T(2,128)S(1)} collective-permute-done((f32[2,1024]{1,0:T(2,128)S(1)}, f32[2,1024]{1,0:T(2,128)S(1)}, u32[]{:S(2)}, u32[]{:S(2)}) %collective-permute-start.18) | collective-permute-done | bytes 8224 | tf_op jit(solution)/shard_map/ppermute | solution.py:493
  92.6 4.1 %collective-permute-done.17.left_ref = f32[2,3072]{1,0:T(2,128)S(1)} collective-permute-done((f32[2,3072]{1,0:T(2,128)S(1)}, f32[2,3072]{1,0:T(2,128)S(1)}, u32[]{:S(2)}, u32[]{:S(2)}) %collective-permute-start.17) | collective-permute-done | bytes 24608 | tf_op jit(solution)/shard_map/ppermute | solution.py:493
  96.9 4.2 %collective-permute-start.20 = (f32[2,6,128]{2,1,0:T(8,128)S(1)}, f32[2,6,128]{2,1,0:T(8,128)S(1)}, u32[]{:S(2)}, u32[]{:S(2)}) collective-permute-start(f32[2,6,128]{2,1,0:T(8,128)S(1)} %get-tuple-element.39), channel_id=1, source_target_pairs={{0,16},{8,24},{16,0},{24,8},{1,17},{9,25},{17,1},{25,9},{2,18},{10... | collective-permute-start | bytes 18440 | tf_op jit(solution)/shard_map/ppermute | solution.py:493
  101.1 1.6 %collective-permute-done.20.refs_6_ = f32[2,6,128]{2,1,0:T(8,128)S(1)} collective-permute-done((f32[2,6,128]{2,1,0:T(8,128)S(1)}, f32[2,6,128]{2,1,0:T(8,128)S(1)}, u32[]{:S(2)}, u32[]{:S(2)}) %collective-permute-start.20) | collective-permute-done | bytes 6176 | tf_op jit(solution)/shard_map/ppermute | solution.py:493
  102.7 2.4 %collective-permute-start.21 = (f32[2,6,128]{2,1,0:T(8,128)S(1)}, f32[2,6,128]{2,1,0:T(8,128)S(1)}, u32[]{:S(2)}, u32[]{:S(2)}) collective-permute-start(f32[2,6,128]{2,1,0:T(8,128)S(1)} %get-tuple-element.40), channel_id=1, source_target_pairs={{0,24},{8,0},{16,8},{24,16},{1,25},{9,1},{17,9},{25,17},{2,26},{10... | collective-permute-start | bytes 18440 | tf_op jit(solution)/shard_map/ppermute | solution.py:493
  105.2 1.4 %collective-permute-done.21.refs_7_ = f32[2,6,128]{2,1,0:T(8,128)S(1)} collective-permute-done((f32[2,6,128]{2,1,0:T(8,128)S(1)}, f32[2,6,128]{2,1,0:T(8,128)S(1)}, u32[]{:S(2)}, u32[]{:S(2)}) %collective-permute-start.21) | collective-permute-done | bytes 6176 | tf_op jit(solution)/shard_map/ppermute | solution.py:493
  106.5 1.7 %collective-permute-start.19 = (f32[2,14,128]{2,1,0:T(8,128)S(1)}, f32[2,14,128]{2,1,0:T(8,128)S(1)}, u32[]{:S(2)}, u32[]{:S(2)}) collective-permute-start(f32[2,14,128]{2,1,0:T(8,128)S(1)} %get-tuple-element.38), channel_id=1, source_target_pairs={{0,8},{8,16},{16,24},{24,0},{1,9},{9,17},{17,25},{25,1},{2,10},{10... | collective-permute-start | bytes 43016 | tf_op jit(solution)/shard_map/ppermute | solution.py:493
  108.3 4.1 %collective-permute-done.19.refs_5_ = f32[2,14,128]{2,1,0:T(8,128)S(1)} collective-permute-done((f32[2,14,128]{2,1,0:T(8,128)S(1)}, f32[2,14,128]{2,1,0:T(8,128)S(1)}, u32[]{:S(2)}, u32[]{:S(2)}) %collective-permute-start.19) | collective-permute-done | bytes 14368 | tf_op jit(solution)/shard_map/ppermute | solution.py:493
  112.4 5.7 %finish.1 = (f32[512,512]{1,0:T(8,128)}, f32[512,512]{1,0:T(8,128)}) custom-call(f32[2,512,512]{2,1,0:T(8,128)S(1)} %copy-done, bf16[2,512,512]{2,1,0:T(8,128)(2,1)S(1)} %collective-permute-done.9.refs_1_, bf16[2,80,512]{2,1,0:T(8,128)(2,1)S(1)} %collective-permute-done.11.refs_2_, bf16[2,144,512]{2,1,0:T(8,128)(2,1)S(1)} %collective-permute-done.13.refs_3_, ...), custom_call_target="tpu_custom_call" | custom-call | tf_op jit(solution)/shard_map/finish/pallas_call | solution.py:437
  (49 shorter events, 0.8 us)
Async XLA Ops:
  0.6 6.6 %copy-start.7 = (f32[512,512]{1,0:T(8,128)S(1)}, f32[512,512]{1,0:T(8,128)}, u32[]{:S(2)}) copy-start(f32[512,512]{1,0:T(8,128)} %refs_4_.1) | copy-start | bytes 3145732
  2.1 17.4 %collective-permute-start.1 = (bf16[2,256,512]{2,1,0:T(8,128)(2,1)S(1)}, bf16[2,256,512]{2,1,0:T(8,128)(2,1)S(1)}, u32[]{:S(2)}, u32[]{:S(2)}) collective-permute-start(bf16[2,256,512]{2,1,0:T(8,128)(2,1)S(1)} %pad_maximum_fusion.1), channel_id=1, source_target_pairs={{0,24},{8,0},{16,8},{24,16},{1,25},{9,1},{17,9},{25,17},{2,26},{10... | collective-permute-start | bytes 1572872 | tf_op jit(solution)/shard_map/ppermute | solution.py:493
  8.4 27.4 %collective-permute-start = (bf16[2,512,512]{2,1,0:T(8,128)(2,1)}, bf16[2,512,512]{2,1,0:T(8,128)(2,1)}, u32[]{:S(2)}, u32[]{:S(2)}) collective-permute-start(bf16[2,512,512]{2,1,0:T(8,128)(2,1)} %pad_maximum_fusion), channel_id=1, source_target_pairs={{0,7},{1,0},{2,1},{3,2},{4,3},{5,4},{6,5},{7,6},{8,15},{9,8},{10,9... | collective-permute-start | bytes 3145736 | tf_op jit(solution)/shard_map/ppermute | solution.py:493
  10.1 22.6 %copy-start.9 = (f32[512,512]{1,0:T(8,128)S(1)}, f32[512,512]{1,0:T(8,128)}, u32[]{:S(2)}) copy-start(f32[512,512]{1,0:T(8,128)} %refs_16_.1) | copy-start | bytes 3145732
  10.1 22.6 %copy-start.10 = (f32[512,512]{1,0:T(8,128)S(1)}, f32[512,512]{1,0:T(8,128)}, u32[]{:S(2)}) copy-start(f32[512,512]{1,0:T(8,128)} %refs_15_.1) | copy-start | bytes 3145732
  10.1 14.0 %collective-permute-start.2 = (bf16[2,128,512]{2,1,0:T(8,128)(2,1)S(1)}, bf16[2,128,512]{2,1,0:T(8,128)(2,1)S(1)}, u32[]{:S(2)}, u32[]{:S(2)}) collective-permute-start(bf16[2,128,512]{2,1,0:T(8,128)(2,1)S(1)} %fusion.2), channel_id=1, source_target_pairs={{0,24},{8,0},{16,8},{24,16},{1,25},{9,1},{17,9},{25,17},{2,26},{10... | collective-permute-start | bytes 786440 | tf_op jit(solution)/shard_map/ppermute | solution.py:493
  19.5 16.3 %collective-permute-start.5 = (bf16[2,256,512]{2,1,0:T(8,128)(2,1)S(1)}, bf16[2,256,512]{2,1,0:T(8,128)(2,1)S(1)}, u32[]{:S(2)}, u32[]{:S(2)}) collective-permute-start(bf16[2,256,512]{2,1,0:T(8,128)(2,1)S(1)} %collective-permute-done.1.refs_7_), channel_id=1, source_target_pairs={{0,7},{1,0},{2,1},{3,2},{4,3},{5,4},{6,5},{7,6},{8,15},{9,8},{10,9... | collective-permute-start | bytes 1572872 | tf_op jit(solution)/shard_map/ppermute | solution.py:493
  19.5 12.3 %collective-permute-start.3 = (bf16[2,80,512]{2,1,0:T(8,128)(2,1)S(1)}, bf16[2,80,512]{2,1,0:T(8,128)(2,1)}, u32[]{:S(2)}, u32[]{:S(2)}) collective-permute-start(bf16[2,80,512]{2,1,0:T(8,128)(2,1)S(1)} %fusion.3), channel_id=1, source_target_pairs={{0,24},{8,0},{16,8},{24,16},{1,25},{9,1},{17,9},{25,17},{2,26},{10... | collective-permute-start | bytes 491528 | tf_op jit(solution)/shard_map/ppermute | solution.py:493
  23.9 12.0 %copy-start.1 = (bf16[512,512]{1,0:T(8,128)(2,1)S(1)}, bf16[512,512]{1,0:T(8,128)(2,1)}, u32[]{:S(2)}) copy-start(bf16[512,512]{1,0:T(8,128)(2,1)} %constant.23.clone.refs_22_) | copy-start | bytes 1572868
  23.9 12.0 %copy-start.2 = (bf16[4,256,256]{2,1,0:T(8,128)(2,1)S(1)}, bf16[4,256,256]{2,1,0:T(8,128)(2,1)}, u32[]{:S(2)}) copy-start(bf16[4,256,256]{2,1,0:T(8,128)(2,1)} %constant.22.clone.refs_21_) | copy-start | bytes 1572868
  23.9 12.0 %copy-start.3 = (bf16[512,512]{1,0:T(8,128)(2,1)S(1)}, bf16[512,512]{1,0:T(8,128)(2,1)}, u32[]{:S(2)}) copy-start(bf16[512,512]{1,0:T(8,128)(2,1)} %constant.20.clone.refs_19_) | copy-start | bytes 1572868
  23.9 11.9 %copy-start.4 = (bf16[4,256,256]{2,1,0:T(8,128)(2,1)S(1)}, bf16[4,256,256]{2,1,0:T(8,128)(2,1)}, u32[]{:S(2)}) copy-start(bf16[4,256,256]{2,1,0:T(8,128)(2,1)} %constant.19.clone.refs_18_) | copy-start | bytes 1572868
  23.9 11.9 %copy-start.5 = (s32[1,4]{1,0:T(1,128)S(1)}, s32[1,4]{1,0:T(1,128)}, u32[]{:S(2)}) copy-start(s32[1,4]{1,0:T(1,128)} %refs_1_.1) | copy-start | bytes 52
  23.9 11.9 %copy-start.6 = (s32[1,4]{1,0:T(1,128)S(1)}, s32[1,4]{1,0:T(1,128)}, u32[]{:S(2)}) copy-start(s32[1,4]{1,0:T(1,128)} %refs_2_.1) | copy-start | bytes 52
  24.0 6.1 %collective-permute-start.4 = (bf16[2,48,512]{2,1,0:T(8,128)(2,1)S(1)}, bf16[2,48,512]{2,1,0:T(8,128)(2,1)S(1)}, u32[]{:S(2)}, u32[]{:S(2)}) collective-permute-start(bf16[2,48,512]{2,1,0:T(8,128)(2,1)S(1)} %fusion.4), channel_id=1, source_target_pairs={{0,24},{8,0},{16,8},{24,16},{1,25},{9,1},{17,9},{25,17},{2,26},{10... | collective-permute-start | bytes 294920 | tf_op jit(solution)/shard_map/ppermute | solution.py:493
  24.0 11.8 %collective-permute-start.6 = (bf16[2,128,512]{2,1,0:T(8,128)(2,1)S(1)}, bf16[2,128,512]{2,1,0:T(8,128)(2,1)}, u32[]{:S(2)}, u32[]{:S(2)}) collective-permute-start(bf16[2,128,512]{2,1,0:T(8,128)(2,1)S(1)} %collective-permute-done.2.refs_8_), channel_id=1, source_target_pairs={{0,7},{1,0},{2,1},{3,2},{4,3},{5,4},{6,5},{7,6},{8,15},{9,8},{10,9... | collective-permute-start | bytes 786440 | tf_op jit(solution)/shard_map/ppermute | solution.py:493
  30.1 4.2 %collective-permute-start.8 = (bf16[2,48,512]{2,1,0:T(8,128)(2,1)S(1)}, bf16[2,48,512]{2,1,0:T(8,128)(2,1)}, u32[]{:S(2)}, u32[]{:S(2)}) collective-permute-start(bf16[2,48,512]{2,1,0:T(8,128)(2,1)S(1)} %collective-permute-done.4.refs_10_), channel_id=1, source_target_pairs={{0,7},{1,0},{2,1},{3,2},{4,3},{5,4},{6,5},{7,6},{8,15},{9,8},{10,9... | collective-permute-start | bytes 294920 | tf_op jit(solution)/shard_map/ppermute | solution.py:493
  31.8 4.0 %collective-permute-start.7 = (bf16[2,80,512]{2,1,0:T(8,128)(2,1)}, bf16[2,80,512]{2,1,0:T(8,128)(2,1)}, u32[]{:S(2)}, u32[]{:S(2)}) collective-permute-start(bf16[2,80,512]{2,1,0:T(8,128)(2,1)} %collective-permute-done.3.refs_9_), channel_id=1, source_target_pairs={{0,7},{1,0},{2,1},{3,2},{4,3},{5,4},{6,5},{7,6},{8,15},{9,8},{10,9... | collective-permute-start | bytes 491528 | tf_op jit(solution)/shard_map/ppermute | solution.py:493
  48.3 13.2 %collective-permute-start.14 = (bf16[2,288,512]{2,1,0:T(8,128)(2,1)S(1)}, bf16[2,288,512]{2,1,0:T(8,128)(2,1)S(1)}, u32[]{:S(2)}, u32[]{:S(2)}) collective-permute-start(bf16[2,288,512]{2,1,0:T(8,128)(2,1)S(1)} %get-tuple-element.33), channel_id=1, source_target_pairs={{0,1},{1,2},{2,3},{3,4},{4,5},{5,6},{6,7},{7,0},{8,9},{9,10},{10,1... | collective-permute-start | bytes 1769480 | tf_op jit(solution)/shard_map/ppermute | solution.py:493
  48.5 63.8 %collective-permute-start.9 = (bf16[2,512,512]{2,1,0:T(8,128)(2,1)S(1)}, bf16[2,512,512]{2,1,0:T(8,128)(2,1)S(1)}, u32[]{:S(2)}, u32[]{:S(2)}) collective-permute-start(bf16[2,512,512]{2,1,0:T(8,128)(2,1)S(1)} %get-tuple-element.27), channel_id=1, source_target_pairs={{0,1},{1,2},{2,3},{3,4},{4,5},{5,6},{6,7},{7,0},{8,9},{9,10},{10,1... | collective-permute-start | bytes 3145736 | tf_op jit(solution)/shard_map/ppermute | solution.py:493
  48.6 24.6 %collective-permute-start.12 = (bf16[2,144,512]{2,1,0:T(8,128)(2,1)S(1)}, bf16[2,144,512]{2,1,0:T(8,128)(2,1)S(1)}, u32[]{:S(2)}, u32[]{:S(2)}) collective-permute-start(bf16[2,144,512]{2,1,0:T(8,128)(2,1)S(1)} %get-tuple-element.31), channel_id=1, source_target_pairs={{0,1},{1,2},{2,3},{3,4},{4,5},{5,6},{6,7},{7,0},{8,9},{9,10},{10,1... | collective-permute-start | bytes 884744 | tf_op jit(solution)/shard_map/ppermute | solution.py:493
  54.6 29.8 %collective-permute-start.10 = (bf16[2,80,512]{2,1,0:T(8,128)(2,1)S(1)}, bf16[2,80,512]{2,1,0:T(8,128)(2,1)S(1)}, u32[]{:S(2)}, u32[]{:S(2)}) collective-permute-start(bf16[2,80,512]{2,1,0:T(8,128)(2,1)S(1)} %get-tuple-element.29), channel_id=1, source_target_pairs={{0,1},{1,2},{2,3},{3,4},{4,5},{5,6},{6,7},{7,0},{8,9},{9,10},{10,1... | collective-permute-start | bytes 491528 | tf_op jit(solution)/shard_map/ppermute | solution.py:493
  61.6 50.8 %copy-start = (f32[2,512,512]{2,1,0:T(8,128)S(1)}, f32[2,512,512]{2,1,0:T(8,128)}, u32[]{:S(2)}) copy-start(f32[2,512,512]{2,1,0:T(8,128)} %get-tuple-element.26.refs_0_) | copy-start | bytes 6291460
  63.2 49.2 %collective-permute-start.15 = (bf16[2,288,512]{2,1,0:T(8,128)(2,1)S(1)}, bf16[2,288,512]{2,1,0:T(8,128)(2,1)S(1)}, u32[]{:S(2)}, u32[]{:S(2)}) collective-permute-start(bf16[2,288,512]{2,1,0:T(8,128)(2,1)S(1)} %add_convert_fusion), channel_id=1, source_target_pairs={{0,8},{8,16},{16,24},{24,0},{1,9},{9,17},{17,25},{25,1},{2,10},{10... | collective-permute-start | bytes 1769480 | tf_op jit(solution)/shard_map/ppermute | solution.py:493
  73.4 39.0 %collective-permute-start.13 = (bf16[2,144,512]{2,1,0:T(8,128)(2,1)S(1)}, bf16[2,144,512]{2,1,0:T(8,128)(2,1)S(1)}, u32[]{:S(2)}, u32[]{:S(2)}) collective-permute-start(bf16[2,144,512]{2,1,0:T(8,128)(2,1)S(1)} %add_convert_fusion.1), channel_id=1, source_target_pairs={{0,8},{8,16},{16,24},{24,0},{1,9},{9,17},{17,25},{25,1},{2,10},{10... | collective-permute-start | bytes 884744 | tf_op jit(solution)/shard_map/ppermute | solution.py:493
  84.4 27.9 %collective-permute-start.11 = (bf16[2,80,512]{2,1,0:T(8,128)(2,1)S(1)}, bf16[2,80,512]{2,1,0:T(8,128)(2,1)S(1)}, u32[]{:S(2)}, u32[]{:S(2)}) collective-permute-start(bf16[2,80,512]{2,1,0:T(8,128)(2,1)S(1)} %add_convert_fusion.2), channel_id=1, source_target_pairs={{0,8},{8,16},{16,24},{24,0},{1,9},{9,17},{17,25},{25,1},{2,10},{10... | collective-permute-start | bytes 491528 | tf_op jit(solution)/shard_map/ppermute | solution.py:493
  86.7 1.4 %collective-permute-start.16 = (f32[2,1024]{1,0:T(2,128)S(1)}, f32[2,1024]{1,0:T(2,128)S(1)}, u32[]{:S(2)}, u32[]{:S(2)}) collective-permute-start(f32[2,1024]{1,0:T(2,128)S(1)} %get-tuple-element.34), channel_id=1, source_target_pairs={{0,7},{1,0},{2,1},{3,2},{4,3},{5,4},{6,5},{7,6},{8,15},{9,8},{10,9... | collective-permute-start | bytes 24584 | tf_op jit(solution)/shard_map/ppermute | solution.py:493
  88.0 4.5 %collective-permute-start.18 = (f32[2,1024]{1,0:T(2,128)S(1)}, f32[2,1024]{1,0:T(2,128)S(1)}, u32[]{:S(2)}, u32[]{:S(2)}) collective-permute-start(f32[2,1024]{1,0:T(2,128)S(1)} %get-tuple-element.36), channel_id=1, source_target_pairs={{0,2},{1,3},{2,4},{3,5},{4,6},{5,7},{6,0},{7,1},{8,10},{9,11},{10,... | collective-permute-start | bytes 24584 | tf_op jit(solution)/shard_map/ppermute | solution.py:493
  92.6 4.2 %collective-permute-start.17 = (f32[2,3072]{1,0:T(2,128)S(1)}, f32[2,3072]{1,0:T(2,128)S(1)}, u32[]{:S(2)}, u32[]{:S(2)}) collective-permute-start(f32[2,3072]{1,0:T(2,128)S(1)} %get-tuple-element.35), channel_id=1, source_target_pairs={{0,1},{1,2},{2,3},{3,4},{4,5},{5,6},{6,7},{7,0},{8,9},{9,10},{10,1... | collective-permute-start | bytes 73736 | tf_op jit(solution)/shard_map/ppermute | solution.py:493
  96.9 5.9 %collective-permute-start.20 = (f32[2,6,128]{2,1,0:T(8,128)S(1)}, f32[2,6,128]{2,1,0:T(8,128)S(1)}, u32[]{:S(2)}, u32[]{:S(2)}) collective-permute-start(f32[2,6,128]{2,1,0:T(8,128)S(1)} %get-tuple-element.39), channel_id=1, source_target_pairs={{0,16},{8,24},{16,0},{24,8},{1,17},{9,25},{17,1},{25,9},{2,18},{10... | collective-permute-start | bytes 18440 | tf_op jit(solution)/shard_map/ppermute | solution.py:493
  102.7 3.8 %collective-permute-start.21 = (f32[2,6,128]{2,1,0:T(8,128)S(1)}, f32[2,6,128]{2,1,0:T(8,128)S(1)}, u32[]{:S(2)}, u32[]{:S(2)}) collective-permute-start(f32[2,6,128]{2,1,0:T(8,128)S(1)} %get-tuple-element.40), channel_id=1, source_target_pairs={{0,24},{8,0},{16,8},{24,16},{1,25},{9,1},{17,9},{25,17},{2,26},{10... | collective-permute-start | bytes 18440 | tf_op jit(solution)/shard_map/ppermute | solution.py:493
  106.5 5.8 %collective-permute-start.19 = (f32[2,14,128]{2,1,0:T(8,128)S(1)}, f32[2,14,128]{2,1,0:T(8,128)S(1)}, u32[]{:S(2)}, u32[]{:S(2)}) collective-permute-start(f32[2,14,128]{2,1,0:T(8,128)S(1)} %get-tuple-element.38), channel_id=1, source_target_pairs={{0,8},{8,16},{16,24},{24,0},{1,9},{9,17},{17,25},{25,1},{2,10},{10... | collective-permute-start | bytes 43016 | tf_op jit(solution)/shard_map/ppermute | solution.py:493
  (1 other events, 5.3 us)

commit v7 on v6

--- a/solution.py
+++ b/solution.py
@@ -74,11 +74,11 @@
     count_ref, oy_ref, ox_ref, scale_ref, own_re, own_im, right_ref = take(7)
     below_refs, diag_refs = take(len(in_parts)), take(len(in_parts))
     probe_re, probe_im, amp_ref = take(3)
-    rows_in, cols_in, cols_out, rows_out, pick = take(5)
+    rows_in, cols_in, cols_out, rows_out = take(4)
     own_out, right_out, left_out, beside_out, kept_out, second_out = take(6)
     below_outs, diag_outs = take(len(out_parts)), take(len(out_parts))
-    region, sums, probe, exits, wide, half, delta, back, amp, held, amp_held, wave = refs[:12]
-    table_held, sems, amp_sems, table_sems = refs[12:17], refs[17], refs[18], refs[19]
+    region, sums, probe, exits, wide, half, delta, back, held, amp_held, wave = refs[:11]
+    table_held, sems, amp_sems, table_sems = refs[11:15], refs[15], refs[16], refs[17]
     quarter, chunks = side // 4, side // LANES
     f32, bf16 = jnp.float32, jnp.bfloat16
 
@@ -92,11 +92,11 @@
         ]
 
     def amp_fetch(s):
-        return pltpu.make_async_copy(amp_ref.at[0, s], amp_held.at[s], amp_sems.at[s])
+        return pltpu.make_async_copy(amp_ref.at[s], amp_held.at[s], amp_sems.at[s])
 
     own_copies = fetches((own_re, own_im), held, 0)
     late_copies = fetches((probe_re, probe_im), probe, 2 * chunks)
-    tables = (rows_in, pick, cols_in, cols_out, rows_out)
+    tables = (rows_in, cols_in, cols_out, rows_out)
     late_copies += [
         pltpu.make_async_copy(table, target, table_sems.at[k]) for k, (table, target) in enumerate(zip(tables, table_held))
     ]
@@ -108,7 +108,7 @@
         return carry
 
     lax.fori_loop(0, count_ref[0, 0], start_amp, 0)
-    rows_in, pick, cols_in, cols_out, rows_out = table_held
+    rows_in, cols_in, cols_out, rows_out = table_held
     sums[...] = jnp.zeros_like(sums)
 
     for p in range(2):
@@ -201,10 +201,6 @@
                     half[cc, m * step : (m + 1) * step, lanes] = o_re.astype(bf16)
                     half[cc, quarter + m * step : quarter + (m + 1) * step, lanes] = o_im.astype(bf16)
 
-        ordered = dot(amp_held[s], pick[...])
-        for a in range(chunks):
-            amp[a] = ordered[:, a * LANES : (a + 1) * LANES]
-
         for cc in range(4):
             wide[cc] = dot(half[cc], cols_in[...])
             take_patch(later, cc)
@@ -220,7 +216,8 @@
                 for sign in range(2):
                     s_re = p1 - p2 if sign == 0 else p1 + p2
                     s_im = p4 + p3 if sign == 0 else p4 - p3
-                    measured = amp[sign * mid + part, pl.ds(cc, quarter, stride=4), :]
+                    at = (sign * mid + part) * LANES
+                    measured = amp_held[s, cc * quarter : (cc + 1) * quarter, at : at + LANES].astype(f32)
                     inverse = jnp.minimum(lax.rsqrt(s_re * s_re + s_im * s_im), 1.0 / modulus_floor)
                     factor = measured * inverse - 1.0
                     rows = slice(cc * quarter, (cc + 1) * quarter)
@@ -285,23 +282,53 @@
                 beside_out[here, at : at + LANES] = scale * sums[p, chunks + a, row : row + 1, :]
 
 
+def order_kernel(amp_ref, pick_ref, out_ref, wide):
+    side = pick_ref.shape[0]
+    quarter = side // 4
+    ordered = dot(amp_ref[0, 0], pick_ref[...])
+    for a in range(side // LANES):
+        lanes = slice(a * LANES, (a + 1) * LANES)
+        wide[a] = ordered[:, lanes]
+        for c in range(4):
+            out_ref[0, c * quarter : (c + 1) * quarter, lanes] = wide[a, pl.ds(c, quarter, stride=4), :].astype(jnp.bfloat16)
+
+
+def run_order(amplitude):
+    slots, side = amplitude.shape[1], amplitude.shape[2]
+    pick = transform_tables(side)[4]
+    return pl.pallas_call(
+        order_kernel,
+        grid=(slots,),
+        out_shape=jax.ShapeDtypeStruct((slots, side, side), jnp.bfloat16),
+        in_specs=[
+            pl.BlockSpec((1, 1, side, side), lambda s: (0, s, 0, 0)),
+            pl.BlockSpec((side, side), lambda s: (0, 0)),
+        ],
+        out_specs=pl.BlockSpec((1, side, side), lambda s: (s, 0, 0)),
+        scratch_shapes=[pltpu.VMEM((side // LANES, side, LANES), jnp.float32)],
+        compiler_params=pltpu.CompilerParams(vmem_limit_bytes=8 * 2**20),
+        cost_estimate=pl.CostEstimate(flops=2 * slots * side**3, bytes_accessed=4 * slots * side**2, transcendentals=0),
+        name="order",
+    )(amplitude, pick)
+
+
 def run_slots(counts, offset_y, offset_x, scale, obj_re, obj_im, right, below, diag, probe_re, probe_im, amplitude, out_parts):
     side = probe_re.shape[0]
     chunks, quarter = side // LANES, side // 4
     f32, bf16 = jnp.float32, jnp.bfloat16
-    tables = transform_tables(side)
+    tables = transform_tables(side)[:4]
     in_parts = [part.shape[1] for part in below]
     smem = pl.BlockSpec(memory_space=pltpu.SMEM)
     vmem = pl.BlockSpec(memory_space=pltpu.VMEM)
     here = pl.BlockSpec(memory_space=pl.ANY)
-    slots = amplitude.shape[1]
+    slots = amplitude.shape[0]
     tile = lambda rows, kind: jax.ShapeDtypeStruct((2, rows, side), kind)
     outs = [tile(side, f32), tile(side, bf16)] + [jax.ShapeDtypeStruct((2, n * side), f32) for n in (2, 6, 6, 2)]
     outs += [tile(rows, f32) for rows in out_parts] + [tile(rows, bf16) for rows in out_parts]
     results = pl.pallas_call(
         functools.partial(slots_kernel, side, in_parts, out_parts),
         out_shape=outs,
-        in_specs=[smem] * 4 + [here] * 2 + [vmem] * (1 + 2 * len(in_parts)) + [here] * 8,
+        in_specs=[smem] * 4 + [here] * 2 + [vmem] * (1 + 2 * len(in_parts)) + [here] * 7,
         out_specs=[vmem] * len(outs),
         scratch_shapes=[
             pltpu.VMEM((2, 2 * chunks, 2 * side, LANES), f32),
@@ -312,14 +339,13 @@
             pltpu.VMEM((4, 2 * quarter, side), bf16),
             pltpu.VMEM((2, side, side), bf16),
             pltpu.VMEM((4, 2 * quarter, side), bf16),
-            pltpu.VMEM((chunks, side, LANES), f32),
             pltpu.VMEM((2, chunks, side, LANES), f32),
             pltpu.VMEM((slots, side, side), bf16),
             pltpu.VMEM((4, 2 * quarter, side), f32),
-            *[pltpu.VMEM(tables[k].shape, bf16) for k in (0, 4, 1, 2, 3)],
+            *[pltpu.VMEM(table.shape, bf16) for table in tables],
             pltpu.SemaphoreType.DMA((4 * chunks,)),
             pltpu.SemaphoreType.DMA((slots,)),
-            pltpu.SemaphoreType.DMA((5,)),
+            pltpu.SemaphoreType.DMA((4,)),
         ],
         compiler_params=pltpu.CompilerParams(vmem_limit_bytes=46 * 2**20),
         name="slots",
@@ -519,6 +545,7 @@
     for rest in split_rows(own, in_parts)[1:]:
         below.append(shifted(rest, "row", -1))
     diag = [shifted(value, "col", -1) for value in below]
+    amplitude = run_order(amplitude)
     probe_power = jnp.mean(probe_re * probe_re + probe_im * probe_im) + epsilon
     scale = (step_size / probe_power).reshape(1, 1)
     own_sum, right_sum, edges, below_sum, diag_sum = run_slots(

time: 118 us -> 120 us (1.017)
  starting transfers between devices: 60.6 us -> 56.6 us
  local copies, waits for them, and re-layouts: 1.42 us -> 3.89 us
  Pallas kernels: 18.2 us -> 20.2 us
    ppermute x22, starting transfers between devices: 60.6 us -> 56.6 us  [shifted(): lax.ppermute(value, axis, [(i, (i + steps) % count) for i in range(count)])]
    unnamed x22 -> x26, local copies, waits for them, and re-layouts: 0.07 us -> 2.54 us
    pallas_call x0 -> x1, Pallas kernels: none -> 2.07 us  [run_order(): pl.pallas_call(order_kernel, grid=(slots,), out_shape=jax.ShapeDtypeStruc...]
  transfers between devices with their start and end apart: 22 -> 22, of which waited for: 10 -> 9; matrix products, arithmetic and copies ran while one was open for 3% -> 4% of each run, Pallas kernels for 0% -> 2%
where the time goes in v7:
time: 120 us
  starting transfers between devices  56.6 us (47%)
  waiting for transfers between devices  32.3 us (27%)
  Pallas kernels  20.2 us (17%)
  other arithmetic  4.59 us (4%)
  local copies, waits for them, and re-layouts  3.89 us (3%)
  between operations  2.15 us (2%)
    ppermute x22, starting transfers between devices, shifted(): lax.ppermute(value, axis, [(i, (i + steps) % count) for i in range(count)])  56.6 us
    ppermute x22, waiting for transfers between devices, shifted(): lax.ppermute(value, axis, [(i, (i + steps) % count) for i in range(count)])  32.3 us
    pallas_call x1, Pallas kernels, run_slots(): pl.pallas_call(functools.partial(slots_kernel, side, in_parts, out_parts)...  12.3 us
    pallas_call x1, Pallas kernels, run_finish(): pl.pallas_call(functools.partial(finish_kernel, parts), out_shape=(tile,...  5.73 us
    unnamed x26, local copies, waits for them, and re-layouts  2.54 us
  transfers between devices with their start and end apart: 22, of which 9 were waited for; matrix products, arithmetic and copies ran while one was open for 4% of the time, Pallas kernels for 2%

profile of v7, /device:TPU:0, one launch (start us, length us, event | category | flops | bytes accessed | tf_op | source)
XLA Modules:
  0.0 119.8 jit_solution(855546174461012958)
XLA Ops:
  0.6 1.4 %fusion = (bf16[1,256,512]{2,1,0:T(8,128)(2,1)S(1)}, bf16[1,256,512]{2,1,0:T(8,128)(2,1)S(1)}) fusion(f32[512,512]{1,0:T(8,128)} %refs_4_.1, f32[512,512]{1,0:T(8,128)} %refs_5_.1), kind=kLoop, calls=%fused_computation.16 | loop fusion | bytes 1048576 | tf_op jit(solution)/shard_map/stack | solution.py:540
  2.1 5.1 %collective-permute-start.1 = (bf16[2,256,512]{2,1,0:T(8,128)(2,1)S(1)}, bf16[2,256,512]{2,1,0:T(8,128)(2,1)}, u32[]{:S(2)}, u32[]{:S(2)}) collective-permute-start(bf16[2,256,512]{2,1,0:T(8,128)(2,1)S(1)} %pad_maximum_fusion.1), channel_id=1, source_target_pairs={{0,24},{8,0},{16,8},{24,16},{1,25},{9,1},{17,9},{25,17},{2,26},{10... | collective-permute-start | bytes 1572872 | tf_op jit(solution)/shard_map/ppermute | solution.py:519
  7.4 1.1 pad_maximum_fusion
  8.4 1.6 %collective-permute-start = (bf16[2,512,512]{2,1,0:T(8,128)(2,1)}, bf16[2,512,512]{2,1,0:T(8,128)(2,1)}, u32[]{:S(2)}, u32[]{:S(2)}) collective-permute-start(bf16[2,512,512]{2,1,0:T(8,128)(2,1)} %pad_maximum_fusion), channel_id=1, source_target_pairs={{0,7},{1,0},{2,1},{3,2},{4,3},{5,4},{6,5},{7,6},{8,15},{9,8},{10,9... | collective-permute-start | bytes 3145736 | tf_op jit(solution)/shard_map/ppermute | solution.py:519
  10.1 1.4 %collective-permute-start.2 = (bf16[2,128,512]{2,1,0:T(8,128)(2,1)S(1)}, bf16[2,128,512]{2,1,0:T(8,128)(2,1)S(1)}, u32[]{:S(2)}, u32[]{:S(2)}) collective-permute-start(bf16[2,128,512]{2,1,0:T(8,128)(2,1)S(1)} %fusion.2), channel_id=1, source_target_pairs={{0,24},{8,0},{16,8},{24,16},{1,25},{9,1},{17,9},{25,17},{2,26},{10... | collective-permute-start | bytes 786440 | tf_op jit(solution)/shard_map/ppermute | solution.py:519
  11.5 8.0 %collective-permute-done.1.refs_7_ = bf16[2,256,512]{2,1,0:T(8,128)(2,1)} collective-permute-done((bf16[2,256,512]{2,1,0:T(8,128)(2,1)S(1)}, bf16[2,256,512]{2,1,0:T(8,128)(2,1)}, u32[]{:S(2)}, u32[]{:S(2)}) %collective-permute-start.1) | collective-permute-done | bytes 524320 | tf_op jit(solution)/shard_map/ppermute | solution.py:519
  19.5 4.4 %collective-permute-start.3 = (bf16[2,80,512]{2,1,0:T(8,128)(2,1)S(1)}, bf16[2,80,512]{2,1,0:T(8,128)(2,1)}, u32[]{:S(2)}, u32[]{:S(2)}) collective-permute-start(bf16[2,80,512]{2,1,0:T(8,128)(2,1)S(1)} %fusion.3), channel_id=1, source_target_pairs={{0,24},{8,0},{16,8},{24,16},{1,25},{9,1},{17,9},{25,17},{2,26},{10... | collective-permute-start | bytes 491528 | tf_op jit(solution)/shard_map/ppermute | solution.py:519
  24.6 3.9 %collective-permute-done.3.refs_9_ = bf16[2,80,512]{2,1,0:T(8,128)(2,1)} collective-permute-done((bf16[2,80,512]{2,1,0:T(8,128)(2,1)S(1)}, bf16[2,80,512]{2,1,0:T(8,128)(2,1)}, u32[]{:S(2)}, u32[]{:S(2)}) %collective-permute-start.3) | collective-permute-done | bytes 163872 | tf_op jit(solution)/shard_map/ppermute | solution.py:519
  28.6 1.2 %collective-permute-start.7 = (bf16[2,80,512]{2,1,0:T(8,128)(2,1)}, bf16[2,80,512]{2,1,0:T(8,128)(2,1)}, u32[]{:S(2)}, u32[]{:S(2)}) collective-permute-start(bf16[2,80,512]{2,1,0:T(8,128)(2,1)} %collective-permute-done.3.refs_9_), channel_id=1, source_target_pairs={{0,7},{1,0},{2,1},{3,2},{4,3},{5,4},{6,5},{7,6},{8,15},{9,8},{10,9... | collective-permute-start | bytes 491528 | tf_op jit(solution)/shard_map/ppermute | solution.py:519
  29.8 1.3 %collective-permute-start.6 = (bf16[2,128,512]{2,1,0:T(8,128)(2,1)S(1)}, bf16[2,128,512]{2,1,0:T(8,128)(2,1)}, u32[]{:S(2)}, u32[]{:S(2)}) collective-permute-start(bf16[2,128,512]{2,1,0:T(8,128)(2,1)S(1)} %collective-permute-done.2.refs_8_), channel_id=1, source_target_pairs={{0,7},{1,0},{2,1},{3,2},{4,3},{5,4},{6,5},{7,6},{8,15},{9,8},{10,9... | collective-permute-start | bytes 786440 | tf_op jit(solution)/shard_map/ppermute | solution.py:519
  31.1 0.9 add_reduce_fusion
  33.5 1.1 copy-done.7
  34.6 2.1 %order.1.refs_17_ = bf16[4,512,512]{2,1,0:T(8,128)(2,1)S(1)} custom-call(bf16[1,4,512,512]{3,2,1,0:T(8,128)(2,1)S(1)} %copy-done.2, bf16[512,512]{1,0:T(8,128)(2,1)S(1)} %copy-done.7), custom_call_target="tpu_custom_call" | custom-call | flops 1073741824 | bytes 4194304 | tf_op jit(solution)/shard_map/order/pallas_call | solution.py:299
  36.7 1.3 %copy-done = bf16[4,512,512]{2,1,0:T(8,128)(2,1)} copy-done((bf16[4,512,512]{2,1,0:T(8,128)(2,1)}, bf16[4,512,512]{2,1,0:T(8,128)(2,1)S(1)}, u32[]{:S(2)}) %copy-start) | copy-done | bytes 2097176
  38.1 12.3 %slots.1 = (f32[2,512,512]{2,1,0:T(8,128)}, bf16[2,512,512]{2,1,0:T(8,128)(2,1)S(1)}, f32[2,1024]{1,0:T(2,128)S(1)}, f32[2,3072]{1,0:T(2,128)S(1)}, f32[2,3072]{...) custom-call(s32[1,1]{1,0:T(1,128)S(6)} %copy.15.refs_0_, ...), custom_call_target="tpu_custom_call" | custom-call | tf_op jit(solution)/shard_map/slots/pallas_call | solution.py:328
  51.7 3.5 %collective-permute-start.12 = (bf16[2,144,512]{2,1,0:T(8,128)(2,1)S(1)}, bf16[2,144,512]{2,1,0:T(8,128)(2,1)S(1)}, u32[]{:S(2)}, u32[]{:S(2)}) collective-permute-start(bf16[2,144,512]{2,1,0:T(8,128)(2,1)S(1)} %get-tuple-element.31), channel_id=1, source_target_pairs={{0,1},{1,2},{2,3},{3,4},{4,5},{5,6},{6,7},{7,0},{8,9},{9,10},{10,1... | collective-permute-start | bytes 884744 | tf_op jit(solution)/shard_map/ppermute | solution.py:519
  55.2 8.1 %collective-permute-start.10 = (bf16[2,80,512]{2,1,0:T(8,128)(2,1)S(1)}, bf16[2,80,512]{2,1,0:T(8,128)(2,1)S(1)}, u32[]{:S(2)}, u32[]{:S(2)}) collective-permute-start(bf16[2,80,512]{2,1,0:T(8,128)(2,1)S(1)} %get-tuple-element.29), channel_id=1, source_target_pairs={{0,1},{1,2},{2,3},{3,4},{4,5},{5,6},{6,7},{7,0},{8,9},{9,10},{10,1... | collective-permute-start | bytes 491528 | tf_op jit(solution)/shard_map/ppermute | solution.py:519
  63.3 1.6 %add_convert_fusion = bf16[2,288,512]{2,1,0:T(8,128)(2,1)S(1)} fusion(f32[2,288,512]{2,1,0:T(8,128)} %get-tuple-element.32, bf16[2,288,512]{2,1,0:T(8,128)(2,1)S(1)} %collective-permute-done.14), kind=kLoop, calls=%fused_computation.7 | loop fusion | flops 884736 | bytes 2359296 | tf_op jit(solution)/shard_map/convert_element_type | solution.py:561
  64.9 6.9 %collective-permute-start.15 = (bf16[2,288,512]{2,1,0:T(8,128)(2,1)S(1)}, bf16[2,288,512]{2,1,0:T(8,128)(2,1)S(1)}, u32[]{:S(2)}, u32[]{:S(2)}) collective-permute-start(bf16[2,288,512]{2,1,0:T(8,128)(2,1)S(1)} %add_convert_fusion), channel_id=1, source_target_pairs={{0,8},{8,16},{16,24},{24,0},{1,9},{9,17},{17,25},{25,1},{2,10},{10... | collective-permute-start | bytes 1769480 | tf_op jit(solution)/shard_map/ppermute | solution.py:519
  71.7 3.4 %collective-permute-done.12 = bf16[2,144,512]{2,1,0:T(8,128)(2,1)S(1)} collective-permute-done((bf16[2,144,512]{2,1,0:T(8,128)(2,1)S(1)}, bf16[2,144,512]{2,1,0:T(8,128)(2,1)S(1)}, u32[]{:S(2)}, u32[]{:S(2)}) %collective-permute-start.12) | collective-permute-done | bytes 294944 | tf_op jit(solution)/shard_map/ppermute | solution.py:519
  75.2 9.4 %collective-permute-start.13 = (bf16[2,144,512]{2,1,0:T(8,128)(2,1)S(1)}, bf16[2,144,512]{2,1,0:T(8,128)(2,1)S(1)}, u32[]{:S(2)}, u32[]{:S(2)}) collective-permute-start(bf16[2,144,512]{2,1,0:T(8,128)(2,1)S(1)} %add_convert_fusion.1), channel_id=1, source_target_pairs={{0,8},{8,16},{16,24},{24,0},{1,9},{9,17},{17,25},{25,1},{2,10},{10... | collective-permute-start | bytes 884744 | tf_op jit(solution)/shard_map/ppermute | solution.py:519
  84.7 2.5 %collective-permute-start.11 = (bf16[2,80,512]{2,1,0:T(8,128)(2,1)S(1)}, bf16[2,80,512]{2,1,0:T(8,128)(2,1)S(1)}, u32[]{:S(2)}, u32[]{:S(2)}) collective-permute-start(bf16[2,80,512]{2,1,0:T(8,128)(2,1)S(1)} %add_convert_fusion.2), channel_id=1, source_target_pairs={{0,8},{8,16},{16,24},{24,0},{1,9},{9,17},{17,25},{25,1},{2,10},{10... | collective-permute-start | bytes 491528 | tf_op jit(solution)/shard_map/ppermute | solution.py:519
  87.2 1.4 %collective-permute-done.16.right_ref = f32[2,1024]{1,0:T(2,128)S(1)} collective-permute-done((f32[2,1024]{1,0:T(2,128)S(1)}, f32[2,1024]{1,0:T(2,128)S(1)}, u32[]{:S(2)}, u32[]{:S(2)}) %collective-permute-start.16) | collective-permute-done | bytes 8224 | tf_op jit(solution)/shard_map/ppermute | solution.py:519
  88.7 4.4 %collective-permute-done.18.second_ref = f32[2,1024]{1,0:T(2,128)S(1)} collective-permute-done((f32[2,1024]{1,0:T(2,128)S(1)}, f32[2,1024]{1,0:T(2,128)S(1)}, u32[]{:S(2)}, u32[]{:S(2)}) %collective-permute-start.18) | collective-permute-done | bytes 8224 | tf_op jit(solution)/shard_map/ppermute | solution.py:519
  93.1 4.1 %collective-permute-done.17.left_ref = f32[2,3072]{1,0:T(2,128)S(1)} collective-permute-done((f32[2,3072]{1,0:T(2,128)S(1)}, f32[2,3072]{1,0:T(2,128)S(1)}, u32[]{:S(2)}, u32[]{:S(2)}) %collective-permute-start.17) | collective-permute-done | bytes 24608 | tf_op jit(solution)/shard_map/ppermute | solution.py:519
  97.4 5.4 %collective-permute-start.20 = (f32[2,6,128]{2,1,0:T(8,128)S(1)}, f32[2,6,128]{2,1,0:T(8,128)S(1)}, u32[]{:S(2)}, u32[]{:S(2)}) collective-permute-start(f32[2,6,128]{2,1,0:T(8,128)S(1)} %get-tuple-element.39), channel_id=1, source_target_pairs={{0,16},{8,24},{16,0},{24,8},{1,17},{9,25},{17,1},{25,9},{2,18},{10... | collective-permute-start | bytes 18440 | tf_op jit(solution)/shard_map/ppermute | solution.py:519
  102.8 1.6 %collective-permute-done.20.refs_6_ = f32[2,6,128]{2,1,0:T(8,128)S(1)} collective-permute-done((f32[2,6,128]{2,1,0:T(8,128)S(1)}, f32[2,6,128]{2,1,0:T(8,128)S(1)}, u32[]{:S(2)}, u32[]{:S(2)}) %collective-permute-start.20) | collective-permute-done | bytes 6176 | tf_op jit(solution)/shard_map/ppermute | solution.py:519
  104.5 2.4 %collective-permute-start.21 = (f32[2,6,128]{2,1,0:T(8,128)S(1)}, f32[2,6,128]{2,1,0:T(8,128)S(1)}, u32[]{:S(2)}, u32[]{:S(2)}) collective-permute-start(f32[2,6,128]{2,1,0:T(8,128)S(1)} %get-tuple-element.40), channel_id=1, source_target_pairs={{0,24},{8,0},{16,8},{24,16},{1,25},{9,1},{17,9},{25,17},{2,26},{10... | collective-permute-start | bytes 18440 | tf_op jit(solution)/shard_map/ppermute | solution.py:519
  106.9 1.4 %collective-permute-done.21.refs_7_ = f32[2,6,128]{2,1,0:T(8,128)S(1)} collective-permute-done((f32[2,6,128]{2,1,0:T(8,128)S(1)}, f32[2,6,128]{2,1,0:T(8,128)S(1)}, u32[]{:S(2)}, u32[]{:S(2)}) %collective-permute-start.21) | collective-permute-done | bytes 6176 | tf_op jit(solution)/shard_map/ppermute | solution.py:519
  108.3 1.7 %collective-permute-start.19 = (f32[2,14,128]{2,1,0:T(8,128)S(1)}, f32[2,14,128]{2,1,0:T(8,128)S(1)}, u32[]{:S(2)}, u32[]{:S(2)}) collective-permute-start(f32[2,14,128]{2,1,0:T(8,128)S(1)} %get-tuple-element.38), channel_id=1, source_target_pairs={{0,8},{8,16},{16,24},{24,0},{1,9},{9,17},{17,25},{25,1},{2,10},{10... | collective-permute-start | bytes 43016 | tf_op jit(solution)/shard_map/ppermute | solution.py:519
  110.0 4.1 %collective-permute-done.19.refs_5_ = f32[2,14,128]{2,1,0:T(8,128)S(1)} collective-permute-done((f32[2,14,128]{2,1,0:T(8,128)S(1)}, f32[2,14,128]{2,1,0:T(8,128)S(1)}, u32[]{:S(2)}, u32[]{:S(2)}) %collective-permute-start.19) | collective-permute-done | bytes 14368 | tf_op jit(solution)/shard_map/ppermute | solution.py:519
  114.1 5.7 %finish.1 = (f32[512,512]{1,0:T(8,128)}, f32[512,512]{1,0:T(8,128)}) custom-call(f32[2,512,512]{2,1,0:T(8,128)S(1)} %copy-done.3, bf16[2,512,512]{2,1,0:T(8,128)(2,1)S(1)} %collective-permute-done.9.refs_1_, bf16[2,80,512]{2,1,0:T(8,128)(2,1)S(1)} %collective-permute-done.11.refs_2_, bf16[2,144,512]{2,1,0:T(8,128)(2,1)S(1)} %collective-permute-done.13.refs_3_, ...), custom_call_target="tpu_custom_call" | custom-call | tf_op jit(solution)/shard_map/finish/pallas_call | solution.py:463
  (54 shorter events, 2.7 us)
Async XLA Ops:
  0.6 6.6 %copy-start.1 = (f32[512,512]{1,0:T(8,128)S(1)}, f32[512,512]{1,0:T(8,128)}, u32[]{:S(2)}) copy-start(f32[512,512]{1,0:T(8,128)} %refs_4_.1) | copy-start | bytes 3145732
  2.0 5.3 %copy-start.10 = (f32[512,512]{1,0:T(8,128)S(1)}, f32[512,512]{1,0:T(8,128)}, u32[]{:S(2)}) copy-start(f32[512,512]{1,0:T(8,128)} %refs_5_.1) | copy-start | bytes 3145732
  2.1 17.4 %collective-permute-start.1 = (bf16[2,256,512]{2,1,0:T(8,128)(2,1)S(1)}, bf16[2,256,512]{2,1,0:T(8,128)(2,1)}, u32[]{:S(2)}, u32[]{:S(2)}) collective-permute-start(bf16[2,256,512]{2,1,0:T(8,128)(2,1)S(1)} %pad_maximum_fusion.1), channel_id=1, source_target_pairs={{0,24},{8,0},{16,8},{24,16},{1,25},{9,1},{17,9},{25,17},{2,26},{10... | collective-permute-start | bytes 1572872 | tf_op jit(solution)/shard_map/ppermute | solution.py:519
  8.4 29.6 %collective-permute-start = (bf16[2,512,512]{2,1,0:T(8,128)(2,1)}, bf16[2,512,512]{2,1,0:T(8,128)(2,1)}, u32[]{:S(2)}, u32[]{:S(2)}) collective-permute-start(bf16[2,512,512]{2,1,0:T(8,128)(2,1)} %pad_maximum_fusion), channel_id=1, source_target_pairs={{0,7},{1,0},{2,1},{3,2},{4,3},{5,4},{6,5},{7,6},{8,15},{9,8},{10,9... | collective-permute-start | bytes 3145736 | tf_op jit(solution)/shard_map/ppermute | solution.py:519
  10.1 21.1 %copy-start.11 = (f32[512,512]{1,0:T(8,128)S(1)}, f32[512,512]{1,0:T(8,128)}, u32[]{:S(2)}) copy-start(f32[512,512]{1,0:T(8,128)} %refs_16_.1) | copy-start | bytes 3145732
  10.1 21.1 %copy-start.12 = (f32[512,512]{1,0:T(8,128)S(1)}, f32[512,512]{1,0:T(8,128)}, u32[]{:S(2)}) copy-start(f32[512,512]{1,0:T(8,128)} %refs_15_.1) | copy-start | bytes 3145732
  10.1 19.7 %collective-permute-start.2 = (bf16[2,128,512]{2,1,0:T(8,128)(2,1)S(1)}, bf16[2,128,512]{2,1,0:T(8,128)(2,1)S(1)}, u32[]{:S(2)}, u32[]{:S(2)}) collective-permute-start(bf16[2,128,512]{2,1,0:T(8,128)(2,1)S(1)} %fusion.2), channel_id=1, source_target_pairs={{0,24},{8,0},{16,8},{24,16},{1,25},{9,1},{17,9},{25,17},{2,26},{10... | collective-permute-start | bytes 786440 | tf_op jit(solution)/shard_map/ppermute | solution.py:519
  19.5 18.5 %collective-permute-start.5 = (bf16[2,256,512]{2,1,0:T(8,128)(2,1)}, bf16[2,256,512]{2,1,0:T(8,128)(2,1)}, u32[]{:S(2)}, u32[]{:S(2)}) collective-permute-start(bf16[2,256,512]{2,1,0:T(8,128)(2,1)} %collective-permute-done.1.refs_7_), channel_id=1, source_target_pairs={{0,7},{1,0},{2,1},{3,2},{4,3},{5,4},{6,5},{7,6},{8,15},{9,8},{10,9... | collective-permute-start | bytes 1572872 | tf_op jit(solution)/shard_map/ppermute | solution.py:519
  19.5 9.0 %collective-permute-start.3 = (bf16[2,80,512]{2,1,0:T(8,128)(2,1)S(1)}, bf16[2,80,512]{2,1,0:T(8,128)(2,1)}, u32[]{:S(2)}, u32[]{:S(2)}) collective-permute-start(bf16[2,80,512]{2,1,0:T(8,128)(2,1)S(1)} %fusion.3), channel_id=1, source_target_pairs={{0,24},{8,0},{16,8},{24,16},{1,25},{9,1},{17,9},{25,17},{2,26},{10... | collective-permute-start | bytes 491528 | tf_op jit(solution)/shard_map/ppermute | solution.py:519
  24.6 8.8 %copy-start.2 = (bf16[1,4,512,512]{3,2,1,0:T(8,128)(2,1)S(1)}, bf16[1,4,512,512]{3,2,1,0:T(8,128)(2,1)}, u32[]{:S(2)}) copy-start(bf16[1,4,512,512]{3,2,1,0:T(8,128)(2,1)} %amp_ref.1) | copy-start | bytes 6291460
  24.6 8.7 %collective-permute-start.4 = (bf16[2,48,512]{2,1,0:T(8,128)(2,1)}, bf16[2,48,512]{2,1,0:T(8,128)(2,1)S(1)}, u32[]{:S(2)}, u32[]{:S(2)}) collective-permute-start(bf16[2,48,512]{2,1,0:T(8,128)(2,1)} %fusion.4), channel_id=1, source_target_pairs={{0,24},{8,0},{16,8},{24,16},{1,25},{9,1},{17,9},{25,17},{2,26},{10... | collective-permute-start | bytes 294920 | tf_op jit(solution)/shard_map/ppermute | solution.py:519
  28.6 9.5 %collective-permute-start.7 = (bf16[2,80,512]{2,1,0:T(8,128)(2,1)}, bf16[2,80,512]{2,1,0:T(8,128)(2,1)}, u32[]{:S(2)}, u32[]{:S(2)}) collective-permute-start(bf16[2,80,512]{2,1,0:T(8,128)(2,1)} %collective-permute-done.3.refs_9_), channel_id=1, source_target_pairs={{0,7},{1,0},{2,1},{3,2},{4,3},{5,4},{6,5},{7,6},{8,15},{9,8},{10,9... | collective-permute-start | bytes 491528 | tf_op jit(solution)/shard_map/ppermute | solution.py:519
  29.8 8.2 %collective-permute-start.6 = (bf16[2,128,512]{2,1,0:T(8,128)(2,1)S(1)}, bf16[2,128,512]{2,1,0:T(8,128)(2,1)}, u32[]{:S(2)}, u32[]{:S(2)}) collective-permute-start(bf16[2,128,512]{2,1,0:T(8,128)(2,1)S(1)} %collective-permute-done.2.refs_8_), channel_id=1, source_target_pairs={{0,7},{1,0},{2,1},{3,2},{4,3},{5,4},{6,5},{7,6},{8,15},{9,8},{10,9... | collective-permute-start | bytes 786440 | tf_op jit(solution)/shard_map/ppermute | solution.py:519
  33.3 4.8 %copy-start.8 = (s32[1,4]{1,0:T(1,128)S(1)}, s32[1,4]{1,0:T(1,128)}, u32[]{:S(2)}) copy-start(s32[1,4]{1,0:T(1,128)} %refs_1_.1) | copy-start | bytes 52
  33.3 4.8 %copy-start.9 = (s32[1,4]{1,0:T(1,128)S(1)}, s32[1,4]{1,0:T(1,128)}, u32[]{:S(2)}) copy-start(s32[1,4]{1,0:T(1,128)} %refs_2_.1) | copy-start | bytes 52
  33.3 4.7 %copy-start.4 = (bf16[4,256,256]{2,1,0:T(8,128)(2,1)S(1)}, bf16[4,256,256]{2,1,0:T(8,128)(2,1)}, u32[]{:S(2)}) copy-start(bf16[4,256,256]{2,1,0:T(8,128)(2,1)} %constant.23.clone.refs_21_) | copy-start | bytes 1572868
  33.3 4.7 %copy-start.5 = (bf16[512,512]{1,0:T(8,128)(2,1)S(1)}, bf16[512,512]{1,0:T(8,128)(2,1)}, u32[]{:S(2)}) copy-start(bf16[512,512]{1,0:T(8,128)(2,1)} %constant.21.clone.refs_19_) | copy-start | bytes 1572868
  33.4 4.6 %collective-permute-start.8 = (bf16[2,48,512]{2,1,0:T(8,128)(2,1)S(1)}, bf16[2,48,512]{2,1,0:T(8,128)(2,1)S(1)}, u32[]{:S(2)}, u32[]{:S(2)}) collective-permute-start(bf16[2,48,512]{2,1,0:T(8,128)(2,1)S(1)} %collective-permute-done.4.refs_10_), channel_id=1, source_target_pairs={{0,7},{1,0},{2,1},{3,2},{4,3},{5,4},{6,5},{7,6},{8,15},{9,8},{10,9... | collective-permute-start | bytes 294920 | tf_op jit(solution)/shard_map/ppermute | solution.py:519
  50.4 12.8 %collective-permute-start.14 = (bf16[2,288,512]{2,1,0:T(8,128)(2,1)S(1)}, bf16[2,288,512]{2,1,0:T(8,128)(2,1)S(1)}, u32[]{:S(2)}, u32[]{:S(2)}) collective-permute-start(bf16[2,288,512]{2,1,0:T(8,128)(2,1)S(1)} %get-tuple-element.33), channel_id=1, source_target_pairs={{0,1},{1,2},{2,3},{3,4},{4,5},{5,6},{6,7},{7,0},{8,9},{9,10},{10,1... | collective-permute-start | bytes 1769480 | tf_op jit(solution)/shard_map/ppermute | solution.py:519
  51.0 63.1 %collective-permute-start.9 = (bf16[2,512,512]{2,1,0:T(8,128)(2,1)S(1)}, bf16[2,512,512]{2,1,0:T(8,128)(2,1)S(1)}, u32[]{:S(2)}, u32[]{:S(2)}) collective-permute-start(bf16[2,512,512]{2,1,0:T(8,128)(2,1)S(1)} %get-tuple-element.27), channel_id=1, source_target_pairs={{0,1},{1,2},{2,3},{3,4},{4,5},{5,6},{6,7},{7,0},{8,9},{9,10},{10,1... | collective-permute-start | bytes 3145736 | tf_op jit(solution)/shard_map/ppermute | solution.py:519
  51.7 23.4 %collective-permute-start.12 = (bf16[2,144,512]{2,1,0:T(8,128)(2,1)S(1)}, bf16[2,144,512]{2,1,0:T(8,128)(2,1)S(1)}, u32[]{:S(2)}, u32[]{:S(2)}) collective-permute-start(bf16[2,144,512]{2,1,0:T(8,128)(2,1)S(1)} %get-tuple-element.31), channel_id=1, source_target_pairs={{0,1},{1,2},{2,3},{3,4},{4,5},{5,6},{6,7},{7,0},{8,9},{9,10},{10,1... | collective-permute-start | bytes 884744 | tf_op jit(solution)/shard_map/ppermute | solution.py:519
  55.2 29.4 %collective-permute-start.10 = (bf16[2,80,512]{2,1,0:T(8,128)(2,1)S(1)}, bf16[2,80,512]{2,1,0:T(8,128)(2,1)S(1)}, u32[]{:S(2)}, u32[]{:S(2)}) collective-permute-start(bf16[2,80,512]{2,1,0:T(8,128)(2,1)S(1)} %get-tuple-element.29), channel_id=1, source_target_pairs={{0,1},{1,2},{2,3},{3,4},{4,5},{5,6},{6,7},{7,0},{8,9},{9,10},{10,1... | collective-permute-start | bytes 491528 | tf_op jit(solution)/shard_map/ppermute | solution.py:519
  63.3 50.8 %copy-start.3 = (f32[2,512,512]{2,1,0:T(8,128)S(1)}, f32[2,512,512]{2,1,0:T(8,128)}, u32[]{:S(2)}) copy-start(f32[2,512,512]{2,1,0:T(8,128)} %get-tuple-element.26.refs_0_) | copy-start | bytes 6291460
  64.9 49.2 %collective-permute-start.15 = (bf16[2,288,512]{2,1,0:T(8,128)(2,1)S(1)}, bf16[2,288,512]{2,1,0:T(8,128)(2,1)S(1)}, u32[]{:S(2)}, u32[]{:S(2)}) collective-permute-start(bf16[2,288,512]{2,1,0:T(8,128)(2,1)S(1)} %add_convert_fusion), channel_id=1, source_target_pairs={{0,8},{8,16},{16,24},{24,0},{1,9},{9,17},{17,25},{25,1},{2,10},{10... | collective-permute-start | bytes 1769480 | tf_op jit(solution)/shard_map/ppermute | solution.py:519
  75.2 38.9 %collective-permute-start.13 = (bf16[2,144,512]{2,1,0:T(8,128)(2,1)S(1)}, bf16[2,144,512]{2,1,0:T(8,128)(2,1)S(1)}, u32[]{:S(2)}, u32[]{:S(2)}) collective-permute-start(bf16[2,144,512]{2,1,0:T(8,128)(2,1)S(1)} %add_convert_fusion.1), channel_id=1, source_target_pairs={{0,8},{8,16},{16,24},{24,0},{1,9},{9,17},{17,25},{25,1},{2,10},{10... | collective-permute-start | bytes 884744 | tf_op jit(solution)/shard_map/ppermute | solution.py:519
  84.7 29.4 %collective-permute-start.11 = (bf16[2,80,512]{2,1,0:T(8,128)(2,1)S(1)}, bf16[2,80,512]{2,1,0:T(8,128)(2,1)S(1)}, u32[]{:S(2)}, u32[]{:S(2)}) collective-permute-start(bf16[2,80,512]{2,1,0:T(8,128)(2,1)S(1)} %add_convert_fusion.2), channel_id=1, source_target_pairs={{0,8},{8,16},{16,24},{24,0},{1,9},{9,17},{17,25},{25,1},{2,10},{10... | collective-permute-start | bytes 491528 | tf_op jit(solution)/shard_map/ppermute | solution.py:519
  87.2 1.4 %collective-permute-start.16 = (f32[2,1024]{1,0:T(2,128)S(1)}, f32[2,1024]{1,0:T(2,128)S(1)}, u32[]{:S(2)}, u32[]{:S(2)}) collective-permute-start(f32[2,1024]{1,0:T(2,128)S(1)} %get-tuple-element.34), channel_id=1, source_target_pairs={{0,7},{1,0},{2,1},{3,2},{4,3},{5,4},{6,5},{7,6},{8,15},{9,8},{10,9... | collective-permute-start | bytes 24584 | tf_op jit(solution)/shard_map/ppermute | solution.py:519
  88.6 4.5 %collective-permute-start.18 = (f32[2,1024]{1,0:T(2,128)S(1)}, f32[2,1024]{1,0:T(2,128)S(1)}, u32[]{:S(2)}, u32[]{:S(2)}) collective-permute-start(f32[2,1024]{1,0:T(2,128)S(1)} %get-tuple-element.36), channel_id=1, source_target_pairs={{0,2},{1,3},{2,4},{3,5},{4,6},{5,7},{6,0},{7,1},{8,10},{9,11},{10,... | collective-permute-start | bytes 24584 | tf_op jit(solution)/shard_map/ppermute | solution.py:519
  93.1 4.2 %collective-permute-start.17 = (f32[2,3072]{1,0:T(2,128)S(1)}, f32[2,3072]{1,0:T(2,128)S(1)}, u32[]{:S(2)}, u32[]{:S(2)}) collective-permute-start(f32[2,3072]{1,0:T(2,128)S(1)} %get-tuple-element.35), channel_id=1, source_target_pairs={{0,1},{1,2},{2,3},{3,4},{4,5},{5,6},{6,7},{7,0},{8,9},{9,10},{10,1... | collective-permute-start | bytes 73736 | tf_op jit(solution)/shard_map/ppermute | solution.py:519
  97.4 7.1 %collective-permute-start.20 = (f32[2,6,128]{2,1,0:T(8,128)S(1)}, f32[2,6,128]{2,1,0:T(8,128)S(1)}, u32[]{:S(2)}, u32[]{:S(2)}) collective-permute-start(f32[2,6,128]{2,1,0:T(8,128)S(1)} %get-tuple-element.39), channel_id=1, source_target_pairs={{0,16},{8,24},{16,0},{24,8},{1,17},{9,25},{17,1},{25,9},{2,18},{10... | collective-permute-start | bytes 18440 | tf_op jit(solution)/shard_map/ppermute | solution.py:519
  104.5 3.8 %collective-permute-start.21 = (f32[2,6,128]{2,1,0:T(8,128)S(1)}, f32[2,6,128]{2,1,0:T(8,128)S(1)}, u32[]{:S(2)}, u32[]{:S(2)}) collective-permute-start(f32[2,6,128]{2,1,0:T(8,128)S(1)} %get-tuple-element.40), channel_id=1, source_target_pairs={{0,24},{8,0},{16,8},{24,16},{1,25},{9,1},{17,9},{25,17},{2,26},{10... | collective-permute-start | bytes 18440 | tf_op jit(solution)/shard_map/ppermute | solution.py:519
  108.3 5.8 %collective-permute-start.19 = (f32[2,14,128]{2,1,0:T(8,128)S(1)}, f32[2,14,128]{2,1,0:T(8,128)S(1)}, u32[]{:S(2)}, u32[]{:S(2)}) collective-permute-start(f32[2,14,128]{2,1,0:T(8,128)S(1)} %get-tuple-element.38), channel_id=1, source_target_pairs={{0,8},{8,16},{16,24},{24,0},{1,9},{9,17},{17,25},{25,1},{2,10},{10... | collective-permute-start | bytes 43016 | tf_op jit(solution)/shard_map/ppermute | solution.py:519
  (3 other events, 7.2 us)
